TPU v7x, 128 devices: a whole 4x4x4 slice. The times are simulated.
128 devices in a mesh: grp: 8 (over x, z_lo), wide: 16 (over y, z_hi, core).
Axes of the slice: x: 4, y: 4, z: 4 (z_hi: 2, z_lo: 2; z = z_hi * 2 + z_lo), core: 2. Of those that a mesh axis runs over, the one named last changes fastest.
Arguments:
- left_env: bfloat16 [64, 32, 128, 128], P('grp', 'wide'), may hold values from -0.5 to 0.5
- right_env: bfloat16 [128, 32, 128, 128], P('wide', 'grp'), may hold values from -0.09375 to 0.09375
- psi: bfloat16 [64, 128, 128, 128], P('grp', 'wide'), may hold values from -6 to 6
- left_shift: int32 [32], replicated, may hold values from -1 to 1
- right_shift: int32 [32], replicated, may hold values from -1 to 1
- active: int32 [64, 128, 32], P('grp', 'wide'), may hold values 0 or 1
Outputs:
- hpsi: float32 [64, 128, 128, 128], P('grp', 'wide')
All inputs are finite; a program needn't handle non-finite values. No bound on the sum of `active` on one device may be relied on, other than what follows from the above.
Results may differ from a plain program's by a relative error of at most 0.0029.
Values may be sent and summed in bfloat16 or wider, within the bound.
No kernel may reach another device: no remote copies, remote signals or barrier semaphores. Data moves between devices by JAX's collectives and lax.ppermute only.
A program may use at most 128 MiB of HBM per device.

v0:
```python
import jax
import jax.numpy as jnp
from jax import lax
from jax.sharding import PartitionSpec as P


def with_halo(value, sides, width):
    for axis, dim in sides:
        devices, length = (lax.axis_size(axis), value.shape[dim])
        up = [(i, (i + 1) % devices) for i in range(devices - 1)]
        down = [(j, i) for i, j in up]
        last = lax.slice_in_dim(value, length - width, length, axis=dim)
        leading = lax.slice_in_dim(value, 0, width, axis=dim)
        before = lax.ppermute(last, axis, up)
        after = lax.ppermute(leading, axis, down)
        value = jnp.concatenate([before, value, after], axis=dim)
    return value


def add_terms(total, padded, left_part, right_part, left_moves, right_moves, enabled_part):
    rows = total.shape[0]
    cols = total.shape[1]
    col_ids = jnp.arange(cols, dtype=jnp.int32)[None, :] + 1 + right_moves[:, None]

    def one_row(row_index):
        row_ids = row_index + 1 + left_moves
        picked = padded[row_ids[:, None], col_ids]
        inner = jnp.einsum(
            "wij,wcjk->wcik", left_part[row_index], picked, preferred_element_type=jnp.float32
        ).astype(jnp.bfloat16)
        inner = inner * jnp.transpose(enabled_part[row_index])[:, :, None, None]
        return jnp.einsum("wcik,cwdk->cid", inner, right_part, preferred_element_type=jnp.float32)

    return lax.map(one_row, jnp.arange(rows, dtype=jnp.int32))


def per_device(left_env, right_env, psi, left_shift, right_shift, active):
    padded = with_halo(psi, (("grp", 0), ("wide", 1)), 1)
    enabled = active.astype(jnp.bfloat16)
    start_total = jnp.zeros((psi.shape[0], psi.shape[1], psi.shape[2], psi.shape[3]), jnp.float32)
    left_all = lax.all_gather(left_env, "wide", axis=1, tiled=True)
    right_all = lax.all_gather(right_env, "grp", axis=1, tiled=True)
    return add_terms(start_total, padded, left_all, right_all, left_shift, right_shift, enabled)


def solution(mesh):
    return jax.shard_map(
        per_device,
        mesh=mesh,
        in_specs=(
            P("grp", "wide", None, None),
            P("wide", "grp", None, None),
            P("grp", "wide", None, None),
            P(),
            P(),
            P("grp", "wide", None),
        ),
        out_specs=P("grp", "wide", None, None),
        check_vma=False,
    )
```

profile of v0, /device:TPU:1, one launch (start us, length us, event | category | flops | bytes accessed | tf_op | source)
XLA Modules:
  0.0 459.4 jit_solution(1416285173617828692)
XLA Ops:
  6.5 0.7 all-gather.5.cloned.1.call-update
  7.3 0.7 all-gather.3.cloned.1.call-update
  8.0 1.1 fusion.35
  9.1 4.4 collective-permute-start
  13.5 1.3 collective-permute-start.1
  14.8 21.2 %collective-permute-done = bf16[1,8,128,128]{3,2,1,0:T(8,128)(2,1)S(1)} collective-permute-done((bf16[1,8,128,128]{3,2,1,0:T(8,128)(2,1)S(1)}, bf16[1,8,128,128]{3,2,1,0:T(8,128)(2,1)S(1)}, u32[]{:S(2)}, u32[]{:S(2)}) %collective-permute-start) | collective-permute-done | bytes 262176 | tf_op jit(solution)/shard_map/ppermute | solution.py:14
  36.3 1.5 copy-done
  37.9 8.6 %collective-permute-start.2 = (bf16[10,1,128,128]{3,2,1,0:T(8,128)(2,1)S(1)}, bf16[10,1,128,128]{3,2,1,0:T(8,128)(2,1)S(1)}, u32[]{:S(2)}, u32[]{:S(2)}) collective-permute-start(bf16[10,1,128,128]{3,2,1,0:T(8,128)(2,1)S(1)} %get-tuple-element.97), channel_id=1, source_target_pairs={{0,1},{1,2},{2,3},{3,4},{4,5},{5,6},{6,7},{7,8},{8,9},{9,10},{10,1... | collective-permute-start | bytes 983048 | tf_op jit(solution)/shard_map/ppermute | solution.py:14
  46.5 1.9 collective-permute-start.3
  48.5 18.1 %collective-permute-done.2 = bf16[10,1,128,128]{3,2,1,0:T(8,128)(2,1)S(1)} collective-permute-done((bf16[10,1,128,128]{3,2,1,0:T(8,128)(2,1)S(1)}, bf16[10,1,128,128]{3,2,1,0:T(8,128)(2,1)S(1)}, u32[]{:S(2)}, u32[]{:S(2)}) %collective-permute-start.2) | collective-permute-done | bytes 327712 | tf_op jit(solution)/shard_map/ppermute | solution.py:14
  66.6 0.7 copy-done.2
  67.4 3.9 collective-permute-done.3
  71.3 2.3 pad_maximum_fusion
  73.6 116.1 %all-gather.5.cloned.1.call-done = bf16[8,32,128,128]{3,2,1,0:T(8,128)(2,1)} async-done(((bf16[8,4,128,128]{3,2,1,0:T(8,128)(2,1)}), bf16[8,32,128,128]{3,2,1,0:T(8,128)(2,1)}) %all-gather.5.cloned.1.call-update) | async-done | bytes 8388624 | tf_op jit(solution)/shard_map/all_gather | solution.py:42
  189.6 84.0 %all-gather.3.cloned.1.call-done = bf16[8,32,128,128]{3,2,1,0:T(8,128)(2,1)} async-done(((bf16[8,2,128,128]{3,2,1,0:T(8,128)(2,1)}), bf16[8,32,128,128]{3,2,1,0:T(8,128)(2,1)}) %all-gather.3.cloned.1.call-update) | async-done | bytes 8388624 | tf_op jit(solution)/shard_map/all_gather | solution.py:41
  273.6 179.0 %while.11 = (s32[]{:T(128)}, f32[8,8,128,128]{3,2,1,0:T(8,128)}, s32[8]{0:T(128)S(1)}, s32[32]{0:T(128)S(1)}, bf16[10,10,128,128]{3,2,1,0:T(8,128)(2,1)S(1)}, /*...) while((s32[]{:T(128)}, f32[8,8,128,128]{3,2,1,0:T(8,128)}, ...), condition=%wide.region_1.2_spmd.clone, body=%wide.region_0.1_spmd.clone.sunk | while | flops 2155874304 | bytes 35137248 | solution.py:34
  276.6 10.0 %gather_fusion = bf16[256,128,128]{2,1,0:T(8,128)(2,1)} fusion(bf16[10,10,128,128]{3,2,1,0:T(8,128)(2,1)S(1)} %get-tuple-element.192, s32[256]{0:T(256)S(1)} %reshape.52), kind=kCustom, calls=%fused_computation.clone.clone.1 | custom fusion | bytes 16779264 | tf_op jit(solution)/shard_map/while/body/eval_jaxpr/gather | solution.py:27
  286.6 9.4 %fusion.50 = f32[8,8,128,128]{3,2,1,0:T(8,128)} fusion(f32[8,8,128,128]{3,2,1,0:T(8,128)} %get-tuple-element.176, s32[]{:T(128)} %get-tuple-element.175, bf16[8,32,128,128]{3,2,1,0:T(8,128)(2,1)} %get-tuple-element.195, bf16[32,8,128,128]{3,2,1,0:T(8,128)(2,1)} %bitcast.45, bf16[32,8]{0,1:T(8,128)(2,1)S(1)} %dynamic-slice_bitcast_fusion.2, ...), kind=kOutput, calls=%fused_computation.10.clone.1 | convolution fusion | flops 2155872256 | bytes 18351108 | tf_op jit(solution)/shard_map/while/body/eval_jaxpr/wcik,cwdk->cid/dot_general | solution.py:32
  299.0 10.0 %gather_fusion = bf16[256,128,128]{2,1,0:T(8,128)(2,1)} fusion(bf16[10,10,128,128]{3,2,1,0:T(8,128)(2,1)S(1)} %get-tuple-element.192, s32[256]{0:T(256)S(1)} %reshape.52), kind=kCustom, calls=%fused_computation.clone.clone.1 | custom fusion | bytes 16779264 | tf_op jit(solution)/shard_map/while/body/eval_jaxpr/gather | solution.py:27
  309.0 9.4 %fusion.50 = f32[8,8,128,128]{3,2,1,0:T(8,128)} fusion(f32[8,8,128,128]{3,2,1,0:T(8,128)} %get-tuple-element.176, s32[]{:T(128)} %get-tuple-element.175, bf16[8,32,128,128]{3,2,1,0:T(8,128)(2,1)} %get-tuple-element.195, bf16[32,8,128,128]{3,2,1,0:T(8,128)(2,1)} %bitcast.45, bf16[32,8]{0,1:T(8,128)(2,1)S(1)} %dynamic-slice_bitcast_fusion.2, ...), kind=kOutput, calls=%fused_computation.10.clone.1 | convolution fusion | flops 2155872256 | bytes 18351108 | tf_op jit(solution)/shard_map/while/body/eval_jaxpr/wcik,cwdk->cid/dot_general | solution.py:32
  321.4 10.0 %gather_fusion = bf16[256,128,128]{2,1,0:T(8,128)(2,1)} fusion(bf16[10,10,128,128]{3,2,1,0:T(8,128)(2,1)S(1)} %get-tuple-element.192, s32[256]{0:T(256)S(1)} %reshape.52), kind=kCustom, calls=%fused_computation.clone.clone.1 | custom fusion | bytes 16779264 | tf_op jit(solution)/shard_map/while/body/eval_jaxpr/gather | solution.py:27
  331.3 9.4 %fusion.50 = f32[8,8,128,128]{3,2,1,0:T(8,128)} fusion(f32[8,8,128,128]{3,2,1,0:T(8,128)} %get-tuple-element.176, s32[]{:T(128)} %get-tuple-element.175, bf16[8,32,128,128]{3,2,1,0:T(8,128)(2,1)} %get-tuple-element.195, bf16[32,8,128,128]{3,2,1,0:T(8,128)(2,1)} %bitcast.45, bf16[32,8]{0,1:T(8,128)(2,1)S(1)} %dynamic-slice_bitcast_fusion.2, ...), kind=kOutput, calls=%fused_computation.10.clone.1 | convolution fusion | flops 2155872256 | bytes 18351108 | tf_op jit(solution)/shard_map/while/body/eval_jaxpr/wcik,cwdk->cid/dot_general | solution.py:32
  343.8 10.0 %gather_fusion = bf16[256,128,128]{2,1,0:T(8,128)(2,1)} fusion(bf16[10,10,128,128]{3,2,1,0:T(8,128)(2,1)S(1)} %get-tuple-element.192, s32[256]{0:T(256)S(1)} %reshape.52), kind=kCustom, calls=%fused_computation.clone.clone.1 | custom fusion | bytes 16779264 | tf_op jit(solution)/shard_map/while/body/eval_jaxpr/gather | solution.py:27
  353.7 9.4 %fusion.50 = f32[8,8,128,128]{3,2,1,0:T(8,128)} fusion(f32[8,8,128,128]{3,2,1,0:T(8,128)} %get-tuple-element.176, s32[]{:T(128)} %get-tuple-element.175, bf16[8,32,128,128]{3,2,1,0:T(8,128)(2,1)} %get-tuple-element.195, bf16[32,8,128,128]{3,2,1,0:T(8,128)(2,1)} %bitcast.45, bf16[32,8]{0,1:T(8,128)(2,1)S(1)} %dynamic-slice_bitcast_fusion.2, ...), kind=kOutput, calls=%fused_computation.10.clone.1 | convolution fusion | flops 2155872256 | bytes 18351108 | tf_op jit(solution)/shard_map/while/body/eval_jaxpr/wcik,cwdk->cid/dot_general | solution.py:32
  366.1 10.0 %gather_fusion = bf16[256,128,128]{2,1,0:T(8,128)(2,1)} fusion(bf16[10,10,128,128]{3,2,1,0:T(8,128)(2,1)S(1)} %get-tuple-element.192, s32[256]{0:T(256)S(1)} %reshape.52), kind=kCustom, calls=%fused_computation.clone.clone.1 | custom fusion | bytes 16779264 | tf_op jit(solution)/shard_map/while/body/eval_jaxpr/gather | solution.py:27
  376.1 9.4 %fusion.50 = f32[8,8,128,128]{3,2,1,0:T(8,128)} fusion(f32[8,8,128,128]{3,2,1,0:T(8,128)} %get-tuple-element.176, s32[]{:T(128)} %get-tuple-element.175, bf16[8,32,128,128]{3,2,1,0:T(8,128)(2,1)} %get-tuple-element.195, bf16[32,8,128,128]{3,2,1,0:T(8,128)(2,1)} %bitcast.45, bf16[32,8]{0,1:T(8,128)(2,1)S(1)} %dynamic-slice_bitcast_fusion.2, ...), kind=kOutput, calls=%fused_computation.10.clone.1 | convolution fusion | flops 2155872256 | bytes 18351108 | tf_op jit(solution)/shard_map/while/body/eval_jaxpr/wcik,cwdk->cid/dot_general | solution.py:32
  388.5 10.0 %gather_fusion = bf16[256,128,128]{2,1,0:T(8,128)(2,1)} fusion(bf16[10,10,128,128]{3,2,1,0:T(8,128)(2,1)S(1)} %get-tuple-element.192, s32[256]{0:T(256)S(1)} %reshape.52), kind=kCustom, calls=%fused_computation.clone.clone.1 | custom fusion | bytes 16779264 | tf_op jit(solution)/shard_map/while/body/eval_jaxpr/gather | solution.py:27
  398.5 9.4 %fusion.50 = f32[8,8,128,128]{3,2,1,0:T(8,128)} fusion(f32[8,8,128,128]{3,2,1,0:T(8,128)} %get-tuple-element.176, s32[]{:T(128)} %get-tuple-element.175, bf16[8,32,128,128]{3,2,1,0:T(8,128)(2,1)} %get-tuple-element.195, bf16[32,8,128,128]{3,2,1,0:T(8,128)(2,1)} %bitcast.45, bf16[32,8]{0,1:T(8,128)(2,1)S(1)} %dynamic-slice_bitcast_fusion.2, ...), kind=kOutput, calls=%fused_computation.10.clone.1 | convolution fusion | flops 2155872256 | bytes 18351108 | tf_op jit(solution)/shard_map/while/body/eval_jaxpr/wcik,cwdk->cid/dot_general | solution.py:32
  410.9 10.0 %gather_fusion = bf16[256,128,128]{2,1,0:T(8,128)(2,1)} fusion(bf16[10,10,128,128]{3,2,1,0:T(8,128)(2,1)S(1)} %get-tuple-element.192, s32[256]{0:T(256)S(1)} %reshape.52), kind=kCustom, calls=%fused_computation.clone.clone.1 | custom fusion | bytes 16779264 | tf_op jit(solution)/shard_map/while/body/eval_jaxpr/gather | solution.py:27
  420.8 9.4 %fusion.50 = f32[8,8,128,128]{3,2,1,0:T(8,128)} fusion(f32[8,8,128,128]{3,2,1,0:T(8,128)} %get-tuple-element.176, s32[]{:T(128)} %get-tuple-element.175, bf16[8,32,128,128]{3,2,1,0:T(8,128)(2,1)} %get-tuple-element.195, bf16[32,8,128,128]{3,2,1,0:T(8,128)(2,1)} %bitcast.45, bf16[32,8]{0,1:T(8,128)(2,1)S(1)} %dynamic-slice_bitcast_fusion.2, ...), kind=kOutput, calls=%fused_computation.10.clone.1 | convolution fusion | flops 2155872256 | bytes 18351108 | tf_op jit(solution)/shard_map/while/body/eval_jaxpr/wcik,cwdk->cid/dot_general | solution.py:32
  433.2 10.0 %gather_fusion = bf16[256,128,128]{2,1,0:T(8,128)(2,1)} fusion(bf16[10,10,128,128]{3,2,1,0:T(8,128)(2,1)S(1)} %get-tuple-element.192, s32[256]{0:T(256)S(1)} %reshape.52), kind=kCustom, calls=%fused_computation.clone.clone.1 | custom fusion | bytes 16779264 | tf_op jit(solution)/shard_map/while/body/eval_jaxpr/gather | solution.py:27
  443.2 9.4 %fusion.50 = f32[8,8,128,128]{3,2,1,0:T(8,128)} fusion(f32[8,8,128,128]{3,2,1,0:T(8,128)} %get-tuple-element.176, s32[]{:T(128)} %get-tuple-element.175, bf16[8,32,128,128]{3,2,1,0:T(8,128)(2,1)} %get-tuple-element.195, bf16[32,8,128,128]{3,2,1,0:T(8,128)(2,1)} %bitcast.45, bf16[32,8]{0,1:T(8,128)(2,1)S(1)} %dynamic-slice_bitcast_fusion.2, ...), kind=kOutput, calls=%fused_computation.10.clone.1 | convolution fusion | flops 2155872256 | bytes 18351108 | tf_op jit(solution)/shard_map/while/body/eval_jaxpr/wcik,cwdk->cid/dot_general | solution.py:32
  (69 shorter events, 6.9 us)
Async XLA Ops:
  6.5 29.4 %copy-start.1 = (bf16[8,8,128,128]{3,2,1,0:T(8,128)(2,1)S(1)}, bf16[8,8,128,128]{3,2,1,0:T(8,128)(2,1)}, u32[]{:S(2)}) copy-start(bf16[8,8,128,128]{3,2,1,0:T(8,128)(2,1)} %param.10) | copy-start | bytes 6291460
  6.5 183.1 %all-gather.5.cloned.1.call-start = ((), (), s32[]{:S(2)}) async-start(), calls=%async_computation.1 | async-start | bytes 9437184 | tf_op jit(solution)/shard_map/all_gather | solution.py:42
  7.3 41.2 %copy-start.3 = (s32[8,8,32]{2,1,0:T(8,128)S(1)}, s32[8,8,32]{2,1,0:T(8,128)}, u32[]{:S(2)}) copy-start(s32[8,8,32]{2,1,0:T(8,128)} %param.13) | copy-start | bytes 24580
  7.3 266.3 %all-gather.3.cloned.1.call-start = ((), (), s32[]{:S(2)}) async-start(), calls=%async_computation | async-start | bytes 8912896 | tf_op jit(solution)/shard_map/all_gather | solution.py:41
  9.1 26.9 %collective-permute-start = (bf16[1,8,128,128]{3,2,1,0:T(8,128)(2,1)S(1)}, bf16[1,8,128,128]{3,2,1,0:T(8,128)(2,1)S(1)}, u32[]{:S(2)}, u32[]{:S(2)}) collective-permute-start(bf16[1,8,128,128]{3,2,1,0:T(8,128)(2,1)S(1)} %get-tuple-element.100), channel_id=1, source_target_pairs={{0,16},{16,32},{32,48},{48,64},{64,80},{80,96},{96,112},{1,17},{17... | collective-permute-start | bytes 786440 | tf_op jit(solution)/shard_map/ppermute | solution.py:14
  13.5 22.8 %collective-permute-start.1 = (bf16[1,8,128,128]{3,2,1,0:T(8,128)(2,1)S(1)}, bf16[1,8,128,128]{3,2,1,0:T(8,128)(2,1)S(1)}, u32[]{:S(2)}, u32[]{:S(2)}) collective-permute-start(bf16[1,8,128,128]{3,2,1,0:T(8,128)(2,1)S(1)} %get-tuple-element.99), channel_id=1, source_target_pairs={{16,0},{32,16},{48,32},{64,48},{80,64},{96,80},{112,96},{17,1},{33... | collective-permute-start | bytes 786440 | tf_op jit(solution)/shard_map/ppermute | solution.py:15
  36.3 237.3 %copy-start.4 = (s32[32]{0:T(128)S(1)}, s32[32]{0:T(128)}, u32[]{:S(2)}) copy-start(s32[32]{0:T(128)} %param.12) | copy-start | bytes 388
  36.3 237.3 %copy-start.5 = (s32[32]{0:T(128)S(1)}, s32[32]{0:T(128)}, u32[]{:S(2)}) copy-start(s32[32]{0:T(128)} %param.11) | copy-start | bytes 388
  36.3 1.5 copy-start
  37.9 28.8 %collective-permute-start.2 = (bf16[10,1,128,128]{3,2,1,0:T(8,128)(2,1)S(1)}, bf16[10,1,128,128]{3,2,1,0:T(8,128)(2,1)S(1)}, u32[]{:S(2)}, u32[]{:S(2)}) collective-permute-start(bf16[10,1,128,128]{3,2,1,0:T(8,128)(2,1)S(1)} %get-tuple-element.97), channel_id=1, source_target_pairs={{0,1},{1,2},{2,3},{3,4},{4,5},{5,6},{6,7},{7,8},{8,9},{9,10},{10,1... | collective-permute-start | bytes 983048 | tf_op jit(solution)/shard_map/ppermute | solution.py:14
  46.5 24.8 %collective-permute-start.3 = (bf16[10,1,128,128]{3,2,1,0:T(8,128)(2,1)S(1)}, bf16[10,1,128,128]{3,2,1,0:T(8,128)(2,1)}, u32[]{:S(2)}, u32[]{:S(2)}) collective-permute-start(bf16[10,1,128,128]{3,2,1,0:T(8,128)(2,1)S(1)} %get-tuple-element.98), channel_id=1, source_target_pairs={{1,0},{2,1},{3,2},{4,3},{5,4},{6,5},{7,6},{8,7},{9,8},{10,9},{11,1... | collective-permute-start | bytes 983048 | tf_op jit(solution)/shard_map/ppermute | solution.py:15
  66.6 0.7 copy-start.2
Sparse Core Ops, SparseCore 0:
  9.0 180.5 all-gather.4
  192.1 81.4 all-gather.2
where the time goes:
time: 460 us; the launch traced here: 459 us
  waiting for transfers between devices  245 us (53%)
  local copies, waits for them, and re-layouts  89.1 us (19%)
  matrix products  75.2 us (16%)
  loops' own time  17.7 us (4%)
  starting transfers between devices  16.3 us (4%)
  between operations  13.5 us (3%)
    all_gather x1, waiting for transfers between devices, per_device(): right_all = lax.all_gather(right_env, 'grp', axis=1, tiled=True)  116 us
    all_gather x1, waiting for transfers between devices, per_device(): left_all = lax.all_gather(left_env, 'wide', axis=1, tiled=True)  84 us
    gather x8, local copies, waits for them, and re-layouts, one_row(): picked = padded[row_ids[:, None], col_ids]  79.6 us
    dot_general x8, matrix products, one_row(): jnp.einsum('wcik,cwdk->cid', inner, right_part, preferred_element_type=jn...  75.2 us
    ppermute x2, waiting for transfers between devices, with_halo(): before = lax.ppermute(last, axis, up)  39.3 us
    another operation x1, loops' own time, add_terms(): return lax.map(one_row, jnp.arange(rows, dtype=jnp.int32))  17.7 us
    ppermute x2, starting transfers between devices, with_halo(): before = lax.ppermute(last, axis, up)  13 us
  transfers between devices with their start and end apart: 6, of which 5 were waited for; matrix products, arithmetic and copies ran while one was open for 1% of the time, Pallas kernels for 0%

commit v1 on v0

v1 whole, which is shorter than its diff:
```python
import functools

import jax
import jax.numpy as jnp
from jax import lax
from jax.experimental import pallas as pl
from jax.experimental.pallas import tpu as pltpu
from jax.sharding import Mesh, PartitionSpec as P

GRP = ("x", "zl")
WIDE = ("y", "zh", "core")
SIZES = (4, 2, 4, 2, 2)
B = 128
ROWS = 8
COLS = 8
TERMS = 4


def terms_kernel(layout, offsets, first, place, ls, rs, act, *refs):
    la, lac, lz, lzc, psi, up, down, west, east = refs[:9]
    rights, rest = [], refs[9:]
    for pieces in layout:
        rights.append(rest[:pieces])
        rest = rest[pieces:]
    if first:
        hout, lbuf, rbuf, grid, inner, psem, lsem, rsem = rest
    else:
        hin, hout, lbuf, rbuf, grid, inner, psem, lsem, rsem = rest
    steps = len(layout)
    n = pl.program_id(0)
    here = place[0]
    core, zh, y, zl, x = here & 1, (here >> 1) & 1, (here >> 2) & 3, (here >> 4) & 1, here >> 5

    def chunk(step):
        return (x + offsets[step][0]) & 3, (zl + offsets[step][1]) & 1

    def left_copies(step, slot, own):
        p, _ = chunk(step)
        a, b, where = (la, lac, p) if own else (lz, lzc, (p - y) & 3)
        return (
            pltpu.make_async_copy(a.at[where], lbuf.at[slot, core], lsem.at[slot, 0]),
            pltpu.make_async_copy(b.at[where], lbuf.at[slot, 1 - core], lsem.at[slot, 1]),
        )

    def right_copies(step, slot):
        pieces = rights[step]
        sources = pieces if len(pieces) == 2 else [pieces[0].at[pl.ds(4 * h, 4)] for h in range(2)]
        return [
            pltpu.make_async_copy(sources[h], rbuf.at[slot, pl.ds(4 * h, 4)], rsem.at[slot, h])
            for h in range(2)
        ]

    def fetch(step, slot):
        for copy in right_copies(step, slot):
            copy.start()

        @pl.when(chunk(step)[1] == zh)
        def _():
            for copy in left_copies(step, slot, True):
                copy.start()

        @pl.when(chunk(step)[1] != zh)
        def _():
            for copy in left_copies(step, slot, False):
                copy.start()

    psi_copies = [
        pltpu.make_async_copy(psi, grid.at[pl.ds(1, ROWS), pl.ds(1, COLS)], psem.at[0]),
        pltpu.make_async_copy(up, grid.at[pl.ds(0, 1), pl.ds(1, COLS)], psem.at[1]),
        pltpu.make_async_copy(down, grid.at[pl.ds(ROWS + 1, 1), pl.ds(1, COLS)], psem.at[2]),
        pltpu.make_async_copy(west, grid.at[:, pl.ds(0, 1)], psem.at[3]),
        pltpu.make_async_copy(east, grid.at[:, pl.ds(COLS + 1, 1)], psem.at[4]),
    ]

    @pl.when(n == 0)
    def _():
        for copy in psi_copies:
            copy.start()
        fetch(0, 0)

    for step in range(1, steps):

        @pl.when(n == step - 1)
        def _():
            fetch(step, step % 2)

    @pl.when(n == 0)
    def _():
        for copy in psi_copies:
            copy.wait()

    slot = lax.rem(n, 2)
    for copy in left_copies(0, slot, True):
        copy.wait()
    for copy in right_copies(0, slot):
        copy.wait()

    base = 0
    for step in range(steps):
        p, q = chunk(step)
        base = jnp.where(n == step, TERMS * (2 * p + q), base)

    def one_row(row, carry):
        for w in range(TERMS):
            picked = grid[row + 1 + ls[base + w], pl.ds(1 + rs[base + w], COLS)]
            joined = jnp.concatenate([picked[c] for c in range(COLS)], axis=1)
            part = jnp.dot(lbuf[slot, w // 2, row, w % 2], joined, preferred_element_type=jnp.float32)
            for c in range(COLS):
                on = act[row, c, base + w].astype(jnp.float32)
                inner[c, pl.ds(pl.multiple_of(row * B, B), B), w * B : (w + 1) * B] = (
                    part[:, c * B : (c + 1) * B] * on
                ).astype(jnp.bfloat16)
        return carry

    lax.fori_loop(0, ROWS, one_row, 0, unroll=True)

    for c in range(COLS):
        joined = jnp.concatenate([rbuf[slot, c, w] for w in range(TERMS)], axis=1)
        part = lax.dot_general(
            inner[c], joined, (((1,), (1,)), ((), ())), preferred_element_type=jnp.float32
        ).reshape(ROWS, B, B)

        @pl.when(n == 0)
        def _():
            hout[:, c] = part if first else hin[:, c] + part

        @pl.when(n != 0)
        def _():
            hout[:, c] += part


def add_terms(offsets, place, ls, rs, act, lefts, psis, rights, total):
    steps = len(rights)
    layout = tuple(len(pieces) for pieces in rights)
    first = total is None
    anywhere = pl.BlockSpec(memory_space=pl.ANY)
    whole = pl.BlockSpec((ROWS, COLS, B, B), lambda n, *_: (0, 0, 0, 0), pipeline_mode=pl.Buffered(1))
    operands = [*lefts, *psis, *(piece for pieces in rights for piece in pieces)]
    in_specs = [anywhere] * len(operands)
    if not first:
        operands.append(total)
        in_specs.append(whole)
    return pl.pallas_call(
        functools.partial(terms_kernel, layout, offsets, first),
        out_shape=jax.ShapeDtypeStruct((ROWS, COLS, B, B), jnp.float32),
        grid_spec=pltpu.PrefetchScalarGridSpec(
            num_scalar_prefetch=4,
            grid=(steps,),
            in_specs=in_specs,
            out_specs=whole,
            scratch_shapes=[
                pltpu.VMEM((2, 2, ROWS, 2, B, B), jnp.bfloat16),
                pltpu.VMEM((2, COLS, TERMS, B, B), jnp.bfloat16),
                pltpu.VMEM((ROWS + 2, COLS + 2, B, B), jnp.bfloat16),
                pltpu.VMEM((COLS, ROWS * B, TERMS * B), jnp.bfloat16),
                pltpu.SemaphoreType.DMA((5,)),
                pltpu.SemaphoreType.DMA((2, 2)),
                pltpu.SemaphoreType.DMA((2, 2)),
            ],
        ),
        input_output_aliases={} if first else {4 + len(operands) - 1: 0},
        compiler_params=pltpu.CompilerParams(
            vmem_limit_bytes=56 << 20, dimension_semantics=("arbitrary",)
        ),
        cost_estimate=pl.CostEstimate(
            flops=steps * 2 * 2 * ROWS * COLS * TERMS * B**3,
            bytes_accessed=(steps * 2 + 11) << 20,
            transcendentals=0,
        ),
    )(place, ls, rs, act, *operands)


def ring(value, axis, shift):
    return lax.ppermute(value, axis, [(i, (i + shift) % 4) for i in range(4)])


def swap(value, axis):
    return lax.ppermute(value, axis, [(0, 1), (1, 0)])


def edges(value, axes, dim):
    count = lax.axis_size(axes)
    length = value.shape[dim]
    up = [(i, i + 1) for i in range(count - 1)]
    down = [(j, i) for i, j in up]
    last = lax.slice_in_dim(value, length - 1, length, axis=dim)
    leading = lax.slice_in_dim(value, 0, 1, axis=dim)
    return lax.ppermute(last, axes, up), lax.ppermute(leading, axes, down)


def after(values, events):
    held = lax.optimization_barrier((tuple(values), tuple(events)))
    return held[0]


def per_device(left_env, right_env, psi, left_shift, right_shift, active):
    place = lax.axis_index((*GRP, *WIDE)).astype(jnp.int32)[None]

    left_y = lax.all_gather(left_env, "y", axis=0)
    right_m = ring(right_env, "x", 1)
    right_p = ring(right_env, "x", -1)
    left_z = swap(left_env, "zh")
    north, south = edges(psi, GRP, 0)

    right_m, right_p, left_z, north, south, own = after(
        (right_m, right_p, left_z, north, south, right_env), ()
    )
    right_z = swap(own, "zl")
    far_0 = ring(right_m[:4], "x", 1)
    far_1 = ring(right_p[4:], "x", -1)
    left_zm = ring(left_z, "y", 1)
    left_zp = ring(left_z, "y", -1)
    left_z2 = ring(left_z, "y", 2)
    sides = jnp.concatenate([north[:, ::7], psi[:, ::7], south[:, ::7]], axis=0)
    west = lax.ppermute(sides[:, 1:], WIDE, [(i, i + 1) for i in range(15)])
    east = lax.ppermute(sides[:, :1], WIDE, [(i + 1, i) for i in range(15)])

    right_z, far_0, far_1 = after((right_z, far_0, far_1), ())
    right_zm = ring(right_z, "x", 1)
    right_zp = ring(right_z, "x", -1)
    far_z0 = swap(far_0, "zl")
    far_z1 = swap(far_1, "zl")
    left_yc = swap(left_y, "core")
    left_zs = jnp.stack([left_z, left_zp, left_z2, left_zm])
    left_zc = swap(left_zs, "core")

    shared = (
        place,
        left_shift,
        right_shift,
        active,
        (left_y, left_yc, left_zs, left_zc),
        (psi, north, south, west, east),
    )
    total = add_terms(
        ((0, 0), (0, 1), (3, 0), (1, 0), (2, 0)),
        *shared,
        [(right_env,), (right_z,), (right_m,), (right_p,), (far_0, far_1)],
        None,
    )
    return add_terms(
        ((3, 1), (1, 1), (2, 1)),
        *shared,
        [(right_zm,), (right_zp,), (far_z0, far_z1)],
        total,
    )


def solution(mesh):
    fine = Mesh(mesh.devices.reshape(SIZES), (*GRP, *WIDE))
    return jax.shard_map(
        per_device,
        mesh=fine,
        in_specs=(
            P(GRP, WIDE, None, None),
            P(WIDE, GRP, None, None),
            P(GRP, WIDE, None, None),
            P(),
            P(),
            P(GRP, WIDE, None),
        ),
        out_specs=P(GRP, WIDE, None, None),
        check_vma=False,
    )
```

time: 460 us -> 193 us (0.42)
  waiting for transfers between devices: 245 us -> 52.3 us
  local copies, waits for them, and re-layouts: 89.1 us -> 5.16 us
  Pallas kernels: 0 us -> 79.6 us
  matrix products: 75.2 us -> 0 us
  starting transfers between devices: 16.3 us -> 38.9 us
  loops' own time: 17.7 us -> 0 us
    all_gather x2 -> x1, waiting for transfers between devices: 200 us -> 0.01 us  [per_device(): left_y = lax.all_gather(left_env, 'y', axis=0)]
    gather x8 -> x0, local copies, waits for them, and re-layouts: 79.6 us -> none  [one_row(): picked = padded[row_ids[:, None], col_ids]]
    pallas_call x0 -> x2, Pallas kernels: none -> 79.6 us  [add_terms(): pl.pallas_call(functools.partial(terms_kernel, layout, offsets, first), o...]
    dot_general x8 -> x0, matrix products: 75.2 us -> none  [one_row(): jnp.einsum('wcik,cwdk->cid', inner, right_part, preferred_element_type=jn...]
    ppermute x4 -> x19, starting transfers between devices: 16.2 us -> 38.9 us  [the longest x9 15.9 us: ring(): return lax.ppermute(value, axis, [(i, (i + shift) % 4) for i in range(4)])]
    another operation x1 -> x0, loops' own time: 17.7 us -> none  [add_terms(): return lax.map(one_row, jnp.arange(rows, dtype=jnp.int32))]
    ppermute x4 -> x19, waiting for transfers between devices: 43.2 us -> 51.6 us  [the longest x9 37.4 us: ring(): return lax.ppermute(value, axis, [(i, (i + shift) % 4) for i in range(4)])]
  transfers between devices with their start and end apart: 6 -> 20, of which waited for: 5 -> 8; matrix products, arithmetic and copies ran while one was open for 1% -> 2% of each run, Pallas kernels for 0% -> 25%
where the time goes in v1:
time: 193 us; the launch traced here: 190 us
  Pallas kernels  79.6 us (41%)
  waiting for transfers between devices  52.3 us (27%)
  starting transfers between devices  38.9 us (20%)
  between operations  13.6 us (7%)
  local copies, waits for them, and re-layouts  5.16 us (3%)
    pallas_call x2, Pallas kernels, add_terms(): pl.pallas_call(functools.partial(terms_kernel, layout, offsets, first), o...  79.6 us
    ppermute x9, waiting for transfers between devices, ring(): return lax.ppermute(value, axis, [(i, (i + shift) % 4) for i in range(4)])  37.4 us
    ppermute x9, starting transfers between devices, ring(): return lax.ppermute(value, axis, [(i, (i + shift) % 4) for i in range(4)])  15.9 us
    ppermute x2, waiting for transfers between devices, edges(): return (lax.ppermute(last, axes, up), lax.ppermute(leading, axes, down))  11.3 us
    ppermute x6, starting transfers between devices, swap(): return lax.ppermute(value, axis, [(0, 1), (1, 0)])  8.35 us
    ppermute x1, starting transfers between devices, per_device(): west = lax.ppermute(sides[:, 1:], WIDE, [(i, i + 1) for i in range(15)])  6.63 us
    ppermute x2, starting transfers between devices, edges(): return (lax.ppermute(last, axes, up), lax.ppermute(leading, axes, down))  5.29 us
  transfers between devices with their start and end apart: 20, of which 8 were waited for; matrix products, arithmetic and copies ran while one was open for 2% of the time, Pallas kernels for 25%

profile of v1, /device:TPU:1, one launch (start us, length us, event | category | flops | bytes accessed | tf_op | source)
XLA Modules:
  0.0 190.0 jit_solution(999856713118028641)
XLA Ops:
  6.5 0.7 all-gather.3.cloned.1.call-update
  7.3 3.4 %collective-permute-start.2 = (bf16[8,4,128,128]{3,2,1,0:T(8,128)(2,1)}, bf16[8,4,128,128]{3,2,1,0:T(8,128)(2,1)S(1)}, u32[]{:S(2)}, u32[]{:S(2)}) collective-permute-start(bf16[8,4,128,128]{3,2,1,0:T(8,128)(2,1)} %refs_9_.1), channel_id=1, source_target_pairs={{0,96},{32,0},{64,32},{96,64},{1,97},{33,1},{65,33},{97,65},{2,98}... | collective-permute-start | bytes 3145736 | tf_op jit(solution)/shard_map/ppermute | solution.py:174
  10.6 3.6 %collective-permute-start.3 = (bf16[8,2,128,128]{3,2,1,0:T(8,128)(2,1)}, bf16[8,2,128,128]{3,2,1,0:T(8,128)(2,1)S(1)}, u32[]{:S(2)}, u32[]{:S(2)}) collective-permute-start(bf16[8,2,128,128]{3,2,1,0:T(8,128)(2,1)} %param.6), channel_id=1, source_target_pairs={{0,2},{2,0},{1,3},{3,1},{4,6},{6,4},{5,7},{7,5},{8,10},{10,8},{9,1... | collective-permute-start | bytes 1572872 | tf_op jit(solution)/shard_map/ppermute | solution.py:178
  14.2 1.1 fusion
  15.3 1.3 collective-permute-start.5
  16.6 4.0 %collective-permute-start.4 = (bf16[1,8,128,128]{3,2,1,0:T(8,128)(2,1)S(1)}, bf16[1,8,128,128]{3,2,1,0:T(8,128)(2,1)S(1)}, u32[]{:S(2)}, u32[]{:S(2)}) collective-permute-start(bf16[1,8,128,128]{3,2,1,0:T(8,128)(2,1)S(1)} %get-tuple-element.24), channel_id=1, source_target_pairs={{0,16},{16,32},{32,48},{48,64},{64,80},{80,96},{96,112},{1,17},{17... | collective-permute-start | bytes 786440 | tf_op jit(solution)/shard_map/ppermute | solution.py:188
  20.6 11.3 %collective-permute-done.5.refs_6_ = bf16[1,8,128,128]{3,2,1,0:T(8,128)(2,1)S(1)} collective-permute-done((bf16[1,8,128,128]{3,2,1,0:T(8,128)(2,1)S(1)}, bf16[1,8,128,128]{3,2,1,0:T(8,128)(2,1)S(1)}, u32[]{:S(2)}, u32[]{:S(2)}) %collective-permute-start.5) | collective-permute-done | bytes 262176 | tf_op jit(solution)/shard_map/ppermute | solution.py:188
  31.9 0.8 collective-permute-done.2.refs_12_
  32.8 3.1 %collective-permute-done.1.refs_11_ = bf16[8,4,128,128]{3,2,1,0:T(8,128)(2,1)S(1)} collective-permute-done((bf16[8,4,128,128]{3,2,1,0:T(8,128)(2,1)}, bf16[8,4,128,128]{3,2,1,0:T(8,128)(2,1)S(1)}, u32[]{:S(2)}, u32[]{:S(2)}) %collective-permute-start.1) | collective-permute-done | bytes 1048608 | tf_op jit(solution)/shard_map/ppermute | solution.py:174
  35.9 1.2 collective-permute-start.8
  37.1 2.7 %collective-permute-start.7 = (bf16[8,2,128,128]{3,2,1,0:T(8,128)(2,1)S(1)}, bf16[8,2,128,128]{3,2,1,0:T(8,128)(2,1)S(1)}, u32[]{:S(2)}, u32[]{:S(2)}) collective-permute-start(bf16[8,2,128,128]{3,2,1,0:T(8,128)(2,1)S(1)} %collective-permute-done.3), channel_id=1, source_target_pairs={{0,8},{4,12},{8,0},{12,4},{1,9},{5,13},{9,1},{13,5},{2,10},{6,14},... | collective-permute-start | bytes 1572872 | tf_op jit(solution)/shard_map/ppermute | solution.py:174
  39.8 1.0 collective-permute-start.6
  40.8 12.8 %collective-permute-done.8 = bf16[8,2,128,128]{3,2,1,0:T(8,128)(2,1)S(1)} collective-permute-done((bf16[8,2,128,128]{3,2,1,0:T(8,128)(2,1)S(1)}, bf16[8,2,128,128]{3,2,1,0:T(8,128)(2,1)S(1)}, u32[]{:S(2)}, u32[]{:S(2)}) %collective-permute-start.8) | collective-permute-done | bytes 524320 | tf_op jit(solution)/shard_map/ppermute | solution.py:174
  53.5 11.5 %collective-permute-done.7 = bf16[8,2,128,128]{3,2,1,0:T(8,128)(2,1)S(1)} collective-permute-done((bf16[8,2,128,128]{3,2,1,0:T(8,128)(2,1)S(1)}, bf16[8,2,128,128]{3,2,1,0:T(8,128)(2,1)S(1)}, u32[]{:S(2)}, u32[]{:S(2)}) %collective-permute-start.7) | collective-permute-done | bytes 524320 | tf_op jit(solution)/shard_map/ppermute | solution.py:174
  65.3 1.2 collective-permute-start.9
  66.6 2.0 %collective-permute-start.12 = (bf16[8,4,128,128]{3,2,1,0:T(8,128)(2,1)}, bf16[8,4,128,128]{3,2,1,0:T(8,128)(2,1)}, u32[]{:S(2)}, u32[]{:S(2)}) collective-permute-start(bf16[8,4,128,128]{3,2,1,0:T(8,128)(2,1)} %refs_9_.1), channel_id=1, source_target_pairs={{0,16},{16,0},{1,17},{17,1},{2,18},{18,2},{3,19},{19,3},{4,20},{20... | collective-permute-start | bytes 3145736 | tf_op jit(solution)/shard_map/ppermute | solution.py:178
  68.6 2.3 %collective-permute-start.14 = (bf16[4,4,128,128]{3,2,1,0:T(8,128)(2,1)S(1)}, bf16[4,4,128,128]{3,2,1,0:T(8,128)(2,1)S(1)}, u32[]{:S(2)}, u32[]{:S(2)}) collective-permute-start(bf16[4,4,128,128]{3,2,1,0:T(8,128)(2,1)S(1)} %slice.35), channel_id=1, source_target_pairs={{0,96},{32,0},{64,32},{96,64},{1,97},{33,1},{65,33},{97,65},{2,98}... | collective-permute-start | bytes 1572872 | tf_op jit(solution)/shard_map/ppermute | solution.py:174
  70.9 1.1 slice.34
  72.1 1.1 slice.30
  73.2 0.8 slice.29
  74.2 8.6 %collective-permute-done.14.refs_14_ = bf16[4,4,128,128]{3,2,1,0:T(8,128)(2,1)S(1)} collective-permute-done((bf16[4,4,128,128]{3,2,1,0:T(8,128)(2,1)S(1)}, bf16[4,4,128,128]{3,2,1,0:T(8,128)(2,1)S(1)}, u32[]{:S(2)}, u32[]{:S(2)}) %collective-permute-start.14) | collective-permute-done | bytes 524320 | tf_op jit(solution)/shard_map/ppermute | solution.py:174
  82.8 2.7 %collective-permute-start.11 = (bf16[10,1,128,128]{3,2,1,0:T(8,128)(2,1)S(1)}, bf16[10,1,128,128]{3,2,1,0:T(8,128)(2,1)S(1)}, u32[]{:S(2)}, u32[]{:S(2)}) collective-permute-start(bf16[10,1,128,128]{3,2,1,0:T(8,128)(2,1)S(1)} %get-tuple-element.25), channel_id=1, source_target_pairs={{1,0},{2,1},{3,2},{4,3},{5,4},{6,5},{7,6},{8,7},{9,8},{10,9},{11,1... | collective-permute-start | bytes 983048 | tf_op jit(solution)/shard_map/ppermute | solution.py:216
  85.5 0.6 collective-permute-done.13.refs_13_
  86.1 6.6 %collective-permute-start.10 = (bf16[10,1,128,128]{3,2,1,0:T(8,128)(2,1)S(1)}, bf16[10,1,128,128]{3,2,1,0:T(8,128)(2,1)}, u32[]{:S(2)}, u32[]{:S(2)}) collective-permute-start(bf16[10,1,128,128]{3,2,1,0:T(8,128)(2,1)S(1)} %get-tuple-element.26), channel_id=1, source_target_pairs={{0,1},{1,2},{2,3},{3,4},{4,5},{5,6},{6,7},{7,8},{8,9},{9,10},{10,1... | collective-permute-start | bytes 983048 | tf_op jit(solution)/shard_map/ppermute | solution.py:215
  92.7 2.9 %collective-permute-done.12.refs_10_ = bf16[8,4,128,128]{3,2,1,0:T(8,128)(2,1)} collective-permute-done((bf16[8,4,128,128]{3,2,1,0:T(8,128)(2,1)}, bf16[8,4,128,128]{3,2,1,0:T(8,128)(2,1)}, u32[]{:S(2)}, u32[]{:S(2)}) %collective-permute-start.12) | collective-permute-done | bytes 1048608 | tf_op jit(solution)/shard_map/ppermute | solution.py:178
  95.6 3.4 %collective-permute-start.16 = (bf16[8,4,128,128]{3,2,1,0:T(8,128)(2,1)}, bf16[8,4,128,128]{3,2,1,0:T(8,128)(2,1)}, u32[]{:S(2)}, u32[]{:S(2)}) collective-permute-start(bf16[8,4,128,128]{3,2,1,0:T(8,128)(2,1)} %collective-permute-done.12.refs_10_), channel_id=1, source_target_pairs={{0,96},{32,0},{64,32},{96,64},{1,97},{33,1},{65,33},{97,65},{2,98}... | collective-permute-start | bytes 3145736 | tf_op jit(solution)/shard_map/ppermute | solution.py:174
  99.0 1.9 %collective-permute-start.15 = (bf16[8,4,128,128]{3,2,1,0:T(8,128)(2,1)}, bf16[8,4,128,128]{3,2,1,0:T(8,128)(2,1)}, u32[]{:S(2)}, u32[]{:S(2)}) collective-permute-start(bf16[8,4,128,128]{3,2,1,0:T(8,128)(2,1)} %collective-permute-done.12.refs_10_), channel_id=1, source_target_pairs={{0,32},{32,64},{64,96},{96,0},{1,33},{33,65},{65,97},{97,1},{2,34}... | collective-permute-start | bytes 3145736 | tf_op jit(solution)/shard_map/ppermute | solution.py:174
  101.0 0.9 collective-permute-start.17
  101.8 0.6 collective-permute-start.18
  102.5 46.7 %shard_map.64.refs_13_ = f32[8,8,128,128]{3,2,1,0:T(8,128)} custom-call(s32[1]{0:T(128)} %bitcast.place, s32[32]{0:T(128)} %ls.3, s32[32]{0:T(128)} %rs.3, s32[8,8,32]{2,1,0:T(8,128)} %act.3, bf16[4,8,2,128,128]{4,3,2,1,0:T(8,128)(2,1)} %bitcast.11, bf16[4,8,2,128,128]{4,3,2,1,0:T(8,128)(2,1)} %collective-permute-done.refs_1_, ...), custom_call_target="tpu_custom_call" | custom-call | flops 10737418240 | bytes 22020096 | tf_op jit(solution)/shard_map/pallas_call | solution.py:143
  149.3 0.8 copy-done.7
  150.2 32.9 %shard_map.65 = f32[8,8,128,128]{3,2,1,0:T(8,128)} custom-call(s32[1]{0:T(128)} %bitcast.place, s32[32]{0:T(128)} %ls.3, s32[32]{0:T(128)} %rs.3, s32[8,8,32]{2,1,0:T(8,128)} %act.3, bf16[4,8,2,128,128]{4,3,2,1,0:T(8,128)(2,1)} %bitcast.12, bf16[4,8,2,128,128]{4,3,2,1,0:T(8,128)(2,1)} %collective-permute-done.refs_1_, ...), custom_call_target="tpu_custom_call", output_to_operand_aliasing={{}: (17, {})} | custom-call | flops 6442450944 | bytes 17825792 | tf_op jit(solution)/shard_map/pallas_call | solution.py:143
  (40 shorter events, 0.9 us)
Async XLA Ops:
  6.5 60.0 %all-gather.3.cloned.1.call-start = ((), (), s32[]{:S(2)}) async-start(), calls=%async_computation | async-start | bytes 2621440 | tf_op jit(solution)/shard_map/all_gather | solution.py:199
  7.3 25.5 %collective-permute-start.2 = (bf16[8,4,128,128]{3,2,1,0:T(8,128)(2,1)}, bf16[8,4,128,128]{3,2,1,0:T(8,128)(2,1)S(1)}, u32[]{:S(2)}, u32[]{:S(2)}) collective-permute-start(bf16[8,4,128,128]{3,2,1,0:T(8,128)(2,1)} %refs_9_.1), channel_id=1, source_target_pairs={{0,96},{32,0},{64,32},{96,64},{1,97},{33,1},{65,33},{97,65},{2,98}... | collective-permute-start | bytes 3145736 | tf_op jit(solution)/shard_map/ppermute | solution.py:174
  10.6 25.2 %collective-permute-start.1 = (bf16[8,4,128,128]{3,2,1,0:T(8,128)(2,1)}, bf16[8,4,128,128]{3,2,1,0:T(8,128)(2,1)S(1)}, u32[]{:S(2)}, u32[]{:S(2)}) collective-permute-start(bf16[8,4,128,128]{3,2,1,0:T(8,128)(2,1)} %refs_9_.1), channel_id=1, source_target_pairs={{0,32},{32,64},{64,96},{96,0},{1,33},{33,65},{65,97},{97,1},{2,34}... | collective-permute-start | bytes 3145736 | tf_op jit(solution)/shard_map/ppermute | solution.py:174
  10.6 21.3 %collective-permute-start.3 = (bf16[8,2,128,128]{3,2,1,0:T(8,128)(2,1)}, bf16[8,2,128,128]{3,2,1,0:T(8,128)(2,1)S(1)}, u32[]{:S(2)}, u32[]{:S(2)}) collective-permute-start(bf16[8,2,128,128]{3,2,1,0:T(8,128)(2,1)} %param.6), channel_id=1, source_target_pairs={{0,2},{2,0},{1,3},{3,1},{4,6},{6,4},{5,7},{7,5},{8,10},{10,8},{9,1... | collective-permute-start | bytes 1572872 | tf_op jit(solution)/shard_map/ppermute | solution.py:178
  15.3 16.6 %collective-permute-start.5 = (bf16[1,8,128,128]{3,2,1,0:T(8,128)(2,1)S(1)}, bf16[1,8,128,128]{3,2,1,0:T(8,128)(2,1)S(1)}, u32[]{:S(2)}, u32[]{:S(2)}) collective-permute-start(bf16[1,8,128,128]{3,2,1,0:T(8,128)(2,1)S(1)} %get-tuple-element.23), channel_id=1, source_target_pairs={{16,0},{32,16},{48,32},{64,48},{80,64},{96,80},{112,96},{17,1},{33... | collective-permute-start | bytes 786440 | tf_op jit(solution)/shard_map/ppermute | solution.py:188
  16.6 15.3 %collective-permute-start.4 = (bf16[1,8,128,128]{3,2,1,0:T(8,128)(2,1)S(1)}, bf16[1,8,128,128]{3,2,1,0:T(8,128)(2,1)S(1)}, u32[]{:S(2)}, u32[]{:S(2)}) collective-permute-start(bf16[1,8,128,128]{3,2,1,0:T(8,128)(2,1)S(1)} %get-tuple-element.24), channel_id=1, source_target_pairs={{0,16},{16,32},{32,48},{48,64},{64,80},{80,96},{96,112},{1,17},{17... | collective-permute-start | bytes 786440 | tf_op jit(solution)/shard_map/ppermute | solution.py:188
  31.9 70.5 %copy-start.3 = (bf16[1,8,128,128]{3,2,1,0:T(8,128)(2,1)}, bf16[1,8,128,128]{3,2,1,0:T(8,128)(2,1)S(1)}, u32[]{:S(2)}) copy-start(bf16[1,8,128,128]{3,2,1,0:T(8,128)(2,1)S(1)} %collective-permute-done.5.refs_6_) | copy-start | bytes 786436
  31.9 33.1 %copy-start.4 = (bf16[1,8,128,128]{3,2,1,0:T(8,128)(2,1)}, bf16[1,8,128,128]{3,2,1,0:T(8,128)(2,1)S(1)}, u32[]{:S(2)}) copy-start(bf16[1,8,128,128]{3,2,1,0:T(8,128)(2,1)S(1)} %collective-permute-done.4.refs_5_) | copy-start | bytes 786436
  32.8 35.8 %copy-start.1 = (bf16[8,4,128,128]{3,2,1,0:T(8,128)(2,1)}, bf16[8,4,128,128]{3,2,1,0:T(8,128)(2,1)S(1)}, u32[]{:S(2)}) copy-start(bf16[8,4,128,128]{3,2,1,0:T(8,128)(2,1)S(1)} %collective-permute-done.2.refs_12_) | copy-start | bytes 3145732
  35.9 29.1 %copy-start.2 = (bf16[8,4,128,128]{3,2,1,0:T(8,128)(2,1)}, bf16[8,4,128,128]{3,2,1,0:T(8,128)(2,1)S(1)}, u32[]{:S(2)}) copy-start(bf16[8,4,128,128]{3,2,1,0:T(8,128)(2,1)S(1)} %collective-permute-done.1.refs_11_) | copy-start | bytes 3145732
  35.9 17.6 %collective-permute-start.8 = (bf16[8,2,128,128]{3,2,1,0:T(8,128)(2,1)S(1)}, bf16[8,2,128,128]{3,2,1,0:T(8,128)(2,1)S(1)}, u32[]{:S(2)}, u32[]{:S(2)}) collective-permute-start(bf16[8,2,128,128]{3,2,1,0:T(8,128)(2,1)S(1)} %collective-permute-done.3), channel_id=1, source_target_pairs={{0,4},{4,8},{8,12},{12,0},{1,5},{5,9},{9,13},{13,1},{2,6},{6,10},{... | collective-permute-start | bytes 1572872 | tf_op jit(solution)/shard_map/ppermute | solution.py:174
  37.1 27.9 %collective-permute-start.7 = (bf16[8,2,128,128]{3,2,1,0:T(8,128)(2,1)S(1)}, bf16[8,2,128,128]{3,2,1,0:T(8,128)(2,1)S(1)}, u32[]{:S(2)}, u32[]{:S(2)}) collective-permute-start(bf16[8,2,128,128]{3,2,1,0:T(8,128)(2,1)S(1)} %collective-permute-done.3), channel_id=1, source_target_pairs={{0,8},{4,12},{8,0},{12,4},{1,9},{5,13},{9,1},{13,5},{2,10},{6,14},... | collective-permute-start | bytes 1572872 | tf_op jit(solution)/shard_map/ppermute | solution.py:174
  39.8 25.2 %collective-permute-start.6 = (bf16[8,2,128,128]{3,2,1,0:T(8,128)(2,1)S(1)}, bf16[8,2,128,128]{3,2,1,0:T(8,128)(2,1)S(1)}, u32[]{:S(2)}, u32[]{:S(2)}) collective-permute-start(bf16[8,2,128,128]{3,2,1,0:T(8,128)(2,1)S(1)} %collective-permute-done.3), channel_id=1, source_target_pairs={{0,12},{4,0},{8,4},{12,8},{1,13},{5,1},{9,5},{13,9},{2,14},{6,2},{... | collective-permute-start | bytes 1572872 | tf_op jit(solution)/shard_map/ppermute | solution.py:174
  65.3 8.9 %copy-start = (bf16[4,8,2,128,128]{4,3,2,1,0:T(8,128)(2,1)}, bf16[4,8,2,128,128]{4,3,2,1,0:T(8,128)(2,1)S(1)}, u32[]{:S(2)}) copy-start(bf16[4,8,2,128,128]{4,3,2,1,0:T(8,128)(2,1)S(1)} %pad_maximum_fusion.refs_2_) | copy-start | bytes 6291460
  65.3 36.5 %collective-permute-start.9 = (bf16[4,8,2,128,128]{4,3,2,1,0:T(8,128)(2,1)S(1)}, bf16[4,8,2,128,128]{4,3,2,1,0:T(8,128)(2,1)}, u32[]{:S(2)}, u32[]{:S(2)}) collective-permute-start(bf16[4,8,2,128,128]{4,3,2,1,0:T(8,128)(2,1)S(1)} %pad_maximum_fusion.refs_2_), channel_id=1, source_target_pairs={{0,1},{1,0},{2,3},{3,2},{4,5},{5,4},{6,7},{7,6},{8,9},{9,8},{10,11... | collective-permute-start | bytes 6291464 | tf_op jit(solution)/shard_map/ppermute | solution.py:178
  66.5 35.9 %collective-permute-start = (bf16[4,8,2,128,128]{4,3,2,1,0:T(8,128)(2,1)}, bf16[4,8,2,128,128]{4,3,2,1,0:T(8,128)(2,1)}, u32[]{:S(2)}, u32[]{:S(2)}) collective-permute-start(bf16[4,8,2,128,128]{4,3,2,1,0:T(8,128)(2,1)} %bitcast.10), channel_id=1, source_target_pairs={{0,1},{1,0},{2,3},{3,2},{4,5},{5,4},{6,7},{7,6},{8,9},{9,8},{10,11... | collective-permute-start | bytes 6291464 | tf_op jit(solution)/shard_map/ppermute | solution.py:178
  66.6 29.0 %collective-permute-start.12 = (bf16[8,4,128,128]{3,2,1,0:T(8,128)(2,1)}, bf16[8,4,128,128]{3,2,1,0:T(8,128)(2,1)}, u32[]{:S(2)}, u32[]{:S(2)}) collective-permute-start(bf16[8,4,128,128]{3,2,1,0:T(8,128)(2,1)} %refs_9_.1), channel_id=1, source_target_pairs={{0,16},{16,0},{1,17},{17,1},{2,18},{18,2},{3,19},{19,3},{4,20},{20... | collective-permute-start | bytes 3145736 | tf_op jit(solution)/shard_map/ppermute | solution.py:178
  68.6 14.2 %collective-permute-start.14 = (bf16[4,4,128,128]{3,2,1,0:T(8,128)(2,1)S(1)}, bf16[4,4,128,128]{3,2,1,0:T(8,128)(2,1)S(1)}, u32[]{:S(2)}, u32[]{:S(2)}) collective-permute-start(bf16[4,4,128,128]{3,2,1,0:T(8,128)(2,1)S(1)} %slice.35), channel_id=1, source_target_pairs={{0,96},{32,0},{64,32},{96,64},{1,97},{33,1},{65,33},{97,65},{2,98}... | collective-permute-start | bytes 1572872 | tf_op jit(solution)/shard_map/ppermute | solution.py:174
  72.0 14.1 %collective-permute-start.13 = (bf16[4,4,128,128]{3,2,1,0:T(8,128)(2,1)S(1)}, bf16[4,4,128,128]{3,2,1,0:T(8,128)(2,1)S(1)}, u32[]{:S(2)}, u32[]{:S(2)}) collective-permute-start(bf16[4,4,128,128]{3,2,1,0:T(8,128)(2,1)S(1)} %slice.34), channel_id=1, source_target_pairs={{0,32},{32,64},{64,96},{96,0},{1,33},{33,65},{65,97},{97,1},{2,34}... | collective-permute-start | bytes 1572872 | tf_op jit(solution)/shard_map/ppermute | solution.py:174
  82.8 19.6 %copy-start.5 = (bf16[4,4,128,128]{3,2,1,0:T(8,128)(2,1)}, bf16[4,4,128,128]{3,2,1,0:T(8,128)(2,1)S(1)}, u32[]{:S(2)}) copy-start(bf16[4,4,128,128]{3,2,1,0:T(8,128)(2,1)S(1)} %collective-permute-done.14.refs_14_) | copy-start | bytes 1572868
  82.8 16.2 %collective-permute-start.11 = (bf16[10,1,128,128]{3,2,1,0:T(8,128)(2,1)S(1)}, bf16[10,1,128,128]{3,2,1,0:T(8,128)(2,1)S(1)}, u32[]{:S(2)}, u32[]{:S(2)}) collective-permute-start(bf16[10,1,128,128]{3,2,1,0:T(8,128)(2,1)S(1)} %get-tuple-element.25), channel_id=1, source_target_pairs={{1,0},{2,1},{3,2},{4,3},{5,4},{6,5},{7,6},{8,7},{9,8},{10,9},{11,1... | collective-permute-start | bytes 983048 | tf_op jit(solution)/shard_map/ppermute | solution.py:216
  86.1 12.9 %copy-start.6 = (bf16[4,4,128,128]{3,2,1,0:T(8,128)(2,1)}, bf16[4,4,128,128]{3,2,1,0:T(8,128)(2,1)S(1)}, u32[]{:S(2)}) copy-start(bf16[4,4,128,128]{3,2,1,0:T(8,128)(2,1)S(1)} %collective-permute-done.13.refs_13_) | copy-start | bytes 1572868
  86.1 14.9 %collective-permute-start.10 = (bf16[10,1,128,128]{3,2,1,0:T(8,128)(2,1)S(1)}, bf16[10,1,128,128]{3,2,1,0:T(8,128)(2,1)}, u32[]{:S(2)}, u32[]{:S(2)}) collective-permute-start(bf16[10,1,128,128]{3,2,1,0:T(8,128)(2,1)S(1)} %get-tuple-element.26), channel_id=1, source_target_pairs={{0,1},{1,2},{2,3},{3,4},{4,5},{5,6},{6,7},{7,8},{8,9},{9,10},{10,1... | collective-permute-start | bytes 983048 | tf_op jit(solution)/shard_map/ppermute | solution.py:215
  95.6 53.6 %collective-permute-start.16 = (bf16[8,4,128,128]{3,2,1,0:T(8,128)(2,1)}, bf16[8,4,128,128]{3,2,1,0:T(8,128)(2,1)}, u32[]{:S(2)}, u32[]{:S(2)}) collective-permute-start(bf16[8,4,128,128]{3,2,1,0:T(8,128)(2,1)} %collective-permute-done.12.refs_10_), channel_id=1, source_target_pairs={{0,96},{32,0},{64,32},{96,64},{1,97},{33,1},{65,33},{97,65},{2,98}... | collective-permute-start | bytes 3145736 | tf_op jit(solution)/shard_map/ppermute | solution.py:174
  99.0 3.4 %copy-start.9 = (bf16[10,1,128,128]{3,2,1,0:T(8,128)(2,1)}, bf16[10,1,128,128]{3,2,1,0:T(8,128)(2,1)S(1)}, u32[]{:S(2)}) copy-start(bf16[10,1,128,128]{3,2,1,0:T(8,128)(2,1)S(1)} %collective-permute-done.11.refs_8_) | copy-start | bytes 983044
  99.0 50.2 %collective-permute-start.15 = (bf16[8,4,128,128]{3,2,1,0:T(8,128)(2,1)}, bf16[8,4,128,128]{3,2,1,0:T(8,128)(2,1)}, u32[]{:S(2)}, u32[]{:S(2)}) collective-permute-start(bf16[8,4,128,128]{3,2,1,0:T(8,128)(2,1)} %collective-permute-done.12.refs_10_), channel_id=1, source_target_pairs={{0,32},{32,64},{64,96},{96,0},{1,33},{33,65},{65,97},{97,1},{2,34}... | collective-permute-start | bytes 3145736 | tf_op jit(solution)/shard_map/ppermute | solution.py:174
  101.0 48.2 %collective-permute-start.17 = (bf16[4,4,128,128]{3,2,1,0:T(8,128)(2,1)}, bf16[4,4,128,128]{3,2,1,0:T(8,128)(2,1)S(1)}, u32[]{:S(2)}, u32[]{:S(2)}) collective-permute-start(bf16[4,4,128,128]{3,2,1,0:T(8,128)(2,1)} %copy-done.6), channel_id=1, source_target_pairs={{0,16},{16,0},{1,17},{17,1},{2,18},{18,2},{3,19},{19,3},{4,20},{20... | collective-permute-start | bytes 1572872 | tf_op jit(solution)/shard_map/ppermute | solution.py:178
  101.8 47.4 %collective-permute-start.18 = (bf16[4,4,128,128]{3,2,1,0:T(8,128)(2,1)S(1)}, bf16[4,4,128,128]{3,2,1,0:T(8,128)(2,1)S(1)}, u32[]{:S(2)}, u32[]{:S(2)}) collective-permute-start(bf16[4,4,128,128]{3,2,1,0:T(8,128)(2,1)S(1)} %collective-permute-done.14.refs_14_), channel_id=1, source_target_pairs={{0,16},{16,0},{1,17},{17,1},{2,18},{18,2},{3,19},{19,3},{4,20},{20... | collective-permute-start | bytes 1572872 | tf_op jit(solution)/shard_map/ppermute | solution.py:178
  149.2 0.8 copy-start.7
  149.2 1.0 copy-start.8
Sparse Core Ops, SparseCore 0:
  9.0 36.2 all-gather.2

commit v2 on v1

--- a/solution.py
+++ b/solution.py
@@ -16,9 +16,9 @@
 TERMS = 4
 
 
-def terms_kernel(layout, offsets, first, place, ls, rs, act, *refs):
-    la, lac, lz, lzc, psi, up, down, west, east = refs[:9]
-    rights, rest = [], refs[9:]
+def terms_kernel(layout, offsets, whole_ring, first, place, ls, rs, act, *refs):
+    left, left_other, psi, up, down, west, east = refs[:7]
+    rights, rest = [], refs[7:]
     for pieces in layout:
         rights.append(rest[:pieces])
         rest = rest[pieces:]
@@ -34,12 +34,12 @@
     def chunk(step):
         return (x + offsets[step][0]) & 3, (zl + offsets[step][1]) & 1
 
-    def left_copies(step, slot, own):
+    def left_copies(step, slot):
         p, _ = chunk(step)
-        a, b, where = (la, lac, p) if own else (lz, lzc, (p - y) & 3)
+        where = p if whole_ring else (p - y) & 3
         return (
-            pltpu.make_async_copy(a.at[where], lbuf.at[slot, core], lsem.at[slot, 0]),
-            pltpu.make_async_copy(b.at[where], lbuf.at[slot, 1 - core], lsem.at[slot, 1]),
+            pltpu.make_async_copy(left.at[where], lbuf.at[slot, core], lsem.at[slot, 0]),
+            pltpu.make_async_copy(left_other.at[where], lbuf.at[slot, 1 - core], lsem.at[slot, 1]),
         )
 
     def right_copies(step, slot):
@@ -51,18 +51,8 @@
         ]
 
     def fetch(step, slot):
-        for copy in right_copies(step, slot):
+        for copy in (*left_copies(step, slot), *right_copies(step, slot)):
             copy.start()
-
-        @pl.when(chunk(step)[1] == zh)
-        def _():
-            for copy in left_copies(step, slot, True):
-                copy.start()
-
-        @pl.when(chunk(step)[1] != zh)
-        def _():
-            for copy in left_copies(step, slot, False):
-                copy.start()
 
     psi_copies = [
         pltpu.make_async_copy(psi, grid.at[pl.ds(1, ROWS), pl.ds(1, COLS)], psem.at[0]),
@@ -86,11 +76,12 @@
 
     @pl.when(n == 0)
     def _():
+        hout[...] = jnp.zeros_like(hout) if first else hin[...]
         for copy in psi_copies:
             copy.wait()
 
     slot = lax.rem(n, 2)
-    for copy in left_copies(0, slot, True):
+    for copy in left_copies(0, slot):
         copy.wait()
     for copy in right_copies(0, slot):
         copy.wait()
@@ -120,16 +111,10 @@
             inner[c], joined, (((1,), (1,)), ((), ())), preferred_element_type=jnp.float32
         ).reshape(ROWS, B, B)
 
-        @pl.when(n == 0)
-        def _():
-            hout[:, c] = part if first else hin[:, c] + part
-
-        @pl.when(n != 0)
-        def _():
-            hout[:, c] += part
-
-
-def add_terms(offsets, place, ls, rs, act, lefts, psis, rights, total):
+        hout[:, c] += part
+
+
+def add_terms(offsets, whole_ring, lefts, place, ls, rs, act, psis, rights, total):
     steps = len(rights)
     layout = tuple(len(pieces) for pieces in rights)
     first = total is None
@@ -141,7 +126,7 @@
         operands.append(total)
         in_specs.append(whole)
     return pl.pallas_call(
-        functools.partial(terms_kernel, layout, offsets, first),
+        functools.partial(terms_kernel, layout, offsets, whole_ring, first),
         out_shape=jax.ShapeDtypeStruct((ROWS, COLS, B, B), jnp.float32),
         grid_spec=pltpu.PrefetchScalarGridSpec(
             num_scalar_prefetch=4,
@@ -162,11 +147,7 @@
         compiler_params=pltpu.CompilerParams(
             vmem_limit_bytes=56 << 20, dimension_semantics=("arbitrary",)
         ),
-        cost_estimate=pl.CostEstimate(
-            flops=steps * 2 * 2 * ROWS * COLS * TERMS * B**3,
-            bytes_accessed=(steps * 2 + 11) << 20,
-            transcendentals=0,
-        ),
+        cost_estimate=pl.CostEstimate(flops=1, bytes_accessed=1, transcendentals=0),
     )(place, ls, rs, act, *operands)
 
 
@@ -195,53 +176,60 @@
 
 def per_device(left_env, right_env, psi, left_shift, right_shift, active):
     place = lax.axis_index((*GRP, *WIDE)).astype(jnp.int32)[None]
-
-    left_y = lax.all_gather(left_env, "y", axis=0)
-    right_m = ring(right_env, "x", 1)
-    right_p = ring(right_env, "x", -1)
+    matched = lax.axis_index("zl") == lax.axis_index("zh")
+
+    low, high = right_env[:4], right_env[4:]
+    low_m = ring(low, "x", 1)
+    high_p = ring(high, "x", -1)
     left_z = swap(left_env, "zh")
     north, south = edges(psi, GRP, 0)
 
-    right_m, right_p, left_z, north, south, own = after(
-        (right_m, right_p, left_z, north, south, right_env), ()
-    )
+    left_z, north, south, low_m, high_p, low, high, own = after(
+        (left_z, north, south, low_m, high_p, low, high, right_env), ()
+    )
+    near = jnp.where(matched, left_env, left_z)
+    other = jnp.where(matched, left_z, left_env)
+    other_y = lax.all_gather(other, "y", axis=0)
     right_z = swap(own, "zl")
-    far_0 = ring(right_m[:4], "x", 1)
-    far_1 = ring(right_p[4:], "x", -1)
-    left_zm = ring(left_z, "y", 1)
-    left_zp = ring(left_z, "y", -1)
-    left_z2 = ring(left_z, "y", 2)
+    near_m = ring(near, "y", 1)
+    near_p = ring(near, "y", -1)
+    high_m = ring(high, "x", 1)
+    low_p = ring(low, "x", -1)
+
+    far_0 = ring(low_m, "x", 1)
+    far_1 = ring(high_p, "x", -1)
+    near_2 = ring(near, "y", 2)
     sides = jnp.concatenate([north[:, ::7], psi[:, ::7], south[:, ::7]], axis=0)
     west = lax.ppermute(sides[:, 1:], WIDE, [(i, i + 1) for i in range(15)])
     east = lax.ppermute(sides[:, :1], WIDE, [(i + 1, i) for i in range(15)])
 
-    right_z, far_0, far_1 = after((right_z, far_0, far_1), ())
+    right_z, far_0, far_1, high_m, low_p, near_2, west, east = after(
+        (right_z, far_0, far_1, high_m, low_p, near_2, west, east), ()
+    )
     right_zm = ring(right_z, "x", 1)
     right_zp = ring(right_z, "x", -1)
     far_z0 = swap(far_0, "zl")
     far_z1 = swap(far_1, "zl")
-    left_yc = swap(left_y, "core")
-    left_zs = jnp.stack([left_z, left_zp, left_z2, left_zm])
-    left_zc = swap(left_zs, "core")
-
-    shared = (
-        place,
-        left_shift,
-        right_shift,
-        active,
-        (left_y, left_yc, left_zs, left_zc),
-        (psi, north, south, west, east),
-    )
+    near_y = jnp.stack([near, near_p, near_2, near_m])
+    near_yc = swap(near_y, "core")
+
+    shared = (place, left_shift, right_shift, active, (psi, north, south, west, east))
+    nears = (near_y, near_yc)
+    other_yc = swap(other_y, "core")
     total = add_terms(
-        ((0, 0), (0, 1), (3, 0), (1, 0), (2, 0)),
+        ((0, 0), (3, 0), (1, 0), (2, 0)),
+        False,
+        nears,
         *shared,
-        [(right_env,), (right_z,), (right_m,), (right_p,), (far_0, far_1)],
+        [(right_env,), (low_m, high_m), (low_p, high_p), (far_0, far_1)],
         None,
     )
     return add_terms(
-        ((3, 1), (1, 1), (2, 1)),
+        ((0, 1), (3, 1), (1, 1), (2, 1)),
+        True,
+        (other_y, other_yc),
         *shared,
-        [(right_zm,), (right_zp,), (far_z0, far_z1)],
+        [(right_z,), (right_zm,), (right_zp,), (far_z0, far_z1)],
         total,
     )
 

time: 193 us -> 163 us (0.84); the launches traced: 190 us -> 163 us
  Pallas kernels: 79.6 us -> 51.7 us
  starting transfers between devices: 38.9 us -> 36.7 us
  other arithmetic: 0.35 us -> 2.41 us
    pallas_call x2, Pallas kernels: 79.6 us -> 51.7 us  [add_terms(): pl.pallas_call(functools.partial(terms_kernel, layout, offsets, whole_rin...]
    ppermute x9 -> x11, waiting for transfers between devices: 37.4 us -> 12.5 us  [ring(): return lax.ppermute(value, axis, [(i, (i + shift) % 4) for i in range(4)])]
    ppermute x1, waiting for transfers between devices: 0.04 us -> 22 us  [per_device(): east = lax.ppermute(sides[:, :1], WIDE, [(i + 1, i) for i in range(15)])]
    ppermute x2, waiting for transfers between devices: 11.3 us -> 16.8 us  [edges(): return (lax.ppermute(last, axes, up), lax.ppermute(leading, axes, down))]
    ppermute x1, starting transfers between devices: 6.63 us -> 4.09 us  [per_device(): west = lax.ppermute(sides[:, 1:], WIDE, [(i, i + 1) for i in range(15)])]
    select_n x0 -> x1, other arithmetic: none -> 2.06 us  [per_device(): near = jnp.where(matched, left_env, left_z)]
    ppermute x9 -> x11, starting transfers between devices: 15.9 us -> 17.6 us  [ring(): return lax.ppermute(value, axis, [(i, (i + shift) % 4) for i in range(4)])]
  transfers between devices with their start and end apart: 20 -> 22, of which waited for: 8 -> 7; matrix products, arithmetic and copies ran while one was open for 2% -> 1% of each run, Pallas kernels for 25% -> 15%
where the time goes in v2:
time: 163 us
  waiting for transfers between devices  53.4 us (33%)
  Pallas kernels  51.7 us (32%)
  starting transfers between devices  36.7 us (23%)
  between operations  13.7 us (8%)
  local copies, waits for them, and re-layouts  4.96 us (3%)
  other arithmetic  2.41 us (1%)
    pallas_call x2, Pallas kernels, add_terms(): pl.pallas_call(functools.partial(terms_kernel, layout, offsets, whole_rin...  51.7 us
    ppermute x1, waiting for transfers between devices, per_device(): east = lax.ppermute(sides[:, :1], WIDE, [(i + 1, i) for i in range(15)])  22 us
    ppermute x11, starting transfers between devices, ring(): return lax.ppermute(value, axis, [(i, (i + shift) % 4) for i in range(4)])  17.6 us
    ppermute x2, waiting for transfers between devices, edges(): return (lax.ppermute(last, axes, up), lax.ppermute(leading, axes, down))  16.8 us
    ppermute x11, waiting for transfers between devices, ring(): return lax.ppermute(value, axis, [(i, (i + shift) % 4) for i in range(4)])  12.5 us
    ppermute x6, starting transfers between devices, swap(): return lax.ppermute(value, axis, [(0, 1), (1, 0)])  7.37 us
    ppermute x1, starting transfers between devices, per_device(): west = lax.ppermute(sides[:, 1:], WIDE, [(i, i + 1) for i in range(15)])  4.09 us
    ppermute x2, starting transfers between devices, edges(): return (lax.ppermute(last, axes, up), lax.ppermute(leading, axes, down))  3.94 us
  transfers between devices with their start and end apart: 22, of which 7 were waited for; matrix products, arithmetic and copies ran while one was open for 1% of the time, Pallas kernels for 15%

profile of v2, /device:TPU:1, one launch (start us, length us, event | category | flops | bytes accessed | tf_op | source)
XLA Modules:
  0.0 162.8 jit_solution(7756663169985865772)
XLA Ops:
  6.5 2.4 %fusion.1 = (bf16[4,4,128,128]{3,2,1,0:T(8,128)(2,1)}, bf16[4,4,128,128]{3,2,1,0:T(8,128)(2,1)}) fusion(bf16[8,4,128,128]{3,2,1,0:T(8,128)(2,1)} %refs_7_.1), kind=kLoop, calls=%fused_computation.5 | loop fusion | bytes 2097152 | tf_op jit(solution)/shard_map/slice | solution.py:181
  9.0 2.0 %collective-permute-start.3 = (bf16[4,4,128,128]{3,2,1,0:T(8,128)(2,1)}, bf16[4,4,128,128]{3,2,1,0:T(8,128)(2,1)S(1)}, u32[]{:S(2)}, u32[]{:S(2)}) collective-permute-start(bf16[4,4,128,128]{3,2,1,0:T(8,128)(2,1)} %get-tuple-element.28), channel_id=1, source_target_pairs={{0,32},{32,64},{64,96},{96,0},{1,33},{33,65},{65,97},{97,1},{2,34}... | collective-permute-start | bytes 1572872 | tf_op jit(solution)/shard_map/ppermute | solution.py:155
  11.0 1.3 collective-permute-start.4
  12.3 3.8 %collective-permute-start = (bf16[8,2,128,128]{3,2,1,0:T(8,128)(2,1)}, bf16[8,2,128,128]{3,2,1,0:T(8,128)(2,1)}, u32[]{:S(2)}, u32[]{:S(2)}) collective-permute-start(bf16[8,2,128,128]{3,2,1,0:T(8,128)(2,1)} %param.6), channel_id=1, source_target_pairs={{0,2},{2,0},{1,3},{3,1},{4,6},{6,4},{5,7},{7,5},{8,10},{10,8},{9,1... | collective-permute-start | bytes 1572872 | tf_op jit(solution)/shard_map/ppermute | solution.py:159
  16.1 0.7 fusion
  16.8 2.6 %collective-permute-start.1 = (bf16[1,8,128,128]{3,2,1,0:T(8,128)(2,1)}, bf16[1,8,128,128]{3,2,1,0:T(8,128)(2,1)S(1)}, u32[]{:S(2)}, u32[]{:S(2)}) collective-permute-start(bf16[1,8,128,128]{3,2,1,0:T(8,128)(2,1)} %get-tuple-element.38), channel_id=1, source_target_pairs={{0,16},{16,32},{32,48},{48,64},{64,80},{80,96},{96,112},{1,17},{17... | collective-permute-start | bytes 786440 | tf_op jit(solution)/shard_map/ppermute | solution.py:169
  19.5 1.3 collective-permute-start.2
  20.8 16.8 %collective-permute-done.1.refs_3_ = bf16[1,8,128,128]{3,2,1,0:T(8,128)(2,1)S(1)} collective-permute-done((bf16[1,8,128,128]{3,2,1,0:T(8,128)(2,1)}, bf16[1,8,128,128]{3,2,1,0:T(8,128)(2,1)S(1)}, u32[]{:S(2)}, u32[]{:S(2)}) %collective-permute-start.1) | collective-permute-done | bytes 262176 | tf_op jit(solution)/shard_map/ppermute | solution.py:169
  37.6 0.9 copy-done.8
  38.5 2.1 %broadcast_select_fusion = (bf16[8,2,128,128]{3,2,1,0:T(8,128)(2,1)S(1)}, bf16[8,2,128,128]{3,2,1,0:T(8,128)(2,1)}) fusion(bf16[8,2,128,128]{3,2,1,0:T(8,128)(2,1)} %param.6, bf16[8,2,128,128]{3,2,1,0:T(8,128)(2,1)} %collective-permute-done, pred[]{:T(512)S(6)} %eq.3), kind=kLoop, calls=%fused_computation.2 | loop fusion | flops 524288 | bytes 2097153 | tf_op jit(solution)/shard_map/jit(_where)/select_n | solution.py:190
  40.9 4.1 %collective-permute-start.12 = (bf16[10,1,128,128]{3,2,1,0:T(8,128)(2,1)S(1)}, bf16[10,1,128,128]{3,2,1,0:T(8,128)(2,1)S(1)}, u32[]{:S(2)}, u32[]{:S(2)}) collective-permute-start(bf16[10,1,128,128]{3,2,1,0:T(8,128)(2,1)S(1)} %get-tuple-element.44), channel_id=1, source_target_pairs={{0,1},{1,2},{2,3},{3,4},{4,5},{5,6},{6,7},{7,8},{8,9},{9,10},{10,1... | collective-permute-start | bytes 983048 | tf_op jit(solution)/shard_map/ppermute | solution.py:203
  45.0 3.0 %collective-permute-start.11 = (bf16[8,2,128,128]{3,2,1,0:T(8,128)(2,1)S(1)}, bf16[8,2,128,128]{3,2,1,0:T(8,128)(2,1)S(1)}, u32[]{:S(2)}, u32[]{:S(2)}) collective-permute-start(bf16[8,2,128,128]{3,2,1,0:T(8,128)(2,1)S(1)} %get-tuple-element.39), channel_id=1, source_target_pairs={{0,8},{4,12},{8,0},{12,4},{1,9},{5,13},{9,1},{13,5},{2,10},{6,14},... | collective-permute-start | bytes 1572872 | tf_op jit(solution)/shard_map/ppermute | solution.py:155
  48.0 1.5 collective-permute-start.6
  49.4 0.8 collective-permute-start.7
  50.3 1.9 %collective-permute-start.8 = (bf16[4,4,128,128]{3,2,1,0:T(8,128)(2,1)}, bf16[4,4,128,128]{3,2,1,0:T(8,128)(2,1)S(1)}, u32[]{:S(2)}, u32[]{:S(2)}) collective-permute-start(bf16[4,4,128,128]{3,2,1,0:T(8,128)(2,1)} %collective-permute-done.4.refs_11_), channel_id=1, source_target_pairs={{0,96},{32,0},{64,32},{96,64},{1,97},{33,1},{65,33},{97,65},{2,98}... | collective-permute-start | bytes 1572872 | tf_op jit(solution)/shard_map/ppermute | solution.py:155
  52.1 3.7 %collective-permute-start.13 = (bf16[10,1,128,128]{3,2,1,0:T(8,128)(2,1)S(1)}, bf16[10,1,128,128]{3,2,1,0:T(8,128)(2,1)S(1)}, u32[]{:S(2)}, u32[]{:S(2)}) collective-permute-start(bf16[10,1,128,128]{3,2,1,0:T(8,128)(2,1)S(1)} %get-tuple-element.43), channel_id=1, source_target_pairs={{1,0},{2,1},{3,2},{4,3},{5,4},{6,5},{7,6},{8,7},{9,8},{10,9},{11,1... | collective-permute-start | bytes 983048 | tf_op jit(solution)/shard_map/ppermute | solution.py:204
  55.9 22.0 %collective-permute-done.13.refs_6_ = bf16[10,1,128,128]{3,2,1,0:T(8,128)(2,1)S(1)} collective-permute-done((bf16[10,1,128,128]{3,2,1,0:T(8,128)(2,1)S(1)}, bf16[10,1,128,128]{3,2,1,0:T(8,128)(2,1)S(1)}, u32[]{:S(2)}, u32[]{:S(2)}) %collective-permute-start.13) | collective-permute-done | bytes 327712 | tf_op jit(solution)/shard_map/ppermute | solution.py:204
  77.8 1.2 collective-permute-start.10
  79.3 4.2 %collective-permute-start.18 = (bf16[8,2,128,128]{3,2,1,0:T(8,128)(2,1)S(1)}, bf16[8,2,128,128]{3,2,1,0:T(8,128)(2,1)S(1)}, u32[]{:S(2)}, u32[]{:S(2)}) collective-permute-start(bf16[8,2,128,128]{3,2,1,0:T(8,128)(2,1)S(1)} %get-tuple-element.39), channel_id=1, source_target_pairs={{0,12},{4,0},{8,4},{12,8},{1,13},{5,1},{9,5},{13,9},{2,14},{6,2},{... | collective-permute-start | bytes 1572872 | tf_op jit(solution)/shard_map/ppermute | solution.py:155
  83.6 2.8 %collective-permute-done.10.refs_10_ = bf16[4,4,128,128]{3,2,1,0:T(8,128)(2,1)S(1)} collective-permute-done((bf16[4,4,128,128]{3,2,1,0:T(8,128)(2,1)}, bf16[4,4,128,128]{3,2,1,0:T(8,128)(2,1)S(1)}, u32[]{:S(2)}, u32[]{:S(2)}) %collective-permute-start.10) | collective-permute-done | bytes 524320 | tf_op jit(solution)/shard_map/ppermute | solution.py:155
  86.4 2.4 %collective-permute-done.9.refs_9_ = bf16[4,4,128,128]{3,2,1,0:T(8,128)(2,1)S(1)} collective-permute-done((bf16[4,4,128,128]{3,2,1,0:T(8,128)(2,1)}, bf16[4,4,128,128]{3,2,1,0:T(8,128)(2,1)S(1)}, u32[]{:S(2)}, u32[]{:S(2)}) %collective-permute-start.9) | collective-permute-done | bytes 524320 | tf_op jit(solution)/shard_map/ppermute | solution.py:155
  88.8 4.9 %collective-permute-done.18 = bf16[8,2,128,128]{3,2,1,0:T(8,128)(2,1)S(1)} collective-permute-done((bf16[8,2,128,128]{3,2,1,0:T(8,128)(2,1)S(1)}, bf16[8,2,128,128]{3,2,1,0:T(8,128)(2,1)S(1)}, u32[]{:S(2)}, u32[]{:S(2)}) %collective-permute-start.18) | collective-permute-done | bytes 524320 | tf_op jit(solution)/shard_map/ppermute | solution.py:155
  93.6 2.4 %collective-permute-done.19 = bf16[8,2,128,128]{3,2,1,0:T(8,128)(2,1)S(1)} collective-permute-done((bf16[8,2,128,128]{3,2,1,0:T(8,128)(2,1)S(1)}, bf16[8,2,128,128]{3,2,1,0:T(8,128)(2,1)S(1)}, u32[]{:S(2)}, u32[]{:S(2)}) %collective-permute-start.19) | collective-permute-done | bytes 524320 | tf_op jit(solution)/shard_map/ppermute | solution.py:155
  96.5 0.5 collective-permute-start.5
  97.0 0.4 collective-permute-start.14
  97.4 2.5 %collective-permute-start.15 = (bf16[8,4,128,128]{3,2,1,0:T(8,128)(2,1)}, bf16[8,4,128,128]{3,2,1,0:T(8,128)(2,1)}, u32[]{:S(2)}, u32[]{:S(2)}) collective-permute-start(bf16[8,4,128,128]{3,2,1,0:T(8,128)(2,1)} %copy-done.7), channel_id=1, source_target_pairs={{0,96},{32,0},{64,32},{96,64},{1,97},{33,1},{65,33},{97,65},{2,98}... | collective-permute-start | bytes 3145736 | tf_op jit(solution)/shard_map/ppermute | solution.py:155
  99.9 0.7 collective-permute-start.16
  100.5 2.0 %collective-permute-done.20.refs_1_ = bf16[4,8,2,128,128]{4,3,2,1,0:T(8,128)(2,1)} collective-permute-done((bf16[4,8,2,128,128]{4,3,2,1,0:T(8,128)(2,1)S(1)}, bf16[4,8,2,128,128]{4,3,2,1,0:T(8,128)(2,1)}, u32[]{:S(2)}, u32[]{:S(2)}) %collective-permute-start.20) | collective-permute-done | bytes 2097184 | tf_op jit(solution)/shard_map/ppermute | solution.py:159
  102.6 0.9 collective-permute-start.17
  103.4 24.8 %shard_map.64.refs_12_ = f32[8,8,128,128]{3,2,1,0:T(8,128)} custom-call(s32[1]{0:T(128)} %bitcast.place, s32[32]{0:T(128)} %ls.3, s32[32]{0:T(128)} %rs.3, s32[8,8,32]{2,1,0:T(8,128)} %act.3, bf16[4,8,2,128,128]{4,3,2,1,0:T(8,128)(2,1)} %copy-done.1, bf16[4,8,2,128,128]{4,3,2,1,0:T(8,128)(2,1)} %collective-permute-done.20.refs_1_, ...), custom_call_target="tpu_custom_call" | custom-call | flops 1 | bytes 1 | tf_op jit(solution)/shard_map/pallas_call | solution.py:128
  128.3 0.8 copy-done.14
  129.0 27.0 %shard_map.65 = f32[8,8,128,128]{3,2,1,0:T(8,128)} custom-call(s32[1]{0:T(128)} %bitcast.place, s32[32]{0:T(128)} %ls.3, s32[32]{0:T(128)} %rs.3, s32[8,8,32]{2,1,0:T(8,128)} %act.3, bf16[4,8,2,128,128]{4,3,2,1,0:T(8,128)(2,1)} %bitcast.7, bf16[4,8,2,128,128]{4,3,2,1,0:T(8,128)(2,1)} %collective-permute-done.5.refs_1_, ...), custom_call_target="tpu_custom_call", output_to_operand_aliasing={{}: (16, {})} | custom-call | flops 1 | bytes 1 | tf_op jit(solution)/shard_map/pallas_call | solution.py:128
  (54 shorter events, 1.0 us)
Async XLA Ops:
  6.5 9.6 %copy-start = (bf16[8,8,128,128]{3,2,1,0:T(8,128)(2,1)S(1)}, bf16[8,8,128,128]{3,2,1,0:T(8,128)(2,1)}, u32[]{:S(2)}) copy-start(bf16[8,8,128,128]{3,2,1,0:T(8,128)(2,1)} %refs_2_.3) | copy-start | bytes 6291460
  6.5 90.0 %all-gather.3.cloned.1.call-start = ((), (), s32[]{:S(2)}) async-start(), calls=%async_computation | async-start | bytes 2621440 | tf_op jit(solution)/shard_map/all_gather | solution.py:192
  9.0 28.6 %collective-permute-start.3 = (bf16[4,4,128,128]{3,2,1,0:T(8,128)(2,1)}, bf16[4,4,128,128]{3,2,1,0:T(8,128)(2,1)S(1)}, u32[]{:S(2)}, u32[]{:S(2)}) collective-permute-start(bf16[4,4,128,128]{3,2,1,0:T(8,128)(2,1)} %get-tuple-element.28), channel_id=1, source_target_pairs={{0,32},{32,64},{64,96},{96,0},{1,33},{33,65},{65,97},{97,1},{2,34}... | collective-permute-start | bytes 1572872 | tf_op jit(solution)/shard_map/ppermute | solution.py:155
  11.0 26.6 %collective-permute-start.4 = (bf16[4,4,128,128]{3,2,1,0:T(8,128)(2,1)}, bf16[4,4,128,128]{3,2,1,0:T(8,128)(2,1)}, u32[]{:S(2)}, u32[]{:S(2)}) collective-permute-start(bf16[4,4,128,128]{3,2,1,0:T(8,128)(2,1)} %get-tuple-element.27), channel_id=1, source_target_pairs={{0,96},{32,0},{64,32},{96,64},{1,97},{33,1},{65,33},{97,65},{2,98}... | collective-permute-start | bytes 1572872 | tf_op jit(solution)/shard_map/ppermute | solution.py:155
  12.3 26.2 %collective-permute-start = (bf16[8,2,128,128]{3,2,1,0:T(8,128)(2,1)}, bf16[8,2,128,128]{3,2,1,0:T(8,128)(2,1)}, u32[]{:S(2)}, u32[]{:S(2)}) collective-permute-start(bf16[8,2,128,128]{3,2,1,0:T(8,128)(2,1)} %param.6), channel_id=1, source_target_pairs={{0,2},{2,0},{1,3},{3,1},{4,6},{6,4},{5,7},{7,5},{8,10},{10,8},{9,1... | collective-permute-start | bytes 1572872 | tf_op jit(solution)/shard_map/ppermute | solution.py:159
  16.8 20.8 %collective-permute-start.1 = (bf16[1,8,128,128]{3,2,1,0:T(8,128)(2,1)}, bf16[1,8,128,128]{3,2,1,0:T(8,128)(2,1)S(1)}, u32[]{:S(2)}, u32[]{:S(2)}) collective-permute-start(bf16[1,8,128,128]{3,2,1,0:T(8,128)(2,1)} %get-tuple-element.38), channel_id=1, source_target_pairs={{0,16},{16,32},{32,48},{48,64},{64,80},{80,96},{96,112},{1,17},{17... | collective-permute-start | bytes 786440 | tf_op jit(solution)/shard_map/ppermute | solution.py:169
  19.5 18.1 %collective-permute-start.2 = (bf16[1,8,128,128]{3,2,1,0:T(8,128)(2,1)S(1)}, bf16[1,8,128,128]{3,2,1,0:T(8,128)(2,1)S(1)}, u32[]{:S(2)}, u32[]{:S(2)}) collective-permute-start(bf16[1,8,128,128]{3,2,1,0:T(8,128)(2,1)S(1)} %get-tuple-element.37), channel_id=1, source_target_pairs={{16,0},{32,16},{48,32},{64,48},{80,64},{96,80},{112,96},{17,1},{33... | collective-permute-start | bytes 786440 | tf_op jit(solution)/shard_map/ppermute | solution.py:169
  40.6 7.4 %copy-start.2 = (bf16[8,4,128,128]{3,2,1,0:T(8,128)(2,1)S(1)}, bf16[8,4,128,128]{3,2,1,0:T(8,128)(2,1)}, u32[]{:S(2)}) copy-start(bf16[8,4,128,128]{3,2,1,0:T(8,128)(2,1)} %refs_7_.1) | copy-start | bytes 3145732
  40.6 8.8 %copy-start.9 = (bf16[4,4,128,128]{3,2,1,0:T(8,128)(2,1)S(1)}, bf16[4,4,128,128]{3,2,1,0:T(8,128)(2,1)}, u32[]{:S(2)}) copy-start(bf16[4,4,128,128]{3,2,1,0:T(8,128)(2,1)} %copy-done.8) | copy-start | bytes 1572868
  40.9 11.3 %collective-permute-start.12 = (bf16[10,1,128,128]{3,2,1,0:T(8,128)(2,1)S(1)}, bf16[10,1,128,128]{3,2,1,0:T(8,128)(2,1)S(1)}, u32[]{:S(2)}, u32[]{:S(2)}) collective-permute-start(bf16[10,1,128,128]{3,2,1,0:T(8,128)(2,1)S(1)} %get-tuple-element.44), channel_id=1, source_target_pairs={{0,1},{1,2},{2,3},{3,4},{4,5},{5,6},{6,7},{7,8},{8,9},{9,10},{10,1... | collective-permute-start | bytes 983048 | tf_op jit(solution)/shard_map/ppermute | solution.py:203
  45.0 34.1 %collective-permute-start.11 = (bf16[8,2,128,128]{3,2,1,0:T(8,128)(2,1)S(1)}, bf16[8,2,128,128]{3,2,1,0:T(8,128)(2,1)S(1)}, u32[]{:S(2)}, u32[]{:S(2)}) collective-permute-start(bf16[8,2,128,128]{3,2,1,0:T(8,128)(2,1)S(1)} %get-tuple-element.39), channel_id=1, source_target_pairs={{0,8},{4,12},{8,0},{12,4},{1,9},{5,13},{9,1},{13,5},{2,10},{6,14},... | collective-permute-start | bytes 1572872 | tf_op jit(solution)/shard_map/ppermute | solution.py:155
  48.0 40.8 %collective-permute-start.6 = (bf16[8,4,128,128]{3,2,1,0:T(8,128)(2,1)S(1)}, bf16[8,4,128,128]{3,2,1,0:T(8,128)(2,1)S(1)}, u32[]{:S(2)}, u32[]{:S(2)}) collective-permute-start(bf16[8,4,128,128]{3,2,1,0:T(8,128)(2,1)S(1)} %copy-done.2), channel_id=1, source_target_pairs={{0,16},{16,0},{1,17},{17,1},{2,18},{18,2},{3,19},{19,3},{4,20},{20... | collective-permute-start | bytes 3145736 | tf_op jit(solution)/shard_map/ppermute | solution.py:159
  49.4 29.9 %collective-permute-start.7 = (bf16[4,4,128,128]{3,2,1,0:T(8,128)(2,1)S(1)}, bf16[4,4,128,128]{3,2,1,0:T(8,128)(2,1)S(1)}, u32[]{:S(2)}, u32[]{:S(2)}) collective-permute-start(bf16[4,4,128,128]{3,2,1,0:T(8,128)(2,1)S(1)} %copy-done.9), channel_id=1, source_target_pairs={{0,32},{32,64},{64,96},{96,0},{1,33},{33,65},{65,97},{97,1},{2,34}... | collective-permute-start | bytes 1572872 | tf_op jit(solution)/shard_map/ppermute | solution.py:155
  50.3 33.3 %collective-permute-start.8 = (bf16[4,4,128,128]{3,2,1,0:T(8,128)(2,1)}, bf16[4,4,128,128]{3,2,1,0:T(8,128)(2,1)S(1)}, u32[]{:S(2)}, u32[]{:S(2)}) collective-permute-start(bf16[4,4,128,128]{3,2,1,0:T(8,128)(2,1)} %collective-permute-done.4.refs_11_), channel_id=1, source_target_pairs={{0,96},{32,0},{64,32},{96,64},{1,97},{33,1},{65,33},{97,65},{2,98}... | collective-permute-start | bytes 1572872 | tf_op jit(solution)/shard_map/ppermute | solution.py:155
  52.1 44.3 %copy-start.5 = (bf16[10,1,128,128]{3,2,1,0:T(8,128)(2,1)}, bf16[10,1,128,128]{3,2,1,0:T(8,128)(2,1)S(1)}, u32[]{:S(2)}) copy-start(bf16[10,1,128,128]{3,2,1,0:T(8,128)(2,1)S(1)} %collective-permute-done.12.refs_5_) | copy-start | bytes 983044
  52.1 25.7 %collective-permute-start.13 = (bf16[10,1,128,128]{3,2,1,0:T(8,128)(2,1)S(1)}, bf16[10,1,128,128]{3,2,1,0:T(8,128)(2,1)S(1)}, u32[]{:S(2)}, u32[]{:S(2)}) collective-permute-start(bf16[10,1,128,128]{3,2,1,0:T(8,128)(2,1)S(1)} %get-tuple-element.43), channel_id=1, source_target_pairs={{1,0},{2,1},{3,2},{4,3},{5,4},{6,5},{7,6},{8,7},{9,8},{10,9},{11,1... | collective-permute-start | bytes 983048 | tf_op jit(solution)/shard_map/ppermute | solution.py:204
  77.8 18.5 %copy-start.6 = (bf16[10,1,128,128]{3,2,1,0:T(8,128)(2,1)}, bf16[10,1,128,128]{3,2,1,0:T(8,128)(2,1)S(1)}, u32[]{:S(2)}) copy-start(bf16[10,1,128,128]{3,2,1,0:T(8,128)(2,1)S(1)} %collective-permute-done.13.refs_6_) | copy-start | bytes 983044
  77.8 8.5 %collective-permute-start.10 = (bf16[4,4,128,128]{3,2,1,0:T(8,128)(2,1)}, bf16[4,4,128,128]{3,2,1,0:T(8,128)(2,1)S(1)}, u32[]{:S(2)}, u32[]{:S(2)}) collective-permute-start(bf16[4,4,128,128]{3,2,1,0:T(8,128)(2,1)} %get-tuple-element.28), channel_id=1, source_target_pairs={{0,96},{32,0},{64,32},{96,64},{1,97},{33,1},{65,33},{97,65},{2,98}... | collective-permute-start | bytes 1572872 | tf_op jit(solution)/shard_map/ppermute | solution.py:155
  79.0 9.7 %collective-permute-start.9 = (bf16[4,4,128,128]{3,2,1,0:T(8,128)(2,1)}, bf16[4,4,128,128]{3,2,1,0:T(8,128)(2,1)S(1)}, u32[]{:S(2)}, u32[]{:S(2)}) collective-permute-start(bf16[4,4,128,128]{3,2,1,0:T(8,128)(2,1)} %get-tuple-element.27), channel_id=1, source_target_pairs={{0,32},{32,64},{64,96},{96,0},{1,33},{33,65},{65,97},{97,1},{2,34}... | collective-permute-start | bytes 1572872 | tf_op jit(solution)/shard_map/ppermute | solution.py:155
  79.3 24.1 %copy-start.10 = (bf16[4,4,128,128]{3,2,1,0:T(8,128)(2,1)}, bf16[4,4,128,128]{3,2,1,0:T(8,128)(2,1)S(1)}, u32[]{:S(2)}) copy-start(bf16[4,4,128,128]{3,2,1,0:T(8,128)(2,1)S(1)} %collective-permute-done.7.refs_12_) | copy-start | bytes 1572868
  79.3 14.3 %collective-permute-start.18 = (bf16[8,2,128,128]{3,2,1,0:T(8,128)(2,1)S(1)}, bf16[8,2,128,128]{3,2,1,0:T(8,128)(2,1)S(1)}, u32[]{:S(2)}, u32[]{:S(2)}) collective-permute-start(bf16[8,2,128,128]{3,2,1,0:T(8,128)(2,1)S(1)} %get-tuple-element.39), channel_id=1, source_target_pairs={{0,12},{4,0},{8,4},{12,8},{1,13},{5,1},{9,5},{13,9},{2,14},{6,2},{... | collective-permute-start | bytes 1572872 | tf_op jit(solution)/shard_map/ppermute | solution.py:155
  83.6 12.5 %copy-start.11 = (bf16[4,4,128,128]{3,2,1,0:T(8,128)(2,1)}, bf16[4,4,128,128]{3,2,1,0:T(8,128)(2,1)S(1)}, u32[]{:S(2)}) copy-start(bf16[4,4,128,128]{3,2,1,0:T(8,128)(2,1)S(1)} %collective-permute-done.8.refs_13_) | copy-start | bytes 1572868
  83.6 12.5 %collective-permute-start.19 = (bf16[8,2,128,128]{3,2,1,0:T(8,128)(2,1)S(1)}, bf16[8,2,128,128]{3,2,1,0:T(8,128)(2,1)S(1)}, u32[]{:S(2)}, u32[]{:S(2)}) collective-permute-start(bf16[8,2,128,128]{3,2,1,0:T(8,128)(2,1)S(1)} %get-tuple-element.39), channel_id=1, source_target_pairs={{0,4},{4,8},{8,12},{12,0},{1,5},{5,9},{9,13},{13,1},{2,6},{6,10},{... | collective-permute-start | bytes 1572872 | tf_op jit(solution)/shard_map/ppermute | solution.py:155
  86.4 9.7 %copy-start.12 = (bf16[4,4,128,128]{3,2,1,0:T(8,128)(2,1)}, bf16[4,4,128,128]{3,2,1,0:T(8,128)(2,1)S(1)}, u32[]{:S(2)}) copy-start(bf16[4,4,128,128]{3,2,1,0:T(8,128)(2,1)S(1)} %collective-permute-done.10.refs_10_) | copy-start | bytes 1572868
  88.8 7.3 %copy-start.13 = (bf16[4,4,128,128]{3,2,1,0:T(8,128)(2,1)}, bf16[4,4,128,128]{3,2,1,0:T(8,128)(2,1)S(1)}, u32[]{:S(2)}) copy-start(bf16[4,4,128,128]{3,2,1,0:T(8,128)(2,1)S(1)} %collective-permute-done.9.refs_9_) | copy-start | bytes 1572868
  88.8 7.3 %copy-start.7 = (bf16[8,4,128,128]{3,2,1,0:T(8,128)(2,1)}, bf16[8,4,128,128]{3,2,1,0:T(8,128)(2,1)S(1)}, u32[]{:S(2)}) copy-start(bf16[8,4,128,128]{3,2,1,0:T(8,128)(2,1)S(1)} %collective-permute-done.6.refs_7_) | copy-start | bytes 3145732
  96.4 6.1 %collective-permute-start.20 = (bf16[4,8,2,128,128]{4,3,2,1,0:T(8,128)(2,1)S(1)}, bf16[4,8,2,128,128]{4,3,2,1,0:T(8,128)(2,1)}, u32[]{:S(2)}, u32[]{:S(2)}) collective-permute-start(bf16[4,8,2,128,128]{4,3,2,1,0:T(8,128)(2,1)S(1)} %pad_maximum_fusion.refs_0_), channel_id=1, source_target_pairs={{0,1},{1,0},{2,3},{3,2},{4,5},{5,4},{6,7},{7,6},{8,9},{9,8},{10,11... | collective-permute-start | bytes 6291464 | tf_op jit(solution)/shard_map/ppermute | solution.py:159
  96.5 31.7 %collective-permute-start.5 = (bf16[4,8,2,128,128]{4,3,2,1,0:T(8,128)(2,1)}, bf16[4,8,2,128,128]{4,3,2,1,0:T(8,128)(2,1)}, u32[]{:S(2)}, u32[]{:S(2)}) collective-permute-start(bf16[4,8,2,128,128]{4,3,2,1,0:T(8,128)(2,1)} %bitcast.6), channel_id=1, source_target_pairs={{0,1},{1,0},{2,3},{3,2},{4,5},{5,4},{6,7},{7,6},{8,9},{9,8},{10,11... | collective-permute-start | bytes 6291464 | tf_op jit(solution)/shard_map/ppermute | solution.py:159
  97.0 31.2 %collective-permute-start.14 = (bf16[8,4,128,128]{3,2,1,0:T(8,128)(2,1)}, bf16[8,4,128,128]{3,2,1,0:T(8,128)(2,1)}, u32[]{:S(2)}, u32[]{:S(2)}) collective-permute-start(bf16[8,4,128,128]{3,2,1,0:T(8,128)(2,1)} %copy-done.7), channel_id=1, source_target_pairs={{0,32},{32,64},{64,96},{96,0},{1,33},{33,65},{65,97},{97,1},{2,34}... | collective-permute-start | bytes 3145736 | tf_op jit(solution)/shard_map/ppermute | solution.py:155
  97.4 30.9 %collective-permute-start.15 = (bf16[8,4,128,128]{3,2,1,0:T(8,128)(2,1)}, bf16[8,4,128,128]{3,2,1,0:T(8,128)(2,1)}, u32[]{:S(2)}, u32[]{:S(2)}) collective-permute-start(bf16[8,4,128,128]{3,2,1,0:T(8,128)(2,1)} %copy-done.7), channel_id=1, source_target_pairs={{0,96},{32,0},{64,32},{96,64},{1,97},{33,1},{65,33},{97,65},{2,98}... | collective-permute-start | bytes 3145736 | tf_op jit(solution)/shard_map/ppermute | solution.py:155
  99.9 28.3 %collective-permute-start.16 = (bf16[4,4,128,128]{3,2,1,0:T(8,128)(2,1)S(1)}, bf16[4,4,128,128]{3,2,1,0:T(8,128)(2,1)S(1)}, u32[]{:S(2)}, u32[]{:S(2)}) collective-permute-start(bf16[4,4,128,128]{3,2,1,0:T(8,128)(2,1)S(1)} %collective-permute-done.7.refs_12_), channel_id=1, source_target_pairs={{0,16},{16,0},{1,17},{17,1},{2,18},{18,2},{3,19},{19,3},{4,20},{20... | collective-permute-start | bytes 1572872 | tf_op jit(solution)/shard_map/ppermute | solution.py:159
  102.6 25.7 %collective-permute-start.17 = (bf16[4,4,128,128]{3,2,1,0:T(8,128)(2,1)}, bf16[4,4,128,128]{3,2,1,0:T(8,128)(2,1)}, u32[]{:S(2)}, u32[]{:S(2)}) collective-permute-start(bf16[4,4,128,128]{3,2,1,0:T(8,128)(2,1)} %copy-done.11), channel_id=1, source_target_pairs={{0,16},{16,0},{1,17},{17,1},{2,18},{18,2},{3,19},{19,3},{4,20},{20... | collective-permute-start | bytes 1572872 | tf_op jit(solution)/shard_map/ppermute | solution.py:159
  (5 other events, 15.1 us)
Sparse Core Ops, SparseCore 0:
  40.7 40.7 all-gather.2

commit v3 on v2

v3 whole, which is shorter than its diff:
```python
import functools

import jax
import jax.numpy as jnp
from jax import lax
from jax.experimental import pallas as pl
from jax.experimental.pallas import tpu as pltpu
from jax.sharding import Mesh, PartitionSpec as P

GRP = ("x", "zl")
WIDE = ("y", "zh", "core")
SIZES = (4, 2, 4, 2, 2)
B = 128
ROWS = 8
COLS = 8
TERMS = 4


def terms_kernel(span, layout, offsets, mode, place, ls, rs, act, *refs):
    start, rows = span
    left, psi, north, south, west, east = refs[:6]
    rights, rest = [], refs[6:]
    for pieces in layout:
        rights.append(rest[:pieces])
        rest = rest[pieces:]
    hin = None
    if mode != "new":
        hin, rest = rest[0], rest[1:]
    hout, lbuf, rbuf, grid, inner, psem, lsem, rsem = rest
    steps = len(layout)
    n = pl.program_id(0)
    here = place[0]
    zl, x = (here >> 4) & 1, here >> 5

    def first_term(step):
        return TERMS * (2 * ((x + offsets[step][0]) & 3) + ((zl + offsets[step][1]) & 1))

    def copies(step, slot):
        pieces = rights[step]
        sources = pieces if len(pieces) == 2 else [pieces[0].at[pl.ds(4 * h, 4)] for h in range(2)]
        return [
            pltpu.make_async_copy(left.at[:, pl.ds(first_term(step), TERMS)], lbuf.at[slot], lsem.at[slot]),
            *(
                pltpu.make_async_copy(sources[h], rbuf.at[slot, pl.ds(4 * h, 4)], rsem.at[slot, h])
                for h in range(2)
            ),
        ]

    low, high = max(start - 1, 0), min(start + rows + 1, ROWS)
    psi_copies = [
        pltpu.make_async_copy(
            psi.at[pl.ds(low, high - low)],
            grid.at[pl.ds(low - start + 1, high - low), pl.ds(1, COLS)],
            psem.at[0],
        ),
        pltpu.make_async_copy(west.at[pl.ds(start, rows + 2)], grid.at[:, pl.ds(0, 1)], psem.at[1]),
        pltpu.make_async_copy(east.at[pl.ds(start, rows + 2)], grid.at[:, pl.ds(COLS + 1, 1)], psem.at[2]),
    ]
    if start == 0:
        psi_copies.append(pltpu.make_async_copy(north, grid.at[pl.ds(0, 1), pl.ds(1, COLS)], psem.at[3]))
    if start + rows == ROWS:
        psi_copies.append(
            pltpu.make_async_copy(south, grid.at[pl.ds(rows + 1, 1), pl.ds(1, COLS)], psem.at[4])
        )

    @pl.when(n == 0)
    def _():
        for copy in (*psi_copies, *copies(0, 0)):
            copy.start()

    for step in range(1, steps):

        @pl.when(n == step - 1)
        def _():
            for copy in copies(step, step % 2):
                copy.start()

    @pl.when(n == 0)
    def _():
        hout[...] = hin[...] if mode == "add" else jnp.zeros_like(hout)
        for copy in psi_copies:
            copy.wait()

    slot = lax.rem(n, 2)
    for copy in copies(0, slot):
        copy.wait()

    base = 0
    for step in range(steps):
        base = jnp.where(n == step, first_term(step), base)

    def one_row(row, carry):
        for w in range(TERMS):
            picked = grid[row + 1 + ls[base + w], pl.ds(1 + rs[base + w], COLS)]
            joined = jnp.concatenate([picked[c] for c in range(COLS)], axis=1)
            part = jnp.dot(lbuf[slot, row, w], joined, preferred_element_type=jnp.float32)
            for c in range(COLS):
                on = act[start + row, c, base + w].astype(jnp.float32)
                inner[c, pl.ds(pl.multiple_of(row * B, B), B), w * B : (w + 1) * B] = (
                    part[:, c * B : (c + 1) * B] * on
                ).astype(jnp.bfloat16)
        return carry

    lax.fori_loop(0, rows, one_row, 0, unroll=True)

    for c in range(COLS):
        joined = jnp.concatenate([rbuf[slot, c, w] for w in range(TERMS)], axis=1)
        part = lax.dot_general(
            inner[c], joined, (((1,), (1,)), ((), ())), preferred_element_type=jnp.float32
        ).reshape(rows, B, B)
        hout[:, c] += part


def add_terms(span, offsets, left, place, ls, rs, act, psis, rights, total, mode):
    start, rows = span
    steps = len(rights)
    layout = tuple(len(pieces) for pieces in rights)
    anywhere = pl.BlockSpec(memory_space=pl.ANY)
    block = pl.BlockSpec(
        (rows, COLS, B, B), lambda n, *_: (start // rows, 0, 0, 0), pipeline_mode=pl.Buffered(1)
    )
    operands = [left, *psis, *(piece for pieces in rights for piece in pieces)]
    in_specs = [anywhere] * len(operands)
    if mode != "new":
        operands.append(total)
        in_specs.append(block if mode == "add" else anywhere)
    return pl.pallas_call(
        functools.partial(terms_kernel, span, layout, offsets, mode),
        out_shape=jax.ShapeDtypeStruct((ROWS, COLS, B, B), jnp.float32),
        grid_spec=pltpu.PrefetchScalarGridSpec(
            num_scalar_prefetch=4,
            grid=(steps,),
            in_specs=in_specs,
            out_specs=block,
            scratch_shapes=[
                pltpu.VMEM((2, rows, TERMS, B, B), jnp.bfloat16),
                pltpu.VMEM((2, COLS, TERMS, B, B), jnp.bfloat16),
                pltpu.VMEM((rows + 2, COLS + 2, B, B), jnp.bfloat16),
                pltpu.VMEM((COLS, rows * B, TERMS * B), jnp.bfloat16),
                pltpu.SemaphoreType.DMA((5,)),
                pltpu.SemaphoreType.DMA((2,)),
                pltpu.SemaphoreType.DMA((2, 2)),
            ],
        ),
        input_output_aliases={} if mode == "new" else {4 + len(operands) - 1: 0},
        compiler_params=pltpu.CompilerParams(
            vmem_limit_bytes=56 << 20, dimension_semantics=("arbitrary",)
        ),
        cost_estimate=pl.CostEstimate(
            flops=steps * 4 * rows * COLS * TERMS * B**3,
            bytes_accessed=steps << 21,
            transcendentals=0,
        ),
    )(place, ls, rs, act, *operands)


def ring(value, axis, shift):
    return lax.ppermute(value, axis, [(i, (i + shift) % 4) for i in range(4)])


def swap(value, axis):
    return lax.ppermute(value, axis, [(0, 1), (1, 0)])


def edges(value, axes, dim):
    count = lax.axis_size(axes)
    length = value.shape[dim]
    up = [(i, i + 1) for i in range(count - 1)]
    down = [(j, i) for i, j in up]
    last = lax.slice_in_dim(value, length - 1, length, axis=dim)
    leading = lax.slice_in_dim(value, 0, 1, axis=dim)
    return lax.ppermute(last, axes, up), lax.ppermute(leading, axes, down)


def after(values, events):
    held = lax.optimization_barrier((tuple(values), tuple(events)))
    return held[0]


def per_device(left_env, right_env, psi, left_shift, right_shift, active):
    place = lax.axis_index((*GRP, *WIDE)).astype(jnp.int32)[None]

    spans = ((0, 4), (4, 2), (6, 2))
    lefts = [
        lax.all_gather(left_env[start : start + rows], WIDE, axis=1, tiled=True) for start, rows in spans
    ]

    right_m = ring(right_env, "x", 1)
    right_p = ring(right_env, "x", -1)
    right_z = swap(right_env, "zl")
    north, south = edges(psi, GRP, 0)

    right_m, right_p, right_z, north, south = after((right_m, right_p, right_z, north, south), ())
    far_0 = ring(right_m[:4], "x", 1)
    far_1 = ring(right_p[4:], "x", -1)
    right_zm = ring(right_z, "x", 1)
    right_zp = ring(right_z, "x", -1)
    sides = jnp.concatenate([north[:, ::7], psi[:, ::7], south[:, ::7]], axis=0)
    west = lax.ppermute(sides[:, 1:], WIDE, [(i, i + 1) for i in range(15)])
    east = lax.ppermute(sides[:, :1], WIDE, [(i + 1, i) for i in range(15)])
    far_z0 = swap(far_0, "zl")
    far_z1 = swap(far_1, "zl")

    shared = (place, left_shift, right_shift, active, (psi, north, south, west, east))
    early = [(right_env,), (right_z,), (right_m,), (right_p,), (far_0, far_1)]
    late = [(right_zm,), (right_zp,), (far_z0, far_z1)]
    early_at = ((0, 0), (0, 1), (3, 0), (1, 0), (2, 0))
    late_at = ((3, 1), (1, 1), (2, 1))
    total = add_terms(spans[0], early_at, lefts[0], *shared, early, None, "new")
    total = add_terms(spans[0], late_at, lefts[0], *shared, late, total, "add")
    for span, left in zip(spans[1:], lefts[1:]):
        total = add_terms(span, early_at + late_at, left, *shared, early + late, total, "rest")
    return total


def solution(mesh):
    fine = Mesh(mesh.devices.reshape(SIZES), (*GRP, *WIDE))
    return jax.shard_map(
        per_device,
        mesh=fine,
        in_specs=(
            P(GRP, WIDE, None, None),
            P(WIDE, GRP, None, None),
            P(GRP, WIDE, None, None),
            P(),
            P(),
            P(GRP, WIDE, None),
        ),
        out_specs=P(GRP, WIDE, None, None),
        check_vma=False,
    )
```

time: 163 us -> 200 us (1.23)
  waiting for transfers between devices: 53.4 us -> 87.6 us
  starting transfers between devices: 36.7 us -> 27.3 us
  Pallas kernels: 51.7 us -> 60.9 us
  local copies, waits for them, and re-layouts: 4.96 us -> 9.52 us
  other arithmetic: 2.41 us -> 0.08 us
    all_gather x1 -> x3, waiting for transfers between devices: 0.02 us -> 37.8 us  [per_device(): lax.all_gather(left_env[start:start + rows], WIDE, axis=1, tiled=True)]
    ppermute x1, waiting for transfers between devices: 22 us -> 0.01 us  [per_device(): east = lax.ppermute(sides[:, :1], WIDE, [(i + 1, i) for i in range(15)])]
    ppermute x2, waiting for transfers between devices: 16.8 us -> 34.8 us  [edges(): return (lax.ppermute(last, axes, up), lax.ppermute(leading, axes, down))]
    ppermute x11 -> x6, starting transfers between devices: 17.6 us -> 7.73 us  [ring(): return lax.ppermute(value, axis, [(i, (i + shift) % 4) for i in range(4)])]
    pallas_call x2 -> x4, Pallas kernels: 51.7 us -> 60.9 us  [add_terms(): pl.pallas_call(functools.partial(terms_kernel, span, layout, offsets, mod...]
    ppermute x1, starting transfers between devices: 4.09 us -> 11 us  [per_device(): west = lax.ppermute(sides[:, 1:], WIDE, [(i, i + 1) for i in range(15)])]
    ppermute x6 -> x3, starting transfers between devices: 7.37 us -> 3.38 us  [swap(): return lax.ppermute(value, axis, [(0, 1), (1, 0)])]
    ppermute x11 -> x6, waiting for transfers between devices: 12.5 us -> 9.05 us  [ring(): return lax.ppermute(value, axis, [(i, (i + shift) % 4) for i in range(4)])]
  transfers between devices with their start and end apart: 22 -> 16, of which waited for: 7 -> 5; matrix products, arithmetic and copies ran while one was open for 1% -> 2% of each run, Pallas kernels for 15% -> 23%
where the time goes in v3:
time: 200 us; the launch traced here: 199 us
  waiting for transfers between devices  87.6 us (44%)
  Pallas kernels  60.9 us (30%)
  starting transfers between devices  27.3 us (14%)
  between operations  13.3 us (7%)
  local copies, waits for them, and re-layouts  9.52 us (5%)
    pallas_call x4, Pallas kernels, add_terms(): pl.pallas_call(functools.partial(terms_kernel, span, layout, offsets, mod...  60.9 us
    all_gather x3, waiting for transfers between devices, per_device(): lax.all_gather(left_env[start:start + rows], WIDE, axis=1, tiled=True)  37.8 us
    ppermute x2, waiting for transfers between devices, edges(): return (lax.ppermute(last, axes, up), lax.ppermute(leading, axes, down))  34.8 us
    ppermute x1, starting transfers between devices, per_device(): west = lax.ppermute(sides[:, 1:], WIDE, [(i, i + 1) for i in range(15)])  11 us
    ppermute x6, waiting for transfers between devices, ring(): return lax.ppermute(value, axis, [(i, (i + shift) % 4) for i in range(4)])  9.05 us
    ppermute x6, starting transfers between devices, ring(): return lax.ppermute(value, axis, [(i, (i + shift) % 4) for i in range(4)])  7.73 us
    ppermute x3, waiting for transfers between devices, swap(): return lax.ppermute(value, axis, [(0, 1), (1, 0)])  5.23 us
  transfers between devices with their start and end apart: 16, of which 5 were waited for; matrix products, arithmetic and copies ran while one was open for 2% of the time, Pallas kernels for 23%

profile of v3, /device:TPU:1, one launch (start us, length us, event | category | flops | bytes accessed | tf_op | source)
XLA Modules:
  0.0 198.7 jit_solution(14174756896971317733)
XLA Ops:
  6.5 1.7 slice.47
  8.3 1.7 fusion.2
  10.0 0.7 all-gather.4.cloned.1.call-update
  10.7 2.1 %collective-permute-start = (bf16[8,4,128,128]{3,2,1,0:T(8,128)(2,1)}, bf16[8,4,128,128]{3,2,1,0:T(8,128)(2,1)S(1)}, u32[]{:S(2)}, u32[]{:S(2)}) collective-permute-start(bf16[8,4,128,128]{3,2,1,0:T(8,128)(2,1)} %refs_6_.5), channel_id=1, source_target_pairs={{0,32},{32,64},{64,96},{96,0},{1,33},{33,65},{65,97},{97,1},{2,34}... | collective-permute-start | bytes 3145736 | tf_op jit(solution)/shard_map/ppermute | solution.py:158
  12.8 1.4 collective-permute-start.1
  14.2 1.8 collective-permute-start.2
  15.9 1.1 fusion
  17.0 1.9 collective-permute-start.3
  19.0 1.3 collective-permute-start.4
  20.3 1.1 slice.40
  21.4 34.8 %collective-permute-done.3.refs_2_ = bf16[1,8,128,128]{3,2,1,0:T(8,128)(2,1)S(1)} collective-permute-done((bf16[1,8,128,128]{3,2,1,0:T(8,128)(2,1)S(1)}, bf16[1,8,128,128]{3,2,1,0:T(8,128)(2,1)S(1)}, u32[]{:S(2)}, u32[]{:S(2)}) %collective-permute-start.3) | collective-permute-done | bytes 262176 | tf_op jit(solution)/shard_map/ppermute | solution.py:172
  56.2 1.0 copy-done.5
  57.3 0.1 copy-done.6
  57.4 0.1 pad_maximum_fusion
  57.4 0.8 fusion.1
  58.2 11.0 %collective-permute-start.5 = (bf16[10,1,128,128]{3,2,1,0:T(8,128)(2,1)S(1)}, bf16[10,1,128,128]{3,2,1,0:T(8,128)(2,1)S(1)}, u32[]{:S(2)}, u32[]{:S(2)}) collective-permute-start(bf16[10,1,128,128]{3,2,1,0:T(8,128)(2,1)S(1)} %get-tuple-element.18), channel_id=1, source_target_pairs={{0,1},{1,2},{2,3},{3,4},{4,5},{5,6},{6,7},{7,8},{8,9},{9,10},{10,1... | collective-permute-start | bytes 983048 | tf_op jit(solution)/shard_map/ppermute | solution.py:199
  69.3 0.1 collective-permute-start.7
  69.4 2.7 %collective-permute-start.8 = (bf16[4,4,128,128]{3,2,1,0:T(8,128)(2,1)S(1)}, bf16[4,4,128,128]{3,2,1,0:T(8,128)(2,1)}, u32[]{:S(2)}, u32[]{:S(2)}) collective-permute-start(bf16[4,4,128,128]{3,2,1,0:T(8,128)(2,1)S(1)} %slice.45), channel_id=1, source_target_pairs={{0,96},{32,0},{64,32},{96,64},{1,97},{33,1},{65,33},{97,65},{2,98}... | collective-permute-start | bytes 1572872 | tf_op jit(solution)/shard_map/ppermute | solution.py:158
  72.1 0.1 collective-permute-start.10
  72.2 1.4 collective-permute-start.9
  73.6 1.9 collective-permute-start.6
  75.5 9.0 %collective-permute-done.7.refs_10_ = bf16[4,4,128,128]{3,2,1,0:T(8,128)(2,1)} collective-permute-done((bf16[4,4,128,128]{3,2,1,0:T(8,128)(2,1)S(1)}, bf16[4,4,128,128]{3,2,1,0:T(8,128)(2,1)}, u32[]{:S(2)}, u32[]{:S(2)}) %collective-permute-start.7) | collective-permute-done | bytes 524320 | tf_op jit(solution)/shard_map/ppermute | solution.py:158
  84.5 1.6 collective-permute-start.11
  86.2 17.1 %shard_map.64.refs_10_ = f32[8,8,128,128]{3,2,1,0:T(8,128)} custom-call(s32[1]{0:T(128)} %bitcast.place, s32[32]{0:T(128)} %ls.7, s32[32]{0:T(128)} %rs.7, s32[8,8,32]{2,1,0:T(8,128)} %act.7, bf16[4,32,128,128]{3,2,1,0:T(8,128)(2,1)} %all-gather.8.cloned.1.call-done.refs_0_, bf16[8,8,128,128]{3,2,1,0:T(8,128)(2,1)} %refs_1_.7, ...), custom_call_target="tpu_custom_call" | custom-call | flops 5368709120 | bytes 10485760 | tf_op jit(solution)/shard_map/pallas_call | solution.py:127
  103.3 5.2 %collective-permute-done.12.refs_9_.refs_15_ = bf16[4,4,128,128]{3,2,1,0:T(8,128)(2,1)} collective-permute-done((bf16[4,4,128,128]{3,2,1,0:T(8,128)(2,1)}, bf16[4,4,128,128]{3,2,1,0:T(8,128)(2,1)}, u32[]{:S(2)}, u32[]{:S(2)}) %collective-permute-start.12) | collective-permute-done | bytes 524320 | tf_op jit(solution)/shard_map/ppermute | solution.py:162
  108.5 1.0 copy-done
  109.5 1.0 copy-done.1
  110.5 13.8 %shard_map.65.refs_16_ = f32[8,8,128,128]{3,2,1,0:T(8,128)} custom-call(s32[1]{0:T(128)} %bitcast.place, s32[32]{0:T(128)} %ls.7, s32[32]{0:T(128)} %rs.7, s32[8,8,32]{2,1,0:T(8,128)} %act.7, bf16[4,32,128,128]{3,2,1,0:T(8,128)(2,1)} %all-gather.8.cloned.1.call-done.refs_0_, bf16[8,8,128,128]{3,2,1,0:T(8,128)(2,1)} %refs_1_.7, ...), custom_call_target="tpu_custom_call", output_to_operand_aliasing={{}: (14, {})} | custom-call | flops 3221225472 | bytes 6291456 | tf_op jit(solution)/shard_map/pallas_call | solution.py:127
  124.3 3.7 %all-gather.6.cloned.1.call-done.refs_0_ = bf16[2,32,128,128]{3,2,1,0:T(8,128)(2,1)} async-done(((bf16[2,2,128,128]{3,2,1,0:T(8,128)(2,1)}), bf16[2,32,128,128]{3,2,1,0:T(8,128)(2,1)}) %all-gather.6.cloned.1.call-update) | async-done | bytes 2097168 | tf_op jit(solution)/shard_map/all_gather | solution.py:185
  128.0 15.0 %shard_map.66.refs_16_ = f32[8,8,128,128]{3,2,1,0:T(8,128)} custom-call(s32[1]{0:T(128)} %bitcast.place, s32[32]{0:T(128)} %ls.7, s32[32]{0:T(128)} %rs.7, s32[8,8,32]{2,1,0:T(8,128)} %act.7, bf16[2,32,128,128]{3,2,1,0:T(8,128)(2,1)} %all-gather.6.cloned.1.call-done.refs_0_, bf16[8,8,128,128]{3,2,1,0:T(8,128)(2,1)} %refs_1_.7, ...), custom_call_target="tpu_custom_call", output_to_operand_aliasing={{}: (20, {})} | custom-call | flops 4294967296 | bytes 16777216 | tf_op jit(solution)/shard_map/pallas_call | solution.py:127
  143.0 34.1 %all-gather.4.cloned.1.call-done.refs_0_ = bf16[2,32,128,128]{3,2,1,0:T(8,128)(2,1)} async-done(((bf16[2,2,128,128]{3,2,1,0:T(8,128)(2,1)}), bf16[2,32,128,128]{3,2,1,0:T(8,128)(2,1)}) %all-gather.4.cloned.1.call-update) | async-done | bytes 2097168 | tf_op jit(solution)/shard_map/all_gather | solution.py:185
  177.1 15.0 %shard_map.67 = f32[8,8,128,128]{3,2,1,0:T(8,128)} custom-call(s32[1]{0:T(128)} %bitcast.place, s32[32]{0:T(128)} %ls.7, s32[32]{0:T(128)} %rs.7, s32[8,8,32]{2,1,0:T(8,128)} %act.7, bf16[2,32,128,128]{3,2,1,0:T(8,128)(2,1)} %all-gather.4.cloned.1.call-done.refs_0_, bf16[8,8,128,128]{3,2,1,0:T(8,128)(2,1)} %refs_1_.7, ...), custom_call_target="tpu_custom_call", output_to_operand_aliasing={{}: (20, {})} | custom-call | flops 4294967296 | bytes 16777216 | tf_op jit(solution)/shard_map/pallas_call | solution.py:127
  (31 shorter events, 0.3 us)
Async XLA Ops:
  6.5 79.6 %all-gather.8.cloned.1.call-start = ((), (), s32[]{:S(2)}) async-start(), calls=%async_computation.2 | async-start | bytes 4456448 | tf_op jit(solution)/shard_map/all_gather | solution.py:185
  8.2 119.8 %all-gather.6.cloned.1.call-start = ((), (), s32[]{:S(2)}) async-start(), calls=%async_computation.1 | async-start | bytes 2228224 | tf_op jit(solution)/shard_map/all_gather | solution.py:185
  10.0 167.1 %all-gather.4.cloned.1.call-start = ((), (), s32[]{:S(2)}) async-start(), calls=%async_computation | async-start | bytes 2228224 | tf_op jit(solution)/shard_map/all_gather | solution.py:185
  10.7 45.4 %collective-permute-start = (bf16[8,4,128,128]{3,2,1,0:T(8,128)(2,1)}, bf16[8,4,128,128]{3,2,1,0:T(8,128)(2,1)S(1)}, u32[]{:S(2)}, u32[]{:S(2)}) collective-permute-start(bf16[8,4,128,128]{3,2,1,0:T(8,128)(2,1)} %refs_6_.5), channel_id=1, source_target_pairs={{0,32},{32,64},{64,96},{96,0},{1,33},{33,65},{65,97},{97,1},{2,34}... | collective-permute-start | bytes 3145736 | tf_op jit(solution)/shard_map/ppermute | solution.py:158
  12.8 43.3 %collective-permute-start.1 = (bf16[8,4,128,128]{3,2,1,0:T(8,128)(2,1)}, bf16[8,4,128,128]{3,2,1,0:T(8,128)(2,1)S(1)}, u32[]{:S(2)}, u32[]{:S(2)}) collective-permute-start(bf16[8,4,128,128]{3,2,1,0:T(8,128)(2,1)} %refs_6_.5), channel_id=1, source_target_pairs={{0,96},{32,0},{64,32},{96,64},{1,97},{33,1},{65,33},{97,65},{2,98}... | collective-permute-start | bytes 3145736 | tf_op jit(solution)/shard_map/ppermute | solution.py:158
  14.2 42.0 %collective-permute-start.2 = (bf16[8,4,128,128]{3,2,1,0:T(8,128)(2,1)}, bf16[8,4,128,128]{3,2,1,0:T(8,128)(2,1)}, u32[]{:S(2)}, u32[]{:S(2)}) collective-permute-start(bf16[8,4,128,128]{3,2,1,0:T(8,128)(2,1)} %refs_6_.5), channel_id=1, source_target_pairs={{0,16},{16,0},{1,17},{17,1},{2,18},{18,2},{3,19},{19,3},{4,20},{20... | collective-permute-start | bytes 3145736 | tf_op jit(solution)/shard_map/ppermute | solution.py:162
  17.0 39.1 %collective-permute-start.3 = (bf16[1,8,128,128]{3,2,1,0:T(8,128)(2,1)S(1)}, bf16[1,8,128,128]{3,2,1,0:T(8,128)(2,1)S(1)}, u32[]{:S(2)}, u32[]{:S(2)}) collective-permute-start(bf16[1,8,128,128]{3,2,1,0:T(8,128)(2,1)S(1)} %get-tuple-element.16), channel_id=1, source_target_pairs={{0,16},{16,32},{32,48},{48,64},{64,80},{80,96},{96,112},{1,17},{17... | collective-permute-start | bytes 786440 | tf_op jit(solution)/shard_map/ppermute | solution.py:172
  19.0 37.2 %collective-permute-start.4 = (bf16[1,8,128,128]{3,2,1,0:T(8,128)(2,1)S(1)}, bf16[1,8,128,128]{3,2,1,0:T(8,128)(2,1)S(1)}, u32[]{:S(2)}, u32[]{:S(2)}) collective-permute-start(bf16[1,8,128,128]{3,2,1,0:T(8,128)(2,1)S(1)} %get-tuple-element.15), channel_id=1, source_target_pairs={{16,0},{32,16},{48,32},{64,48},{80,64},{96,80},{112,96},{17,1},{33... | collective-permute-start | bytes 786440 | tf_op jit(solution)/shard_map/ppermute | solution.py:172
  56.2 1.1 copy-start.5
  56.2 1.2 copy-start.6
  56.2 30.0 %copy-start.2 = (bf16[8,4,128,128]{3,2,1,0:T(8,128)(2,1)}, bf16[8,4,128,128]{3,2,1,0:T(8,128)(2,1)S(1)}, u32[]{:S(2)}) copy-start(bf16[8,4,128,128]{3,2,1,0:T(8,128)(2,1)S(1)} %collective-permute-done.refs_8_) | copy-start | bytes 3145732
  56.2 15.9 %copy-start.3 = (bf16[8,4,128,128]{3,2,1,0:T(8,128)(2,1)}, bf16[8,4,128,128]{3,2,1,0:T(8,128)(2,1)S(1)}, u32[]{:S(2)}) copy-start(bf16[8,4,128,128]{3,2,1,0:T(8,128)(2,1)S(1)} %collective-permute-done.1.refs_9_) | copy-start | bytes 3145732
  58.2 15.3 %collective-permute-start.5 = (bf16[10,1,128,128]{3,2,1,0:T(8,128)(2,1)S(1)}, bf16[10,1,128,128]{3,2,1,0:T(8,128)(2,1)S(1)}, u32[]{:S(2)}, u32[]{:S(2)}) collective-permute-start(bf16[10,1,128,128]{3,2,1,0:T(8,128)(2,1)S(1)} %get-tuple-element.18), channel_id=1, source_target_pairs={{0,1},{1,2},{2,3},{3,4},{4,5},{5,6},{6,7},{7,8},{8,9},{9,10},{10,1... | collective-permute-start | bytes 983048 | tf_op jit(solution)/shard_map/ppermute | solution.py:199
  69.3 15.3 %collective-permute-start.7 = (bf16[4,4,128,128]{3,2,1,0:T(8,128)(2,1)S(1)}, bf16[4,4,128,128]{3,2,1,0:T(8,128)(2,1)}, u32[]{:S(2)}, u32[]{:S(2)}) collective-permute-start(bf16[4,4,128,128]{3,2,1,0:T(8,128)(2,1)S(1)} %slice.44), channel_id=1, source_target_pairs={{0,32},{32,64},{64,96},{96,0},{1,33},{33,65},{65,97},{97,1},{2,34}... | collective-permute-start | bytes 1572872 | tf_op jit(solution)/shard_map/ppermute | solution.py:158
  69.4 16.8 %collective-permute-start.8 = (bf16[4,4,128,128]{3,2,1,0:T(8,128)(2,1)S(1)}, bf16[4,4,128,128]{3,2,1,0:T(8,128)(2,1)}, u32[]{:S(2)}, u32[]{:S(2)}) collective-permute-start(bf16[4,4,128,128]{3,2,1,0:T(8,128)(2,1)S(1)} %slice.45), channel_id=1, source_target_pairs={{0,96},{32,0},{64,32},{96,64},{1,97},{33,1},{65,33},{97,65},{2,98}... | collective-permute-start | bytes 1572872 | tf_op jit(solution)/shard_map/ppermute | solution.py:158
  72.1 36.4 %collective-permute-start.10 = (bf16[8,4,128,128]{3,2,1,0:T(8,128)(2,1)}, bf16[8,4,128,128]{3,2,1,0:T(8,128)(2,1)S(1)}, u32[]{:S(2)}, u32[]{:S(2)}) collective-permute-start(bf16[8,4,128,128]{3,2,1,0:T(8,128)(2,1)} %collective-permute-done.2.refs_7_), channel_id=1, source_target_pairs={{0,96},{32,0},{64,32},{96,64},{1,97},{33,1},{65,33},{97,65},{2,98}... | collective-permute-start | bytes 3145736 | tf_op jit(solution)/shard_map/ppermute | solution.py:158
  72.2 36.3 %collective-permute-start.9 = (bf16[8,4,128,128]{3,2,1,0:T(8,128)(2,1)}, bf16[8,4,128,128]{3,2,1,0:T(8,128)(2,1)S(1)}, u32[]{:S(2)}, u32[]{:S(2)}) collective-permute-start(bf16[8,4,128,128]{3,2,1,0:T(8,128)(2,1)} %collective-permute-done.2.refs_7_), channel_id=1, source_target_pairs={{0,32},{32,64},{64,96},{96,0},{1,33},{33,65},{65,97},{97,1},{2,34}... | collective-permute-start | bytes 3145736 | tf_op jit(solution)/shard_map/ppermute | solution.py:158
  73.6 12.6 %copy-start.4 = (bf16[10,1,128,128]{3,2,1,0:T(8,128)(2,1)}, bf16[10,1,128,128]{3,2,1,0:T(8,128)(2,1)S(1)}, u32[]{:S(2)}) copy-start(bf16[10,1,128,128]{3,2,1,0:T(8,128)(2,1)S(1)} %collective-permute-done.5.refs_4_) | copy-start | bytes 983044
  73.6 12.6 %collective-permute-start.6 = (bf16[10,1,128,128]{3,2,1,0:T(8,128)(2,1)}, bf16[10,1,128,128]{3,2,1,0:T(8,128)(2,1)}, u32[]{:S(2)}, u32[]{:S(2)}) collective-permute-start(bf16[10,1,128,128]{3,2,1,0:T(8,128)(2,1)} %get-tuple-element.17), channel_id=1, source_target_pairs={{1,0},{2,1},{3,2},{4,3},{5,4},{6,5},{7,6},{8,7},{9,8},{10,9},{11,1... | collective-permute-start | bytes 983048 | tf_op jit(solution)/shard_map/ppermute | solution.py:200
  84.5 18.7 %collective-permute-start.11 = (bf16[4,4,128,128]{3,2,1,0:T(8,128)(2,1)}, bf16[4,4,128,128]{3,2,1,0:T(8,128)(2,1)}, u32[]{:S(2)}, u32[]{:S(2)}) collective-permute-start(bf16[4,4,128,128]{3,2,1,0:T(8,128)(2,1)} %collective-permute-done.7.refs_10_), channel_id=1, source_target_pairs={{0,16},{16,0},{1,17},{17,1},{2,18},{18,2},{3,19},{19,3},{4,20},{20... | collective-permute-start | bytes 1572872 | tf_op jit(solution)/shard_map/ppermute | solution.py:162
  86.1 22.4 %collective-permute-start.12 = (bf16[4,4,128,128]{3,2,1,0:T(8,128)(2,1)}, bf16[4,4,128,128]{3,2,1,0:T(8,128)(2,1)}, u32[]{:S(2)}, u32[]{:S(2)}) collective-permute-start(bf16[4,4,128,128]{3,2,1,0:T(8,128)(2,1)} %collective-permute-done.8.refs_11_), channel_id=1, source_target_pairs={{0,16},{16,0},{1,17},{17,1},{2,18},{18,2},{3,19},{19,3},{4,20},{20... | collective-permute-start | bytes 1572872 | tf_op jit(solution)/shard_map/ppermute | solution.py:162
  108.5 1.0 copy-start
  109.5 1.0 copy-start.1
Sparse Core Ops, SparseCore 0:
  9.8 68.6 all-gather.7
  81.0 46.9 all-gather.5
  130.5 46.5 all-gather.3

commit v4 on v2

--- a/solution.py
+++ b/solution.py
@@ -16,17 +16,14 @@
 TERMS = 4
 
 
-def terms_kernel(layout, offsets, whole_ring, first, place, ls, rs, act, *refs):
-    left, left_other, psi, up, down, west, east = refs[:7]
-    rights, rest = [], refs[7:]
-    for pieces in layout:
-        rights.append(rest[:pieces])
-        rest = rest[pieces:]
+def terms_kernel(layout, offsets, first, place, ls, rs, act, *refs):
+    lefts, (psi, up, down, west, east) = refs[:4], refs[4:9]
+    steps = len(offsets)
+    rights, rest = [refs[9 + where] for where in layout], refs[9 + max(layout) + 1 :]
     if first:
         hout, lbuf, rbuf, grid, inner, psem, lsem, rsem = rest
     else:
         hin, hout, lbuf, rbuf, grid, inner, psem, lsem, rsem = rest
-    steps = len(layout)
     n = pl.program_id(0)
     here = place[0]
     core, zh, y, zl, x = here & 1, (here >> 1) & 1, (here >> 2) & 3, (here >> 4) & 1, here >> 5
@@ -36,22 +33,21 @@
 
     def left_copies(step, slot):
         p, _ = chunk(step)
-        where = p if whole_ring else (p - y) & 3
+        where = (p - y) & 3
+        mine, theirs = lefts[2 * offsets[step][1] : 2 * offsets[step][1] + 2]
         return (
-            pltpu.make_async_copy(left.at[where], lbuf.at[slot, core], lsem.at[slot, 0]),
-            pltpu.make_async_copy(left_other.at[where], lbuf.at[slot, 1 - core], lsem.at[slot, 1]),
+            pltpu.make_async_copy(mine.at[where], lbuf.at[slot, core], lsem.at[slot, 0]),
+            pltpu.make_async_copy(theirs.at[where], lbuf.at[slot, 1 - core], lsem.at[slot, 1]),
         )
 
-    def right_copies(step, slot):
-        pieces = rights[step]
-        sources = pieces if len(pieces) == 2 else [pieces[0].at[pl.ds(4 * h, 4)] for h in range(2)]
-        return [
-            pltpu.make_async_copy(sources[h], rbuf.at[slot, pl.ds(4 * h, 4)], rsem.at[slot, h])
-            for h in range(2)
-        ]
+    def right_copy(step, slot):
+        source = rights[step]
+        if len(source.shape) == 5:
+            source = source.at[chunk(step)[0]]
+        return pltpu.make_async_copy(source, rbuf.at[slot], rsem.at[slot])
 
     def fetch(step, slot):
-        for copy in (*left_copies(step, slot), *right_copies(step, slot)):
+        for copy in (*left_copies(step, slot), right_copy(step, slot)):
             copy.start()
 
     psi_copies = [
@@ -83,8 +79,7 @@
     slot = lax.rem(n, 2)
     for copy in left_copies(0, slot):
         copy.wait()
-    for copy in right_copies(0, slot):
-        copy.wait()
+    pltpu.make_async_copy(rbuf.at[1 - slot], rbuf.at[slot], rsem.at[slot]).wait()
 
     base = 0
     for step in range(steps):
@@ -114,19 +109,18 @@
         hout[:, c] += part
 
 
-def add_terms(offsets, whole_ring, lefts, place, ls, rs, act, psis, rights, total):
-    steps = len(rights)
-    layout = tuple(len(pieces) for pieces in rights)
+def add_terms(offsets, layout, lefts, place, ls, rs, act, psis, rights, total):
+    steps = len(offsets)
     first = total is None
     anywhere = pl.BlockSpec(memory_space=pl.ANY)
     whole = pl.BlockSpec((ROWS, COLS, B, B), lambda n, *_: (0, 0, 0, 0), pipeline_mode=pl.Buffered(1))
-    operands = [*lefts, *psis, *(piece for pieces in rights for piece in pieces)]
+    operands = [*lefts, *psis, *rights]
     in_specs = [anywhere] * len(operands)
     if not first:
         operands.append(total)
         in_specs.append(whole)
     return pl.pallas_call(
-        functools.partial(terms_kernel, layout, offsets, whole_ring, first),
+        functools.partial(terms_kernel, layout, offsets, first),
         out_shape=jax.ShapeDtypeStruct((ROWS, COLS, B, B), jnp.float32),
         grid_spec=pltpu.PrefetchScalarGridSpec(
             num_scalar_prefetch=4,
@@ -140,7 +134,7 @@
                 pltpu.VMEM((COLS, ROWS * B, TERMS * B), jnp.bfloat16),
                 pltpu.SemaphoreType.DMA((5,)),
                 pltpu.SemaphoreType.DMA((2, 2)),
-                pltpu.SemaphoreType.DMA((2, 2)),
+                pltpu.SemaphoreType.DMA((2,)),
             ],
         ),
         input_output_aliases={} if first else {4 + len(operands) - 1: 0},
@@ -174,63 +168,52 @@
     return held[0]
 
 
+def to_ring(value, axis):
+    count = lax.axis_size(axis)
+    return lax.all_to_all(jnp.broadcast_to(value[None], (count, *value.shape)), axis, 0, 0)
+
+
+def around(value):
+    return ring(value, "y", -1), ring(value, "y", 2), ring(value, "y", 1)
+
+
 def per_device(left_env, right_env, psi, left_shift, right_shift, active):
     place = lax.axis_index((*GRP, *WIDE)).astype(jnp.int32)[None]
     matched = lax.axis_index("zl") == lax.axis_index("zh")
 
-    low, high = right_env[:4], right_env[4:]
-    low_m = ring(low, "x", 1)
-    high_p = ring(high, "x", -1)
+    right_x = to_ring(right_env, "x")
+    right_z = swap(right_env, "zl")
     left_z = swap(left_env, "zh")
     north, south = edges(psi, GRP, 0)
 
-    left_z, north, south, low_m, high_p, low, high, own = after(
-        (left_z, north, south, low_m, high_p, low, high, right_env), ()
-    )
+    left_z, north, south = after((left_z, north, south), ())
     near = jnp.where(matched, left_env, left_z)
     other = jnp.where(matched, left_z, left_env)
-    other_y = lax.all_gather(other, "y", axis=0)
-    right_z = swap(own, "zl")
-    near_m = ring(near, "y", 1)
-    near_p = ring(near, "y", -1)
-    high_m = ring(high, "x", 1)
-    low_p = ring(low, "x", -1)
-
-    far_0 = ring(low_m, "x", 1)
-    far_1 = ring(high_p, "x", -1)
-    near_2 = ring(near, "y", 2)
+    near_ring = around(near)
     sides = jnp.concatenate([north[:, ::7], psi[:, ::7], south[:, ::7]], axis=0)
     west = lax.ppermute(sides[:, 1:], WIDE, [(i, i + 1) for i in range(15)])
     east = lax.ppermute(sides[:, :1], WIDE, [(i + 1, i) for i in range(15)])
 
-    right_z, far_0, far_1, high_m, low_p, near_2, west, east = after(
-        (right_z, far_0, far_1, high_m, low_p, near_2, west, east), ()
-    )
+    near_ring, other, right_z = after((near_ring, other, right_z), ())
+    near_y = jnp.stack([near, *near_ring])
+    near_yc = swap(near_y, "core")
+    other_y = jnp.stack([other, *around(other)])
+    other_yc = swap(other_y, "core")
+
+    lefts = (near_y, near_yc, other_y, other_yc)
+    shared = (place, left_shift, right_shift, active, (psi, north, south, west, east))
+    total = add_terms(((0, 0),), (0,), (near_y, near_yc, near_y, near_yc), *shared, (right_env,), None)
+
+    right_x, right_z = after((right_x, right_z), ())
     right_zm = ring(right_z, "x", 1)
     right_zp = ring(right_z, "x", -1)
-    far_z0 = swap(far_0, "zl")
-    far_z1 = swap(far_1, "zl")
-    near_y = jnp.stack([near, near_p, near_2, near_m])
-    near_yc = swap(near_y, "core")
-
-    shared = (place, left_shift, right_shift, active, (psi, north, south, west, east))
-    nears = (near_y, near_yc)
-    other_yc = swap(other_y, "core")
+    far = lax.dynamic_index_in_dim(right_x, (lax.axis_index("x") + 2) & 3, 0, keepdims=False)
+    far_z = swap(far, "zl")
     total = add_terms(
-        ((0, 0), (3, 0), (1, 0), (2, 0)),
-        False,
-        nears,
-        *shared,
-        [(right_env,), (low_m, high_m), (low_p, high_p), (far_0, far_1)],
-        None,
+        ((3, 0), (1, 0), (2, 0), (0, 1)), (0, 0, 0, 1), lefts, *shared, (right_x, right_z), total
     )
     return add_terms(
-        ((0, 1), (3, 1), (1, 1), (2, 1)),
-        True,
-        (other_y, other_yc),
-        *shared,
-        [(right_z,), (right_zm,), (right_zp,), (far_z0, far_z1)],
-        total,
+        ((3, 1), (1, 1), (2, 1)), (0, 1, 2), lefts, *shared, (right_zm, right_zp, far_z), total
     )
 
 

time: 163 us -> 201 us (1.23)
  starting transfers between devices: 36.7 us -> 77.8 us
  between operations: 13.7 us -> 0.35 us
  Pallas kernels: 51.7 us -> 59.9 us
  local copies, waits for them, and re-layouts: 4.96 us -> 9.71 us
  waiting for transfers between devices: 53.4 us -> 50.7 us
    ppermute x6 -> x5, starting transfers between devices: 7.37 us -> 41.9 us  [swap(): return lax.ppermute(value, axis, [(0, 1), (1, 0)])]
    ppermute x11 -> x8, waiting for transfers between devices: 12.5 us -> 41 us  [ring(): return lax.ppermute(value, axis, [(i, (i + shift) % 4) for i in range(4)])]
    ppermute x1, waiting for transfers between devices: 22 us -> 0.01 us  [per_device(): east = lax.ppermute(sides[:, :1], WIDE, [(i + 1, i) for i in range(15)])]
    pallas_call x2 -> x3, Pallas kernels: 51.7 us -> 59.9 us  [add_terms(): pl.pallas_call(functools.partial(terms_kernel, layout, offsets, first), o...]
    ppermute x2, waiting for transfers between devices: 16.8 us -> 9.69 us  [edges(): return (lax.ppermute(last, axes, up), lax.ppermute(leading, axes, down))]
    all_to_all x0 -> x1, starting transfers between devices: none -> 5.01 us  [to_ring(): lax.all_to_all(jnp.broadcast_to(value[None], (count, *value.shape)), axis...]
    broadcast_in_dim x0 -> x1, local copies, waits for them, and re-layouts: none -> 4.29 us  [to_ring(): jnp.broadcast_to(value[None], (count, *value.shape))]
    slice x1 -> x0, local copies, waits for them, and re-layouts: 2.44 us -> none  [per_device(): low, high = (right_env[:4], right_env[4:])]
  transfers between devices with their start and end apart: 22 -> 18, of which waited for: 7 -> 6; matrix products, arithmetic and copies ran while one was open for 1% -> 4% of each run, Pallas kernels for 15% -> 19%
where the time goes in v4:
time: 201 us; the launch traced here: 200 us
  starting transfers between devices  77.8 us (39%)
  Pallas kernels  59.9 us (30%)
  waiting for transfers between devices  50.7 us (25%)
  local copies, waits for them, and re-layouts  9.71 us (5%)
  other arithmetic  2.07 us (1%)
    pallas_call x3, Pallas kernels, add_terms(): pl.pallas_call(functools.partial(terms_kernel, layout, offsets, first), o...  59.9 us
    ppermute x5, starting transfers between devices, swap(): return lax.ppermute(value, axis, [(0, 1), (1, 0)])  41.9 us
    ppermute x8, waiting for transfers between devices, ring(): return lax.ppermute(value, axis, [(i, (i + shift) % 4) for i in range(4)])  41 us
    ppermute x8, starting transfers between devices, ring(): return lax.ppermute(value, axis, [(i, (i + shift) % 4) for i in range(4)])  18.5 us
    ppermute x2, waiting for transfers between devices, edges(): return (lax.ppermute(last, axes, up), lax.ppermute(leading, axes, down))  9.69 us
    ppermute x2, starting transfers between devices, edges(): return (lax.ppermute(last, axes, up), lax.ppermute(leading, axes, down))  5.29 us
    ppermute x1, starting transfers between devices, per_device(): west = lax.ppermute(sides[:, 1:], WIDE, [(i, i + 1) for i in range(15)])  5.15 us
    all_to_all x1, starting transfers between devices, to_ring(): lax.all_to_all(jnp.broadcast_to(value[None], (count, *value.shape)), axis...  5.01 us
  transfers between devices with their start and end apart: 18, of which 6 were waited for; matrix products, arithmetic and copies ran while one was open for 4% of the time, Pallas kernels for 19%

profile of v4, /device:TPU:1, one launch (start us, length us, event | category | flops | bytes accessed | tf_op | source)
XLA Modules:
  0.0 200.5 jit_solution(9700768003972890283)
XLA Ops:
  0.0 4.3 %broadcast_in_dim.10 = bf16[4,8,4,128,128]{4,3,2,1,0:T(8,128)(2,1)} broadcast(bf16[8,4,128,128]{3,2,1,0:T(8,128)(2,1)} %refs_9_.1), dimensions={1,2,3,4} | broadcast | bytes 5242880 | tf_op jit(solution)/shard_map/broadcast_in_dim | solution.py:173
  4.3 5.0 %all-to-all-start = ((bf16[4,8,4,128,128]{4,3,2,1,0:T(8,128)(2,1)}), bf16[4,8,4,128,128]{4,3,2,1,0:T(8,128)(2,1)}, u32[]{:S(2)}, u32[]{:S(2)}) async-start(bf16[4,8,4,128,128]{4,3,2,1,0:T(8,128)(2,1)} %broadcast_in_dim.10), calls=%async_computation | async-start | bytes 8388608 | tf_op jit(solution)/shard_map/all_to_all | solution.py:173
  9.3 4.5 %collective-permute-start = (bf16[8,2,128,128]{3,2,1,0:T(8,128)(2,1)S(1)}, bf16[8,2,128,128]{3,2,1,0:T(8,128)(2,1)S(1)}, u32[]{:S(2)}, u32[]{:S(2)}) collective-permute-start(bf16[8,2,128,128]{3,2,1,0:T(8,128)(2,1)S(1)} %copy-done.6), channel_id=1, source_target_pairs={{0,2},{2,0},{1,3},{3,1},{4,6},{6,4},{5,7},{7,5},{8,10},{10,8},{9,1... | collective-permute-start | bytes 1572872 | tf_op jit(solution)/shard_map/ppermute | solution.py:153
  13.8 1.1 fusion
  14.9 1.3 collective-permute-start.2
  16.2 4.0 %collective-permute-start.1 = (bf16[1,8,128,128]{3,2,1,0:T(8,128)(2,1)S(1)}, bf16[1,8,128,128]{3,2,1,0:T(8,128)(2,1)S(1)}, u32[]{:S(2)}, u32[]{:S(2)}) collective-permute-start(bf16[1,8,128,128]{3,2,1,0:T(8,128)(2,1)S(1)} %get-tuple-element.26), channel_id=1, source_target_pairs={{0,16},{16,32},{32,48},{48,64},{64,80},{80,96},{96,112},{1,17},{17... | collective-permute-start | bytes 786440 | tf_op jit(solution)/shard_map/ppermute | solution.py:163
  20.2 1.7 collective-permute-start.6
  21.9 9.7 %collective-permute-done.2.refs_6_ = bf16[1,8,128,128]{3,2,1,0:T(8,128)(2,1)S(1)} collective-permute-done((bf16[1,8,128,128]{3,2,1,0:T(8,128)(2,1)S(1)}, bf16[1,8,128,128]{3,2,1,0:T(8,128)(2,1)S(1)}, u32[]{:S(2)}, u32[]{:S(2)}) %collective-permute-start.2) | collective-permute-done | bytes 262176 | tf_op jit(solution)/shard_map/ppermute | solution.py:163
  31.7 1.4 collective-permute-start.5
  33.1 2.6 %collective-permute-start.4 = (bf16[8,2,128,128]{3,2,1,0:T(8,128)(2,1)S(1)}, bf16[8,2,128,128]{3,2,1,0:T(8,128)(2,1)S(1)}, u32[]{:S(2)}, u32[]{:S(2)}) collective-permute-start(bf16[8,2,128,128]{3,2,1,0:T(8,128)(2,1)S(1)} %get-tuple-element.28), channel_id=1, source_target_pairs={{0,8},{4,12},{8,0},{12,4},{1,9},{5,13},{9,1},{13,5},{2,10},{6,14},... | collective-permute-start | bytes 1572872 | tf_op jit(solution)/shard_map/ppermute | solution.py:149
  35.7 1.1 collective-permute-start.3
  36.8 7.3 %collective-permute-done.5 = bf16[8,2,128,128]{3,2,1,0:T(8,128)(2,1)S(1)} collective-permute-done((bf16[8,2,128,128]{3,2,1,0:T(8,128)(2,1)S(1)}, bf16[8,2,128,128]{3,2,1,0:T(8,128)(2,1)S(1)}, u32[]{:S(2)}, u32[]{:S(2)}) %collective-permute-start.5) | collective-permute-done | bytes 524320 | tf_op jit(solution)/shard_map/ppermute | solution.py:149
  44.1 12.4 %collective-permute-done.4 = bf16[8,2,128,128]{3,2,1,0:T(8,128)(2,1)S(1)} collective-permute-done((bf16[8,2,128,128]{3,2,1,0:T(8,128)(2,1)S(1)}, bf16[8,2,128,128]{3,2,1,0:T(8,128)(2,1)S(1)}, u32[]{:S(2)}, u32[]{:S(2)}) %collective-permute-start.4) | collective-permute-done | bytes 524320 | tf_op jit(solution)/shard_map/ppermute | solution.py:149
  56.4 1.4 collective-permute-done.3
  57.8 1.8 collective-permute-start.10
  59.6 2.9 %collective-permute-start.9 = (bf16[8,2,128,128]{3,2,1,0:T(8,128)(2,1)S(1)}, bf16[8,2,128,128]{3,2,1,0:T(8,128)(2,1)S(1)}, u32[]{:S(2)}, u32[]{:S(2)}) collective-permute-start(bf16[8,2,128,128]{3,2,1,0:T(8,128)(2,1)S(1)} %get-tuple-element.19), channel_id=1, source_target_pairs={{0,8},{4,12},{8,0},{12,4},{1,9},{5,13},{9,1},{13,5},{2,10},{6,14},... | collective-permute-start | bytes 1572872 | tf_op jit(solution)/shard_map/ppermute | solution.py:149
  62.8 2.6 %collective-permute-start.7 = (bf16[4,8,2,128,128]{4,3,2,1,0:T(8,128)(2,1)S(1)}, bf16[4,8,2,128,128]{4,3,2,1,0:T(8,128)(2,1)}, u32[]{:S(2)}, u32[]{:S(2)}) collective-permute-start(bf16[4,8,2,128,128]{4,3,2,1,0:T(8,128)(2,1)S(1)} %pad_maximum_fusion.refs_0_.refs_2_), channel_id=1, source_target_pairs={{0,1},{1,0},{2,3},{3,2},{4,5},{5,4},{6,7},{7,6},{8,9},{9,8},{10,11... | collective-permute-start | bytes 6291464 | tf_op jit(solution)/shard_map/ppermute | solution.py:153
  65.4 6.7 %collective-permute-done.10 = bf16[8,2,128,128]{3,2,1,0:T(8,128)(2,1)S(1)} collective-permute-done((bf16[8,2,128,128]{3,2,1,0:T(8,128)(2,1)S(1)}, bf16[8,2,128,128]{3,2,1,0:T(8,128)(2,1)S(1)}, u32[]{:S(2)}, u32[]{:S(2)}) %collective-permute-start.10) | collective-permute-done | bytes 524320 | tf_op jit(solution)/shard_map/ppermute | solution.py:149
  72.1 13.3 %collective-permute-done.9 = bf16[8,2,128,128]{3,2,1,0:T(8,128)(2,1)S(1)} collective-permute-done((bf16[8,2,128,128]{3,2,1,0:T(8,128)(2,1)S(1)}, bf16[8,2,128,128]{3,2,1,0:T(8,128)(2,1)S(1)}, u32[]{:S(2)}, u32[]{:S(2)}) %collective-permute-start.9) | collective-permute-done | bytes 524320 | tf_op jit(solution)/shard_map/ppermute | solution.py:149
  85.4 1.7 pad_maximum_fusion.1.refs_2_
  87.0 1.2 collective-permute-start.11
  88.3 1.1 slice.24
  89.3 0.8 slice.23
  90.3 1.9 collective-permute-start.13
  92.3 5.1 %collective-permute-start.12 = (bf16[10,1,128,128]{3,2,1,0:T(8,128)(2,1)S(1)}, bf16[10,1,128,128]{3,2,1,0:T(8,128)(2,1)S(1)}, u32[]{:S(2)}, u32[]{:S(2)}) collective-permute-start(bf16[10,1,128,128]{3,2,1,0:T(8,128)(2,1)S(1)} %get-tuple-element.30), channel_id=1, source_target_pairs={{0,1},{1,2},{2,3},{3,4},{4,5},{5,6},{6,7},{7,8},{8,9},{9,10},{10,1... | collective-permute-start | bytes 983048 | tf_op jit(solution)/shard_map/ppermute | solution.py:194
  97.4 2.3 %dynamic-slice_bitcast_fusion = bf16[8,4,128,128]{3,2,1,0:T(8,128)(2,1)} fusion(bf16[4,8,4,128,128]{4,3,2,1,0:T(8,128)(2,1)} %all-to-all-done.refs_9_, s32[]{:T(128)S(6)} %select_n.19), kind=kLoop, calls=%fused_computation.2 | loop fusion | bytes 2097156 | tf_op jit(solution)/shard_map/jit(dynamic_index_in_dim)/squeeze | solution.py:210
  99.8 31.9 %collective-permute-start.16 = (bf16[8,4,128,128]{3,2,1,0:T(8,128)(2,1)}, bf16[8,4,128,128]{3,2,1,0:T(8,128)(2,1)}, u32[]{:S(2)}, u32[]{:S(2)}) collective-permute-start(bf16[8,4,128,128]{3,2,1,0:T(8,128)(2,1)} %dynamic-slice_bitcast_fusion), channel_id=1, source_target_pairs={{0,16},{16,0},{1,17},{17,1},{2,18},{18,2},{3,19},{19,3},{4,20},{20... | collective-permute-start | bytes 3145736 | tf_op jit(solution)/shard_map/ppermute | solution.py:153
  131.7 2.4 %collective-permute-start.15 = (bf16[8,4,128,128]{3,2,1,0:T(8,128)(2,1)}, bf16[8,4,128,128]{3,2,1,0:T(8,128)(2,1)}, u32[]{:S(2)}, u32[]{:S(2)}) collective-permute-start(bf16[8,4,128,128]{3,2,1,0:T(8,128)(2,1)} %collective-permute-done.6.refs_10_), channel_id=1, source_target_pairs={{0,96},{32,0},{64,32},{96,64},{1,97},{33,1},{65,33},{97,65},{2,98}... | collective-permute-start | bytes 3145736 | tf_op jit(solution)/shard_map/ppermute | solution.py:149
  134.1 6.3 %collective-permute-start.14 = (bf16[8,4,128,128]{3,2,1,0:T(8,128)(2,1)}, bf16[8,4,128,128]{3,2,1,0:T(8,128)(2,1)}, u32[]{:S(2)}, u32[]{:S(2)}) collective-permute-start(bf16[8,4,128,128]{3,2,1,0:T(8,128)(2,1)} %collective-permute-done.6.refs_10_), channel_id=1, source_target_pairs={{0,32},{32,64},{64,96},{96,0},{1,33},{33,65},{65,97},{97,1},{2,34}... | collective-permute-start | bytes 3145736 | tf_op jit(solution)/shard_map/ppermute | solution.py:149
  140.4 10.4 %shard_map.64.refs_11_ = f32[8,8,128,128]{3,2,1,0:T(8,128)} custom-call(s32[1]{0:T(128)} %bitcast.place, s32[32]{0:T(128)} %ls.5, s32[32]{0:T(128)} %rs.5, s32[8,8,32]{2,1,0:T(8,128)} %act.5, bf16[4,8,2,128,128]{4,3,2,1,0:T(8,128)(2,1)} %copy-done, bf16[4,8,2,128,128]{4,3,2,1,0:T(8,128)(2,1)} %collective-permute-done.7.refs_1_.refs_3_, ...), custom_call_target="tpu_custom_call" | custom-call | flops 1 | bytes 1 | tf_op jit(solution)/shard_map/pallas_call | solution.py:122
  150.8 27.1 %shard_map.65.refs_12_ = f32[8,8,128,128]{3,2,1,0:T(8,128)} custom-call(s32[1]{0:T(128)} %bitcast.place, s32[32]{0:T(128)} %ls.5, s32[32]{0:T(128)} %rs.5, s32[8,8,32]{2,1,0:T(8,128)} %act.5, bf16[4,8,2,128,128]{4,3,2,1,0:T(8,128)(2,1)} %copy-done, ...), custom_call_target="tpu_custom_call", output_to_operand_aliasing={{}: (15, {})} | custom-call | flops 1 | bytes 1 | tf_op jit(solution)/shard_map/pallas_call | solution.py:122
  178.0 22.4 %shard_map.66 = f32[8,8,128,128]{3,2,1,0:T(8,128)} custom-call(s32[1]{0:T(128)} %bitcast.place, s32[32]{0:T(128)} %ls.5, s32[32]{0:T(128)} %rs.5, s32[8,8,32]{2,1,0:T(8,128)} %act.5, bf16[4,8,2,128,128]{4,3,2,1,0:T(8,128)(2,1)} %copy-done, bf16[4,8,2,128,128]{4,3,2,1,0:T(8,128)(2,1)} %collective-permute-done.7.refs_1_.refs_3_, ...), custom_call_target="tpu_custom_call", output_to_operand_aliasing={{}: (16, {})} | custom-call | flops 1 | bytes 1 | tf_op jit(solution)/shard_map/pallas_call | solution.py:122
  (32 shorter events, 0.5 us)
Async XLA Ops:
  4.3 5.0 %copy-start.6 = (bf16[8,2,128,128]{3,2,1,0:T(8,128)(2,1)S(1)}, bf16[8,2,128,128]{3,2,1,0:T(8,128)(2,1)}, u32[]{:S(2)}) copy-start(bf16[8,2,128,128]{3,2,1,0:T(8,128)(2,1)} %param.6) | copy-start | bytes 1572868
  4.3 15.9 %copy-start.1 = (bf16[8,4,128,128]{3,2,1,0:T(8,128)(2,1)S(1)}, bf16[8,4,128,128]{3,2,1,0:T(8,128)(2,1)}, u32[]{:S(2)}) copy-start(bf16[8,4,128,128]{3,2,1,0:T(8,128)(2,1)} %refs_9_.1) | copy-start | bytes 3145732
  4.3 93.1 %all-to-all-start = ((bf16[4,8,4,128,128]{4,3,2,1,0:T(8,128)(2,1)}), bf16[4,8,4,128,128]{4,3,2,1,0:T(8,128)(2,1)}, u32[]{:S(2)}, u32[]{:S(2)}) async-start(bf16[4,8,4,128,128]{4,3,2,1,0:T(8,128)(2,1)} %broadcast_in_dim.10), calls=%async_computation | async-start | bytes 8388608 | tf_op jit(solution)/shard_map/all_to_all | solution.py:173
  9.3 22.3 %collective-permute-start = (bf16[8,2,128,128]{3,2,1,0:T(8,128)(2,1)S(1)}, bf16[8,2,128,128]{3,2,1,0:T(8,128)(2,1)S(1)}, u32[]{:S(2)}, u32[]{:S(2)}) collective-permute-start(bf16[8,2,128,128]{3,2,1,0:T(8,128)(2,1)S(1)} %copy-done.6), channel_id=1, source_target_pairs={{0,2},{2,0},{1,3},{3,1},{4,6},{6,4},{5,7},{7,5},{8,10},{10,8},{9,1... | collective-permute-start | bytes 1572872 | tf_op jit(solution)/shard_map/ppermute | solution.py:153
  14.9 16.7 %collective-permute-start.2 = (bf16[1,8,128,128]{3,2,1,0:T(8,128)(2,1)S(1)}, bf16[1,8,128,128]{3,2,1,0:T(8,128)(2,1)S(1)}, u32[]{:S(2)}, u32[]{:S(2)}) collective-permute-start(bf16[1,8,128,128]{3,2,1,0:T(8,128)(2,1)S(1)} %get-tuple-element.25), channel_id=1, source_target_pairs={{16,0},{32,16},{48,32},{64,48},{80,64},{96,80},{112,96},{17,1},{33... | collective-permute-start | bytes 786440 | tf_op jit(solution)/shard_map/ppermute | solution.py:163
  16.2 15.4 %collective-permute-start.1 = (bf16[1,8,128,128]{3,2,1,0:T(8,128)(2,1)S(1)}, bf16[1,8,128,128]{3,2,1,0:T(8,128)(2,1)S(1)}, u32[]{:S(2)}, u32[]{:S(2)}) collective-permute-start(bf16[1,8,128,128]{3,2,1,0:T(8,128)(2,1)S(1)} %get-tuple-element.26), channel_id=1, source_target_pairs={{0,16},{16,32},{32,48},{48,64},{64,80},{80,96},{96,112},{1,17},{17... | collective-permute-start | bytes 786440 | tf_op jit(solution)/shard_map/ppermute | solution.py:163
  20.2 37.6 %collective-permute-start.6 = (bf16[8,4,128,128]{3,2,1,0:T(8,128)(2,1)S(1)}, bf16[8,4,128,128]{3,2,1,0:T(8,128)(2,1)}, u32[]{:S(2)}, u32[]{:S(2)}) collective-permute-start(bf16[8,4,128,128]{3,2,1,0:T(8,128)(2,1)S(1)} %copy-done.1), channel_id=1, source_target_pairs={{0,16},{16,0},{1,17},{17,1},{2,18},{18,2},{3,19},{19,3},{4,20},{20... | collective-permute-start | bytes 3145736 | tf_op jit(solution)/shard_map/ppermute | solution.py:153
  31.6 58.6 %copy-start.4 = (bf16[1,8,128,128]{3,2,1,0:T(8,128)(2,1)}, bf16[1,8,128,128]{3,2,1,0:T(8,128)(2,1)S(1)}, u32[]{:S(2)}) copy-start(bf16[1,8,128,128]{3,2,1,0:T(8,128)(2,1)S(1)} %collective-permute-done.2.refs_6_) | copy-start | bytes 786436
  31.6 30.9 %copy-start.5 = (bf16[1,8,128,128]{3,2,1,0:T(8,128)(2,1)}, bf16[1,8,128,128]{3,2,1,0:T(8,128)(2,1)S(1)}, u32[]{:S(2)}) copy-start(bf16[1,8,128,128]{3,2,1,0:T(8,128)(2,1)S(1)} %collective-permute-done.1.refs_5_) | copy-start | bytes 786436
  31.7 12.3 %collective-permute-start.5 = (bf16[8,2,128,128]{3,2,1,0:T(8,128)(2,1)S(1)}, bf16[8,2,128,128]{3,2,1,0:T(8,128)(2,1)S(1)}, u32[]{:S(2)}, u32[]{:S(2)}) collective-permute-start(bf16[8,2,128,128]{3,2,1,0:T(8,128)(2,1)S(1)} %get-tuple-element.28), channel_id=1, source_target_pairs={{0,4},{4,8},{8,12},{12,0},{1,5},{5,9},{9,13},{13,1},{2,6},{6,10},{... | collective-permute-start | bytes 1572872 | tf_op jit(solution)/shard_map/ppermute | solution.py:149
  33.1 23.3 %collective-permute-start.4 = (bf16[8,2,128,128]{3,2,1,0:T(8,128)(2,1)S(1)}, bf16[8,2,128,128]{3,2,1,0:T(8,128)(2,1)S(1)}, u32[]{:S(2)}, u32[]{:S(2)}) collective-permute-start(bf16[8,2,128,128]{3,2,1,0:T(8,128)(2,1)S(1)} %get-tuple-element.28), channel_id=1, source_target_pairs={{0,8},{4,12},{8,0},{12,4},{1,9},{5,13},{9,1},{13,5},{2,10},{6,14},... | collective-permute-start | bytes 1572872 | tf_op jit(solution)/shard_map/ppermute | solution.py:149
  35.7 22.1 %collective-permute-start.3 = (bf16[8,2,128,128]{3,2,1,0:T(8,128)(2,1)S(1)}, bf16[8,2,128,128]{3,2,1,0:T(8,128)(2,1)S(1)}, u32[]{:S(2)}, u32[]{:S(2)}) collective-permute-start(bf16[8,2,128,128]{3,2,1,0:T(8,128)(2,1)S(1)} %get-tuple-element.28), channel_id=1, source_target_pairs={{0,12},{4,0},{8,4},{12,8},{1,13},{5,1},{9,5},{13,9},{2,14},{6,2},{... | collective-permute-start | bytes 1572872 | tf_op jit(solution)/shard_map/ppermute | solution.py:149
  57.8 14.3 %collective-permute-start.10 = (bf16[8,2,128,128]{3,2,1,0:T(8,128)(2,1)S(1)}, bf16[8,2,128,128]{3,2,1,0:T(8,128)(2,1)S(1)}, u32[]{:S(2)}, u32[]{:S(2)}) collective-permute-start(bf16[8,2,128,128]{3,2,1,0:T(8,128)(2,1)S(1)} %get-tuple-element.19), channel_id=1, source_target_pairs={{0,4},{4,8},{8,12},{12,0},{1,5},{5,9},{9,13},{13,1},{2,6},{6,10},{... | collective-permute-start | bytes 1572872 | tf_op jit(solution)/shard_map/ppermute | solution.py:149
  59.6 25.8 %collective-permute-start.9 = (bf16[8,2,128,128]{3,2,1,0:T(8,128)(2,1)S(1)}, bf16[8,2,128,128]{3,2,1,0:T(8,128)(2,1)S(1)}, u32[]{:S(2)}, u32[]{:S(2)}) collective-permute-start(bf16[8,2,128,128]{3,2,1,0:T(8,128)(2,1)S(1)} %get-tuple-element.19), channel_id=1, source_target_pairs={{0,8},{4,12},{8,0},{12,4},{1,9},{5,13},{9,1},{13,5},{2,10},{6,14},... | collective-permute-start | bytes 1572872 | tf_op jit(solution)/shard_map/ppermute | solution.py:149
  62.5 22.9 %collective-permute-start.8 = (bf16[8,2,128,128]{3,2,1,0:T(8,128)(2,1)S(1)}, bf16[8,2,128,128]{3,2,1,0:T(8,128)(2,1)S(1)}, u32[]{:S(2)}, u32[]{:S(2)}) collective-permute-start(bf16[8,2,128,128]{3,2,1,0:T(8,128)(2,1)S(1)} %get-tuple-element.19), channel_id=1, source_target_pairs={{0,12},{4,0},{8,4},{12,8},{1,13},{5,1},{9,5},{13,9},{2,14},{6,2},{... | collective-permute-start | bytes 1572872 | tf_op jit(solution)/shard_map/ppermute | solution.py:149
  62.8 24.3 %copy-start = (bf16[4,8,2,128,128]{4,3,2,1,0:T(8,128)(2,1)}, bf16[4,8,2,128,128]{4,3,2,1,0:T(8,128)(2,1)S(1)}, u32[]{:S(2)}) copy-start(bf16[4,8,2,128,128]{4,3,2,1,0:T(8,128)(2,1)S(1)} %pad_maximum_fusion.refs_0_.refs_2_) | copy-start | bytes 6291460
  62.8 77.6 %collective-permute-start.7 = (bf16[4,8,2,128,128]{4,3,2,1,0:T(8,128)(2,1)S(1)}, bf16[4,8,2,128,128]{4,3,2,1,0:T(8,128)(2,1)}, u32[]{:S(2)}, u32[]{:S(2)}) collective-permute-start(bf16[4,8,2,128,128]{4,3,2,1,0:T(8,128)(2,1)S(1)} %pad_maximum_fusion.refs_0_.refs_2_), channel_id=1, source_target_pairs={{0,1},{1,0},{2,3},{3,2},{4,5},{5,4},{6,7},{7,6},{8,9},{9,8},{10,11... | collective-permute-start | bytes 6291464 | tf_op jit(solution)/shard_map/ppermute | solution.py:153
  87.0 63.8 %collective-permute-start.11 = (bf16[4,8,2,128,128]{4,3,2,1,0:T(8,128)(2,1)}, bf16[4,8,2,128,128]{4,3,2,1,0:T(8,128)(2,1)}, u32[]{:S(2)}, u32[]{:S(2)}) collective-permute-start(bf16[4,8,2,128,128]{4,3,2,1,0:T(8,128)(2,1)} %pad_maximum_fusion.1.refs_2_), channel_id=1, source_target_pairs={{0,1},{1,0},{2,3},{3,2},{4,5},{5,4},{6,7},{7,6},{8,9},{9,8},{10,11... | collective-permute-start | bytes 6291464 | tf_op jit(solution)/shard_map/ppermute | solution.py:153
  90.3 41.3 %collective-permute-start.13 = (bf16[10,1,128,128]{3,2,1,0:T(8,128)(2,1)S(1)}, bf16[10,1,128,128]{3,2,1,0:T(8,128)(2,1)S(1)}, u32[]{:S(2)}, u32[]{:S(2)}) collective-permute-start(bf16[10,1,128,128]{3,2,1,0:T(8,128)(2,1)S(1)} %get-tuple-element.29), channel_id=1, source_target_pairs={{1,0},{2,1},{3,2},{4,3},{5,4},{6,5},{7,6},{8,7},{9,8},{10,9},{11,1... | collective-permute-start | bytes 983048 | tf_op jit(solution)/shard_map/ppermute | solution.py:195
  92.3 41.8 %collective-permute-start.12 = (bf16[10,1,128,128]{3,2,1,0:T(8,128)(2,1)S(1)}, bf16[10,1,128,128]{3,2,1,0:T(8,128)(2,1)S(1)}, u32[]{:S(2)}, u32[]{:S(2)}) collective-permute-start(bf16[10,1,128,128]{3,2,1,0:T(8,128)(2,1)S(1)} %get-tuple-element.30), channel_id=1, source_target_pairs={{0,1},{1,2},{2,3},{3,4},{4,5},{5,6},{6,7},{7,8},{8,9},{9,10},{10,1... | collective-permute-start | bytes 983048 | tf_op jit(solution)/shard_map/ppermute | solution.py:194
  99.8 78.2 %collective-permute-start.16 = (bf16[8,4,128,128]{3,2,1,0:T(8,128)(2,1)}, bf16[8,4,128,128]{3,2,1,0:T(8,128)(2,1)}, u32[]{:S(2)}, u32[]{:S(2)}) collective-permute-start(bf16[8,4,128,128]{3,2,1,0:T(8,128)(2,1)} %dynamic-slice_bitcast_fusion), channel_id=1, source_target_pairs={{0,16},{16,0},{1,17},{17,1},{2,18},{18,2},{3,19},{19,3},{4,20},{20... | collective-permute-start | bytes 3145736 | tf_op jit(solution)/shard_map/ppermute | solution.py:153
  131.7 8.7 %copy-start.2 = (bf16[10,1,128,128]{3,2,1,0:T(8,128)(2,1)}, bf16[10,1,128,128]{3,2,1,0:T(8,128)(2,1)S(1)}, u32[]{:S(2)}) copy-start(bf16[10,1,128,128]{3,2,1,0:T(8,128)(2,1)S(1)} %collective-permute-done.13.refs_8_) | copy-start | bytes 983044
  131.7 46.3 %collective-permute-start.15 = (bf16[8,4,128,128]{3,2,1,0:T(8,128)(2,1)}, bf16[8,4,128,128]{3,2,1,0:T(8,128)(2,1)}, u32[]{:S(2)}, u32[]{:S(2)}) collective-permute-start(bf16[8,4,128,128]{3,2,1,0:T(8,128)(2,1)} %collective-permute-done.6.refs_10_), channel_id=1, source_target_pairs={{0,96},{32,0},{64,32},{96,64},{1,97},{33,1},{65,33},{97,65},{2,98}... | collective-permute-start | bytes 3145736 | tf_op jit(solution)/shard_map/ppermute | solution.py:149
  134.1 6.3 %copy-start.3 = (bf16[10,1,128,128]{3,2,1,0:T(8,128)(2,1)}, bf16[10,1,128,128]{3,2,1,0:T(8,128)(2,1)S(1)}, u32[]{:S(2)}) copy-start(bf16[10,1,128,128]{3,2,1,0:T(8,128)(2,1)S(1)} %collective-permute-done.12.refs_7_) | copy-start | bytes 983044
  134.1 43.9 %collective-permute-start.14 = (bf16[8,4,128,128]{3,2,1,0:T(8,128)(2,1)}, bf16[8,4,128,128]{3,2,1,0:T(8,128)(2,1)}, u32[]{:S(2)}, u32[]{:S(2)}) collective-permute-start(bf16[8,4,128,128]{3,2,1,0:T(8,128)(2,1)} %collective-permute-done.6.refs_10_), channel_id=1, source_target_pairs={{0,32},{32,64},{64,96},{96,0},{1,33},{33,65},{65,97},{97,1},{2,34}... | collective-permute-start | bytes 3145736 | tf_op jit(solution)/shard_map/ppermute | solution.py:149

commit v5 on v1

--- a/solution.py
+++ b/solution.py
@@ -17,15 +17,15 @@
 
 
 def terms_kernel(layout, offsets, first, place, ls, rs, act, *refs):
-    la, lac, lz, lzc, psi, up, down, west, east = refs[:9]
+    whole, whole_other, turned, turned_other, psi, up, down, west, east = refs[:9]
     rights, rest = [], refs[9:]
     for pieces in layout:
         rights.append(rest[:pieces])
         rest = rest[pieces:]
-    if first:
-        hout, lbuf, rbuf, grid, inner, psem, lsem, rsem = rest
-    else:
-        hin, hout, lbuf, rbuf, grid, inner, psem, lsem, rsem = rest
+    hin = None
+    if not first:
+        hin, rest = rest[0], rest[1:]
+    hout, lbuf, rbuf, grid, inner, acc, psem, lsem, rsem, hsem = rest
     steps = len(layout)
     n = pl.program_id(0)
     here = place[0]
@@ -36,10 +36,10 @@
 
     def left_copies(step, slot, own):
         p, _ = chunk(step)
-        a, b, where = (la, lac, p) if own else (lz, lzc, (p - y) & 3)
+        mine, theirs, where = (whole, whole_other, p) if own else (turned, turned_other, (p - y) & 3)
         return (
-            pltpu.make_async_copy(a.at[where], lbuf.at[slot, core], lsem.at[slot, 0]),
-            pltpu.make_async_copy(b.at[where], lbuf.at[slot, 1 - core], lsem.at[slot, 1]),
+            pltpu.make_async_copy(mine.at[where], lbuf.at[slot, core], lsem.at[slot, 0]),
+            pltpu.make_async_copy(theirs.at[where], lbuf.at[slot, 1 - core], lsem.at[slot, 1]),
         )
 
     def right_copies(step, slot):
@@ -77,6 +77,8 @@
         for copy in psi_copies:
             copy.start()
         fetch(0, 0)
+        if not first:
+            pltpu.make_async_copy(hin, acc, hsem.at[COLS]).start()
 
     for step in range(1, steps):
 
@@ -86,6 +88,8 @@
 
     @pl.when(n == 0)
     def _():
+        if first:
+            acc[...] = jnp.zeros_like(acc)
         for copy in psi_copies:
             copy.wait()
 
@@ -114,32 +118,43 @@
 
     lax.fori_loop(0, ROWS, one_row, 0, unroll=True)
 
-    for c in range(COLS):
-        joined = jnp.concatenate([rbuf[slot, c, w] for w in range(TERMS)], axis=1)
-        part = lax.dot_general(
-            inner[c], joined, (((1,), (1,)), ((), ())), preferred_element_type=jnp.float32
-        ).reshape(ROWS, B, B)
+    if not first:
 
         @pl.when(n == 0)
         def _():
-            hout[:, c] = part if first else hin[:, c] + part
-
-        @pl.when(n != 0)
-        def _():
-            hout[:, c] += part
-
-
-def add_terms(offsets, place, ls, rs, act, lefts, psis, rights, total):
+            pltpu.make_async_copy(hin, acc, hsem.at[COLS]).wait()
+
+    outward = [pltpu.make_async_copy(acc.at[:, c], hout.at[:, c], hsem.at[c]) for c in range(COLS)]
+    for half in range(2):
+        columns = range(half * COLS // 2, (half + 1) * COLS // 2)
+        for c in columns:
+            joined = jnp.concatenate([rbuf[slot, c, w] for w in range(TERMS)], axis=1)
+            part = lax.dot_general(
+                inner[c], joined, (((1,), (1,)), ((), ())), preferred_element_type=jnp.float32
+            ).reshape(ROWS, B, B)
+            acc[:, c] += part
+
+        @pl.when(n == steps - 1)
+        def _():
+            for c in columns:
+                outward[c].start()
+
+    @pl.when(n == steps - 1)
+    def _():
+        for copy in outward:
+            copy.wait()
+
+
+def add_terms(offsets, lefts, place, ls, rs, act, psis, rights, total):
     steps = len(rights)
     layout = tuple(len(pieces) for pieces in rights)
     first = total is None
     anywhere = pl.BlockSpec(memory_space=pl.ANY)
-    whole = pl.BlockSpec((ROWS, COLS, B, B), lambda n, *_: (0, 0, 0, 0), pipeline_mode=pl.Buffered(1))
     operands = [*lefts, *psis, *(piece for pieces in rights for piece in pieces)]
     in_specs = [anywhere] * len(operands)
     if not first:
         operands.append(total)
-        in_specs.append(whole)
+        in_specs.append(anywhere)
     return pl.pallas_call(
         functools.partial(terms_kernel, layout, offsets, first),
         out_shape=jax.ShapeDtypeStruct((ROWS, COLS, B, B), jnp.float32),
@@ -147,26 +162,24 @@
             num_scalar_prefetch=4,
             grid=(steps,),
             in_specs=in_specs,
-            out_specs=whole,
+            out_specs=anywhere,
             scratch_shapes=[
                 pltpu.VMEM((2, 2, ROWS, 2, B, B), jnp.bfloat16),
                 pltpu.VMEM((2, COLS, TERMS, B, B), jnp.bfloat16),
                 pltpu.VMEM((ROWS + 2, COLS + 2, B, B), jnp.bfloat16),
                 pltpu.VMEM((COLS, ROWS * B, TERMS * B), jnp.bfloat16),
+                pltpu.VMEM((ROWS, COLS, B, B), jnp.float32),
                 pltpu.SemaphoreType.DMA((5,)),
                 pltpu.SemaphoreType.DMA((2, 2)),
                 pltpu.SemaphoreType.DMA((2, 2)),
+                pltpu.SemaphoreType.DMA((COLS + 1,)),
             ],
         ),
         input_output_aliases={} if first else {4 + len(operands) - 1: 0},
         compiler_params=pltpu.CompilerParams(
             vmem_limit_bytes=56 << 20, dimension_semantics=("arbitrary",)
         ),
-        cost_estimate=pl.CostEstimate(
-            flops=steps * 2 * 2 * ROWS * COLS * TERMS * B**3,
-            bytes_accessed=(steps * 2 + 11) << 20,
-            transcendentals=0,
-        ),
+        cost_estimate=pl.CostEstimate(flops=1, bytes_accessed=1, transcendentals=0),
     )(place, ls, rs, act, *operands)
 
 
@@ -197,25 +210,29 @@
     place = lax.axis_index((*GRP, *WIDE)).astype(jnp.int32)[None]
 
     left_y = lax.all_gather(left_env, "y", axis=0)
-    right_m = ring(right_env, "x", 1)
-    right_p = ring(right_env, "x", -1)
     left_z = swap(left_env, "zh")
     north, south = edges(psi, GRP, 0)
 
-    right_m, right_p, left_z, north, south, own = after(
-        (right_m, right_p, left_z, north, south, right_env), ()
-    )
+    north, south, own = after((north, south, right_env), ())
+    right_m = ring(own, "x", 1)
+    right_p = ring(own, "x", -1)
+
+    left_z, own = after((left_z, own), ())
     right_z = swap(own, "zl")
+    left_zm = ring(left_z, "y", 1)
+    left_zp = ring(left_z, "y", -1)
+
+    right_m, right_p, left_zm, left_zp, left_z = after((right_m, right_p, left_zm, left_zp, left_z), ())
     far_0 = ring(right_m[:4], "x", 1)
     far_1 = ring(right_p[4:], "x", -1)
-    left_zm = ring(left_z, "y", 1)
-    left_zp = ring(left_z, "y", -1)
     left_z2 = ring(left_z, "y", 2)
     sides = jnp.concatenate([north[:, ::7], psi[:, ::7], south[:, ::7]], axis=0)
     west = lax.ppermute(sides[:, 1:], WIDE, [(i, i + 1) for i in range(15)])
     east = lax.ppermute(sides[:, :1], WIDE, [(i + 1, i) for i in range(15)])
 
-    right_z, far_0, far_1 = after((right_z, far_0, far_1), ())
+    right_z, far_0, far_1, left_z2, west, east = after(
+        (right_z, far_0, far_1, left_z2, west, east), ()
+    )
     right_zm = ring(right_z, "x", 1)
     right_zp = ring(right_z, "x", -1)
     far_z0 = swap(far_0, "zl")
@@ -225,11 +242,11 @@
     left_zc = swap(left_zs, "core")
 
     shared = (
+        (left_y, left_yc, left_zs, left_zc),
         place,
         left_shift,
         right_shift,
         active,
-        (left_y, left_yc, left_zs, left_zc),
         (psi, north, south, west, east),
     )
     total = add_terms(

time: 193 us -> 144 us (0.75)
  the two profiles are of different devices: /device:TPU:1 before, /device:TPU:15 now
where the time goes in v5:
time: 144 us
  Pallas kernels  48.9 us (34%)
  waiting for transfers between devices  40.6 us (28%)
  starting transfers between devices  37.1 us (26%)
  between operations  13.7 us (10%)
  local copies, waits for them, and re-layouts  2.93 us (2%)
    pallas_call x2, Pallas kernels, add_terms(): pl.pallas_call(functools.partial(terms_kernel, layout, offsets, first), o...  48.9 us
    ppermute x6, starting transfers between devices, swap(): return lax.ppermute(value, axis, [(0, 1), (1, 0)])  14.1 us
    ppermute x6, waiting for transfers between devices, swap(): return lax.ppermute(value, axis, [(0, 1), (1, 0)])  12.8 us
    ppermute x9, starting transfers between devices, ring(): return lax.ppermute(value, axis, [(i, (i + shift) % 4) for i in range(4)])  12.4 us
    ppermute x9, waiting for transfers between devices, ring(): return lax.ppermute(value, axis, [(i, (i + shift) % 4) for i in range(4)])  12 us
    ppermute x1, waiting for transfers between devices, per_device(): east = lax.ppermute(sides[:, :1], WIDE, [(i + 1, i) for i in range(15)])  6.72 us
    ppermute x2, starting transfers between devices, edges(): return (lax.ppermute(last, axes, up), lax.ppermute(leading, axes, down))  5.73 us
    ppermute x2, waiting for transfers between devices, edges(): return (lax.ppermute(last, axes, up), lax.ppermute(leading, axes, down))  4.42 us
  transfers between devices with their start and end apart: 20, of which 8 were waited for; matrix products, arithmetic and copies ran while one was open for 2% of the time, Pallas kernels for 20%

profile of v5, /device:TPU:15, one launch (start us, length us, event | category | flops | bytes accessed | tf_op | source)
XLA Modules:
  0.0 143.6 jit_solution(8649608552701277486)
XLA Ops:
  6.5 0.7 all-gather.3.cloned.1.call-update
  7.3 1.1 fusion
  8.3 3.8 %collective-permute-start.2 = (bf16[1,8,128,128]{3,2,1,0:T(8,128)(2,1)S(1)}, bf16[1,8,128,128]{3,2,1,0:T(8,128)(2,1)S(1)}, u32[]{:S(2)}, u32[]{:S(2)}) collective-permute-start(bf16[1,8,128,128]{3,2,1,0:T(8,128)(2,1)S(1)} %get-tuple-element.37), channel_id=1, source_target_pairs={{16,0},{32,16},{48,32},{64,48},{80,64},{96,80},{112,96},{17,1},{33... | collective-permute-start | bytes 786440 | tf_op jit(solution)/shard_map/ppermute | solution.py:201
  12.2 1.9 %collective-permute-start.1 = (bf16[1,8,128,128]{3,2,1,0:T(8,128)(2,1)S(1)}, bf16[1,8,128,128]{3,2,1,0:T(8,128)(2,1)S(1)}, u32[]{:S(2)}, u32[]{:S(2)}) collective-permute-start(bf16[1,8,128,128]{3,2,1,0:T(8,128)(2,1)S(1)} %get-tuple-element.38), channel_id=1, source_target_pairs={{0,16},{16,32},{32,48},{48,64},{64,80},{80,96},{96,112},{1,17},{17... | collective-permute-start | bytes 786440 | tf_op jit(solution)/shard_map/ppermute | solution.py:201
  14.1 3.4 %collective-permute-start.5 = (bf16[8,2,128,128]{3,2,1,0:T(8,128)(2,1)}, bf16[8,2,128,128]{3,2,1,0:T(8,128)(2,1)S(1)}, u32[]{:S(2)}, u32[]{:S(2)}) collective-permute-start(bf16[8,2,128,128]{3,2,1,0:T(8,128)(2,1)} %param.6), channel_id=1, source_target_pairs={{0,2},{2,0},{1,3},{3,1},{4,6},{6,4},{5,7},{7,5},{8,10},{10,8},{9,1... | collective-permute-start | bytes 1572872 | tf_op jit(solution)/shard_map/ppermute | solution.py:191
  17.5 4.4 %collective-permute-done.1.refs_5_ = bf16[1,8,128,128]{3,2,1,0:T(8,128)(2,1)S(1)} collective-permute-done((bf16[1,8,128,128]{3,2,1,0:T(8,128)(2,1)S(1)}, bf16[1,8,128,128]{3,2,1,0:T(8,128)(2,1)S(1)}, u32[]{:S(2)}, u32[]{:S(2)}) %collective-permute-start.1) | collective-permute-done | bytes 262176 | tf_op jit(solution)/shard_map/ppermute | solution.py:201
  21.9 3.1 %collective-permute-start.4 = (bf16[8,4,128,128]{3,2,1,0:T(8,128)(2,1)}, bf16[8,4,128,128]{3,2,1,0:T(8,128)(2,1)S(1)}, u32[]{:S(2)}, u32[]{:S(2)}) collective-permute-start(bf16[8,4,128,128]{3,2,1,0:T(8,128)(2,1)} %refs_9_.1), channel_id=1, source_target_pairs={{0,96},{32,0},{64,32},{96,64},{1,97},{33,1},{65,33},{97,65},{2,98}... | collective-permute-start | bytes 3145736 | tf_op jit(solution)/shard_map/ppermute | solution.py:187
  25.0 9.2 %collective-permute-done.5 = bf16[8,2,128,128]{3,2,1,0:T(8,128)(2,1)S(1)} collective-permute-done((bf16[8,2,128,128]{3,2,1,0:T(8,128)(2,1)}, bf16[8,2,128,128]{3,2,1,0:T(8,128)(2,1)S(1)}, u32[]{:S(2)}, u32[]{:S(2)}) %collective-permute-start.5) | collective-permute-done | bytes 524320 | tf_op jit(solution)/shard_map/ppermute | solution.py:191
  34.1 0.2 collective-permute-start.7
  34.3 1.3 collective-permute-start.6
  35.6 3.1 %collective-permute-start.8 = (bf16[8,4,128,128]{3,2,1,0:T(8,128)(2,1)}, bf16[8,4,128,128]{3,2,1,0:T(8,128)(2,1)S(1)}, u32[]{:S(2)}, u32[]{:S(2)}) collective-permute-start(bf16[8,4,128,128]{3,2,1,0:T(8,128)(2,1)} %refs_9_.1), channel_id=1, source_target_pairs={{0,16},{16,0},{1,17},{17,1},{2,18},{18,2},{3,19},{19,3},{4,20},{20... | collective-permute-start | bytes 3145736 | tf_op jit(solution)/shard_map/ppermute | solution.py:191
  38.7 1.1 slice.32
  40.0 11.6 %collective-permute-done.7 = bf16[8,2,128,128]{3,2,1,0:T(8,128)(2,1)S(1)} collective-permute-done((bf16[8,2,128,128]{3,2,1,0:T(8,128)(2,1)S(1)}, bf16[8,2,128,128]{3,2,1,0:T(8,128)(2,1)S(1)}, u32[]{:S(2)}, u32[]{:S(2)}) %collective-permute-start.7) | collective-permute-done | bytes 524320 | tf_op jit(solution)/shard_map/ppermute | solution.py:187
  51.6 3.0 %collective-permute-start.13 = (bf16[10,1,128,128]{3,2,1,0:T(8,128)(2,1)S(1)}, bf16[10,1,128,128]{3,2,1,0:T(8,128)(2,1)S(1)}, u32[]{:S(2)}, u32[]{:S(2)}) collective-permute-start(bf16[10,1,128,128]{3,2,1,0:T(8,128)(2,1)S(1)} %get-tuple-element.39), channel_id=1, source_target_pairs={{1,0},{2,1},{3,2},{4,3},{5,4},{6,5},{7,6},{8,7},{9,8},{10,9},{11,1... | collective-permute-start | bytes 983048 | tf_op jit(solution)/shard_map/ppermute | solution.py:231
  54.8 1.9 %collective-permute-start.10 = (bf16[4,4,128,128]{3,2,1,0:T(8,128)(2,1)S(1)}, bf16[4,4,128,128]{3,2,1,0:T(8,128)(2,1)S(1)}, u32[]{:S(2)}, u32[]{:S(2)}) collective-permute-start(bf16[4,4,128,128]{3,2,1,0:T(8,128)(2,1)S(1)} %slice.30), channel_id=1, source_target_pairs={{0,96},{32,0},{64,32},{96,64},{1,97},{33,1},{65,33},{97,65},{2,98}... | collective-permute-start | bytes 1572872 | tf_op jit(solution)/shard_map/ppermute | solution.py:187
  56.7 0.8 collective-permute-start.9
  57.5 2.4 %collective-permute-start.11 = (bf16[8,2,128,128]{3,2,1,0:T(8,128)(2,1)S(1)}, bf16[8,2,128,128]{3,2,1,0:T(8,128)(2,1)S(1)}, u32[]{:S(2)}, u32[]{:S(2)}) collective-permute-start(bf16[8,2,128,128]{3,2,1,0:T(8,128)(2,1)S(1)} %collective-permute-done.5), channel_id=1, source_target_pairs={{0,8},{4,12},{8,0},{12,4},{1,9},{5,13},{9,1},{13,5},{2,10},{6,14},... | collective-permute-start | bytes 1572872 | tf_op jit(solution)/shard_map/ppermute | solution.py:187
  59.9 6.7 %collective-permute-done.13.refs_8_ = bf16[10,1,128,128]{3,2,1,0:T(8,128)(2,1)S(1)} collective-permute-done((bf16[10,1,128,128]{3,2,1,0:T(8,128)(2,1)S(1)}, bf16[10,1,128,128]{3,2,1,0:T(8,128)(2,1)S(1)}, u32[]{:S(2)}, u32[]{:S(2)}) %collective-permute-start.13) | collective-permute-done | bytes 327712 | tf_op jit(solution)/shard_map/ppermute | solution.py:231
  66.7 1.9 %collective-permute-start.12 = (bf16[10,1,128,128]{3,2,1,0:T(8,128)(2,1)S(1)}, bf16[10,1,128,128]{3,2,1,0:T(8,128)(2,1)S(1)}, u32[]{:S(2)}, u32[]{:S(2)}) collective-permute-start(bf16[10,1,128,128]{3,2,1,0:T(8,128)(2,1)S(1)} %get-tuple-element.40), channel_id=1, source_target_pairs={{0,1},{1,2},{2,3},{3,4},{4,5},{5,6},{6,7},{7,8},{8,9},{9,10},{10,1... | collective-permute-start | bytes 983048 | tf_op jit(solution)/shard_map/ppermute | solution.py:230
  68.6 4.0 %collective-permute-done.12.refs_7_ = bf16[10,1,128,128]{3,2,1,0:T(8,128)(2,1)S(1)} collective-permute-done((bf16[10,1,128,128]{3,2,1,0:T(8,128)(2,1)S(1)}, bf16[10,1,128,128]{3,2,1,0:T(8,128)(2,1)S(1)}, u32[]{:S(2)}, u32[]{:S(2)}) %collective-permute-start.12) | collective-permute-done | bytes 327712 | tf_op jit(solution)/shard_map/ppermute | solution.py:230
  72.6 0.4 collective-permute-done.11
  73.0 0.4 copy-done.8
  73.4 0.2 copy-done.9
  73.6 0.3 pad_maximum_fusion.refs_2_
  73.9 6.7 %collective-permute-start.14 = (bf16[4,8,2,128,128]{4,3,2,1,0:T(8,128)(2,1)S(1)}, bf16[4,8,2,128,128]{4,3,2,1,0:T(8,128)(2,1)}, u32[]{:S(2)}, u32[]{:S(2)}) collective-permute-start(bf16[4,8,2,128,128]{4,3,2,1,0:T(8,128)(2,1)S(1)} %pad_maximum_fusion.refs_2_), channel_id=1, source_target_pairs={{0,1},{1,0},{2,3},{3,2},{4,5},{5,4},{6,7},{7,6},{8,9},{9,8},{10,11... | collective-permute-start | bytes 6291464 | tf_op jit(solution)/shard_map/ppermute | solution.py:191
  80.8 2.7 %collective-permute-start.15 = (bf16[8,4,128,128]{3,2,1,0:T(8,128)(2,1)S(1)}, bf16[8,4,128,128]{3,2,1,0:T(8,128)(2,1)}, u32[]{:S(2)}, u32[]{:S(2)}) collective-permute-start(bf16[8,4,128,128]{3,2,1,0:T(8,128)(2,1)S(1)} %collective-permute-done.8.refs_10_), channel_id=1, source_target_pairs={{0,32},{32,64},{64,96},{96,0},{1,33},{33,65},{65,97},{97,1},{2,34}... | collective-permute-start | bytes 3145736 | tf_op jit(solution)/shard_map/ppermute | solution.py:187
  83.4 0.4 collective-permute-start.17
  83.8 2.5 %collective-permute-done.14.refs_3_ = bf16[4,8,2,128,128]{4,3,2,1,0:T(8,128)(2,1)} collective-permute-done((bf16[4,8,2,128,128]{4,3,2,1,0:T(8,128)(2,1)S(1)}, bf16[4,8,2,128,128]{4,3,2,1,0:T(8,128)(2,1)}, u32[]{:S(2)}, u32[]{:S(2)}) %collective-permute-start.14) | collective-permute-done | bytes 2097184 | tf_op jit(solution)/shard_map/ppermute | solution.py:191
  86.3 0.4 collective-permute-start.18
  86.7 1.1 collective-permute-done.refs_1_
  87.8 28.8 %shard_map.64.refs_13_ = f32[8,8,128,128]{3,2,1,0:T(8,128)} custom-call(s32[1]{0:T(128)} %bitcast.place, s32[32]{0:T(128)} %ls.3, s32[32]{0:T(128)} %rs.3, s32[8,8,32]{2,1,0:T(8,128)} %act.3, bf16[4,8,2,128,128]{4,3,2,1,0:T(8,128)(2,1)} %bitcast.7, bf16[4,8,2,128,128]{4,3,2,1,0:T(8,128)(2,1)} %collective-permute-done.refs_1_, ...), custom_call_target="tpu_custom_call" | custom-call | flops 1 | bytes 1 | tf_op jit(solution)/shard_map/pallas_call | solution.py:158
  116.6 20.1 %shard_map.65 = f32[8,8,128,128]{3,2,1,0:T(8,128)} custom-call(s32[1]{0:T(128)} %bitcast.place, s32[32]{0:T(128)} %ls.3, s32[32]{0:T(128)} %rs.3, s32[8,8,32]{2,1,0:T(8,128)} %act.3, bf16[4,8,2,128,128]{4,3,2,1,0:T(8,128)(2,1)} %bitcast.8, bf16[4,8,2,128,128]{4,3,2,1,0:T(8,128)(2,1)} %collective-permute-done.refs_1_, ...), custom_call_target="tpu_custom_call", output_to_operand_aliasing={{}: (17, {})} | custom-call | flops 1 | bytes 1 | tf_op jit(solution)/shard_map/pallas_call | solution.py:158
  (40 shorter events, 0.4 us)
Async XLA Ops:
  6.5 74.1 %all-gather.3.cloned.1.call-start = ((), (), s32[]{:S(2)}) async-start(), calls=%async_computation | async-start | bytes 2621440 | tf_op jit(solution)/shard_map/all_gather | solution.py:212
  8.3 9.1 %collective-permute-start.2 = (bf16[1,8,128,128]{3,2,1,0:T(8,128)(2,1)S(1)}, bf16[1,8,128,128]{3,2,1,0:T(8,128)(2,1)S(1)}, u32[]{:S(2)}, u32[]{:S(2)}) collective-permute-start(bf16[1,8,128,128]{3,2,1,0:T(8,128)(2,1)S(1)} %get-tuple-element.37), channel_id=1, source_target_pairs={{16,0},{32,16},{48,32},{64,48},{80,64},{96,80},{112,96},{17,1},{33... | collective-permute-start | bytes 786440 | tf_op jit(solution)/shard_map/ppermute | solution.py:201
  12.2 9.7 %collective-permute-start.1 = (bf16[1,8,128,128]{3,2,1,0:T(8,128)(2,1)S(1)}, bf16[1,8,128,128]{3,2,1,0:T(8,128)(2,1)S(1)}, u32[]{:S(2)}, u32[]{:S(2)}) collective-permute-start(bf16[1,8,128,128]{3,2,1,0:T(8,128)(2,1)S(1)} %get-tuple-element.38), channel_id=1, source_target_pairs={{0,16},{16,32},{32,48},{48,64},{64,80},{80,96},{96,112},{1,17},{17... | collective-permute-start | bytes 786440 | tf_op jit(solution)/shard_map/ppermute | solution.py:201
  14.1 20.1 %collective-permute-start.5 = (bf16[8,2,128,128]{3,2,1,0:T(8,128)(2,1)}, bf16[8,2,128,128]{3,2,1,0:T(8,128)(2,1)S(1)}, u32[]{:S(2)}, u32[]{:S(2)}) collective-permute-start(bf16[8,2,128,128]{3,2,1,0:T(8,128)(2,1)} %param.6), channel_id=1, source_target_pairs={{0,2},{2,0},{1,3},{3,1},{4,6},{6,4},{5,7},{7,5},{8,10},{10,8},{9,1... | collective-permute-start | bytes 1572872 | tf_op jit(solution)/shard_map/ppermute | solution.py:191
  17.5 37.2 %copy-start.3 = (bf16[1,8,128,128]{3,2,1,0:T(8,128)(2,1)}, bf16[1,8,128,128]{3,2,1,0:T(8,128)(2,1)S(1)}, u32[]{:S(2)}) copy-start(bf16[1,8,128,128]{3,2,1,0:T(8,128)(2,1)S(1)} %collective-permute-done.2.refs_6_) | copy-start | bytes 786436
  21.9 17.9 %copy-start.4 = (bf16[1,8,128,128]{3,2,1,0:T(8,128)(2,1)}, bf16[1,8,128,128]{3,2,1,0:T(8,128)(2,1)S(1)}, u32[]{:S(2)}) copy-start(bf16[1,8,128,128]{3,2,1,0:T(8,128)(2,1)S(1)} %collective-permute-done.1.refs_5_) | copy-start | bytes 786436
  21.9 32.7 %collective-permute-start.4 = (bf16[8,4,128,128]{3,2,1,0:T(8,128)(2,1)}, bf16[8,4,128,128]{3,2,1,0:T(8,128)(2,1)S(1)}, u32[]{:S(2)}, u32[]{:S(2)}) collective-permute-start(bf16[8,4,128,128]{3,2,1,0:T(8,128)(2,1)} %refs_9_.1), channel_id=1, source_target_pairs={{0,96},{32,0},{64,32},{96,64},{1,97},{33,1},{65,33},{97,65},{2,98}... | collective-permute-start | bytes 3145736 | tf_op jit(solution)/shard_map/ppermute | solution.py:187
  25.0 29.7 %collective-permute-start.3 = (bf16[8,4,128,128]{3,2,1,0:T(8,128)(2,1)}, bf16[8,4,128,128]{3,2,1,0:T(8,128)(2,1)S(1)}, u32[]{:S(2)}, u32[]{:S(2)}) collective-permute-start(bf16[8,4,128,128]{3,2,1,0:T(8,128)(2,1)} %refs_9_.1), channel_id=1, source_target_pairs={{0,32},{32,64},{64,96},{96,0},{1,33},{33,65},{65,97},{97,1},{2,34}... | collective-permute-start | bytes 3145736 | tf_op jit(solution)/shard_map/ppermute | solution.py:187
  34.1 17.4 %collective-permute-start.7 = (bf16[8,2,128,128]{3,2,1,0:T(8,128)(2,1)S(1)}, bf16[8,2,128,128]{3,2,1,0:T(8,128)(2,1)S(1)}, u32[]{:S(2)}, u32[]{:S(2)}) collective-permute-start(bf16[8,2,128,128]{3,2,1,0:T(8,128)(2,1)S(1)} %collective-permute-done.5), channel_id=1, source_target_pairs={{0,12},{4,0},{8,4},{12,8},{1,13},{5,1},{9,5},{13,9},{2,14},{6,2},{... | collective-permute-start | bytes 1572872 | tf_op jit(solution)/shard_map/ppermute | solution.py:187
  34.3 20.3 %collective-permute-start.6 = (bf16[8,2,128,128]{3,2,1,0:T(8,128)(2,1)S(1)}, bf16[8,2,128,128]{3,2,1,0:T(8,128)(2,1)S(1)}, u32[]{:S(2)}, u32[]{:S(2)}) collective-permute-start(bf16[8,2,128,128]{3,2,1,0:T(8,128)(2,1)S(1)} %collective-permute-done.5), channel_id=1, source_target_pairs={{0,4},{4,8},{8,12},{12,0},{1,5},{5,9},{9,13},{13,1},{2,6},{6,10},{... | collective-permute-start | bytes 1572872 | tf_op jit(solution)/shard_map/ppermute | solution.py:187
  35.6 37.0 %collective-permute-start.8 = (bf16[8,4,128,128]{3,2,1,0:T(8,128)(2,1)}, bf16[8,4,128,128]{3,2,1,0:T(8,128)(2,1)S(1)}, u32[]{:S(2)}, u32[]{:S(2)}) collective-permute-start(bf16[8,4,128,128]{3,2,1,0:T(8,128)(2,1)} %refs_9_.1), channel_id=1, source_target_pairs={{0,16},{16,0},{1,17},{17,1},{2,18},{18,2},{3,19},{19,3},{4,20},{20... | collective-permute-start | bytes 3145736 | tf_op jit(solution)/shard_map/ppermute | solution.py:191
  51.6 15.1 %collective-permute-start.13 = (bf16[10,1,128,128]{3,2,1,0:T(8,128)(2,1)S(1)}, bf16[10,1,128,128]{3,2,1,0:T(8,128)(2,1)S(1)}, u32[]{:S(2)}, u32[]{:S(2)}) collective-permute-start(bf16[10,1,128,128]{3,2,1,0:T(8,128)(2,1)S(1)} %get-tuple-element.39), channel_id=1, source_target_pairs={{1,0},{2,1},{3,2},{4,3},{5,4},{6,5},{7,6},{8,7},{9,8},{10,9},{11,1... | collective-permute-start | bytes 983048 | tf_op jit(solution)/shard_map/ppermute | solution.py:231
  54.6 19.3 %copy-start.1 = (bf16[8,4,128,128]{3,2,1,0:T(8,128)(2,1)}, bf16[8,4,128,128]{3,2,1,0:T(8,128)(2,1)S(1)}, u32[]{:S(2)}) copy-start(bf16[8,4,128,128]{3,2,1,0:T(8,128)(2,1)S(1)} %collective-permute-done.4.refs_12_) | copy-start | bytes 3145732
  54.6 18.4 %copy-start.2 = (bf16[8,4,128,128]{3,2,1,0:T(8,128)(2,1)}, bf16[8,4,128,128]{3,2,1,0:T(8,128)(2,1)S(1)}, u32[]{:S(2)}) copy-start(bf16[8,4,128,128]{3,2,1,0:T(8,128)(2,1)S(1)} %collective-permute-done.3.refs_11_) | copy-start | bytes 3145732
  54.8 17.8 %collective-permute-start.10 = (bf16[4,4,128,128]{3,2,1,0:T(8,128)(2,1)S(1)}, bf16[4,4,128,128]{3,2,1,0:T(8,128)(2,1)S(1)}, u32[]{:S(2)}, u32[]{:S(2)}) collective-permute-start(bf16[4,4,128,128]{3,2,1,0:T(8,128)(2,1)S(1)} %slice.30), channel_id=1, source_target_pairs={{0,96},{32,0},{64,32},{96,64},{1,97},{33,1},{65,33},{97,65},{2,98}... | collective-permute-start | bytes 1572872 | tf_op jit(solution)/shard_map/ppermute | solution.py:187
  56.7 15.9 %collective-permute-start.9 = (bf16[4,4,128,128]{3,2,1,0:T(8,128)(2,1)S(1)}, bf16[4,4,128,128]{3,2,1,0:T(8,128)(2,1)S(1)}, u32[]{:S(2)}, u32[]{:S(2)}) collective-permute-start(bf16[4,4,128,128]{3,2,1,0:T(8,128)(2,1)S(1)} %slice.29), channel_id=1, source_target_pairs={{0,32},{32,64},{64,96},{96,0},{1,33},{33,65},{65,97},{97,1},{2,34}... | collective-permute-start | bytes 1572872 | tf_op jit(solution)/shard_map/ppermute | solution.py:187
  57.5 15.5 %collective-permute-start.11 = (bf16[8,2,128,128]{3,2,1,0:T(8,128)(2,1)S(1)}, bf16[8,2,128,128]{3,2,1,0:T(8,128)(2,1)S(1)}, u32[]{:S(2)}, u32[]{:S(2)}) collective-permute-start(bf16[8,2,128,128]{3,2,1,0:T(8,128)(2,1)S(1)} %collective-permute-done.5), channel_id=1, source_target_pairs={{0,8},{4,12},{8,0},{12,4},{1,9},{5,13},{9,1},{13,5},{2,10},{6,14},... | collective-permute-start | bytes 1572872 | tf_op jit(solution)/shard_map/ppermute | solution.py:187
  66.7 6.4 %copy-start.5 = (bf16[10,1,128,128]{3,2,1,0:T(8,128)(2,1)}, bf16[10,1,128,128]{3,2,1,0:T(8,128)(2,1)S(1)}, u32[]{:S(2)}) copy-start(bf16[10,1,128,128]{3,2,1,0:T(8,128)(2,1)S(1)} %collective-permute-done.13.refs_8_) | copy-start | bytes 983044
  66.7 5.9 %collective-permute-start.12 = (bf16[10,1,128,128]{3,2,1,0:T(8,128)(2,1)S(1)}, bf16[10,1,128,128]{3,2,1,0:T(8,128)(2,1)S(1)}, u32[]{:S(2)}, u32[]{:S(2)}) collective-permute-start(bf16[10,1,128,128]{3,2,1,0:T(8,128)(2,1)S(1)} %get-tuple-element.40), channel_id=1, source_target_pairs={{0,1},{1,2},{2,3},{3,4},{4,5},{5,6},{6,7},{7,8},{8,9},{9,10},{10,1... | collective-permute-start | bytes 983048 | tf_op jit(solution)/shard_map/ppermute | solution.py:230
  72.6 1.3 copy-start.6
  72.6 15.2 %copy-start.7 = (bf16[8,4,128,128]{3,2,1,0:T(8,128)(2,1)}, bf16[8,4,128,128]{3,2,1,0:T(8,128)(2,1)S(1)}, u32[]{:S(2)}) copy-start(bf16[8,4,128,128]{3,2,1,0:T(8,128)(2,1)S(1)} %collective-permute-done.8.refs_10_) | copy-start | bytes 3145732
  72.6 0.9 copy-start.8
  72.6 1.0 copy-start.9
  73.9 13.9 %copy-start = (bf16[4,8,2,128,128]{4,3,2,1,0:T(8,128)(2,1)}, bf16[4,8,2,128,128]{4,3,2,1,0:T(8,128)(2,1)S(1)}, u32[]{:S(2)}) copy-start(bf16[4,8,2,128,128]{4,3,2,1,0:T(8,128)(2,1)S(1)} %pad_maximum_fusion.refs_2_) | copy-start | bytes 6291460
  73.9 12.4 %collective-permute-start.14 = (bf16[4,8,2,128,128]{4,3,2,1,0:T(8,128)(2,1)S(1)}, bf16[4,8,2,128,128]{4,3,2,1,0:T(8,128)(2,1)}, u32[]{:S(2)}, u32[]{:S(2)}) collective-permute-start(bf16[4,8,2,128,128]{4,3,2,1,0:T(8,128)(2,1)S(1)} %pad_maximum_fusion.refs_2_), channel_id=1, source_target_pairs={{0,1},{1,0},{2,3},{3,2},{4,5},{5,4},{6,7},{7,6},{8,9},{9,8},{10,11... | collective-permute-start | bytes 6291464 | tf_op jit(solution)/shard_map/ppermute | solution.py:191
  80.6 7.1 %collective-permute-start = (bf16[4,8,2,128,128]{4,3,2,1,0:T(8,128)(2,1)}, bf16[4,8,2,128,128]{4,3,2,1,0:T(8,128)(2,1)}, u32[]{:S(2)}, u32[]{:S(2)}) collective-permute-start(bf16[4,8,2,128,128]{4,3,2,1,0:T(8,128)(2,1)} %bitcast.6), channel_id=1, source_target_pairs={{0,1},{1,0},{2,3},{3,2},{4,5},{5,4},{6,7},{7,6},{8,9},{9,8},{10,11... | collective-permute-start | bytes 6291464 | tf_op jit(solution)/shard_map/ppermute | solution.py:191
  80.8 35.8 %collective-permute-start.16 = (bf16[8,4,128,128]{3,2,1,0:T(8,128)(2,1)S(1)}, bf16[8,4,128,128]{3,2,1,0:T(8,128)(2,1)}, u32[]{:S(2)}, u32[]{:S(2)}) collective-permute-start(bf16[8,4,128,128]{3,2,1,0:T(8,128)(2,1)S(1)} %collective-permute-done.8.refs_10_), channel_id=1, source_target_pairs={{0,96},{32,0},{64,32},{96,64},{1,97},{33,1},{65,33},{97,65},{2,98}... | collective-permute-start | bytes 3145736 | tf_op jit(solution)/shard_map/ppermute | solution.py:187
  80.8 35.9 %collective-permute-start.15 = (bf16[8,4,128,128]{3,2,1,0:T(8,128)(2,1)S(1)}, bf16[8,4,128,128]{3,2,1,0:T(8,128)(2,1)}, u32[]{:S(2)}, u32[]{:S(2)}) collective-permute-start(bf16[8,4,128,128]{3,2,1,0:T(8,128)(2,1)S(1)} %collective-permute-done.8.refs_10_), channel_id=1, source_target_pairs={{0,32},{32,64},{64,96},{96,0},{1,33},{33,65},{65,97},{97,1},{2,34}... | collective-permute-start | bytes 3145736 | tf_op jit(solution)/shard_map/ppermute | solution.py:187
  83.4 33.1 %collective-permute-start.17 = (bf16[4,4,128,128]{3,2,1,0:T(8,128)(2,1)}, bf16[4,4,128,128]{3,2,1,0:T(8,128)(2,1)}, u32[]{:S(2)}, u32[]{:S(2)}) collective-permute-start(bf16[4,4,128,128]{3,2,1,0:T(8,128)(2,1)} %copy-done.9), channel_id=1, source_target_pairs={{0,16},{16,0},{1,17},{17,1},{2,18},{18,2},{3,19},{19,3},{4,20},{20... | collective-permute-start | bytes 1572872 | tf_op jit(solution)/shard_map/ppermute | solution.py:191
  86.3 30.3 %collective-permute-start.18 = (bf16[4,4,128,128]{3,2,1,0:T(8,128)(2,1)}, bf16[4,4,128,128]{3,2,1,0:T(8,128)(2,1)}, u32[]{:S(2)}, u32[]{:S(2)}) collective-permute-start(bf16[4,4,128,128]{3,2,1,0:T(8,128)(2,1)} %copy-done.8), channel_id=1, source_target_pairs={{0,16},{16,0},{1,17},{17,1},{2,18},{18,2},{3,19},{19,3},{4,20},{20... | collective-permute-start | bytes 1572872 | tf_op jit(solution)/shard_map/ppermute | solution.py:191
Sparse Core Ops, SparseCore 0:
  9.0 35.3 all-gather.2

commit v6 on v5

--- a/solution.py
+++ b/solution.py
@@ -222,7 +222,7 @@
     left_zm = ring(left_z, "y", 1)
     left_zp = ring(left_z, "y", -1)
 
-    right_m, right_p, left_zm, left_zp, left_z = after((right_m, right_p, left_zm, left_zp, left_z), ())
+    left_zm, left_zp, left_z = after((left_zm, left_zp, left_z), ())
     far_0 = ring(right_m[:4], "x", 1)
     far_1 = ring(right_p[4:], "x", -1)
     left_z2 = ring(left_z, "y", 2)

time: 144 us -> 142 us (0.986)
  the two profiles are of different devices: /device:TPU:15 before, /device:TPU:1 now
where the time goes in v6:
time: 142 us; the launch traced here: 141 us
  Pallas kernels  48.9 us (34%)
  waiting for transfers between devices  48 us (34%)
  starting transfers between devices  27 us (19%)
  between operations  13.7 us (10%)
  local copies, waits for them, and re-layouts  3.31 us (2%)
    pallas_call x2, Pallas kernels, add_terms(): pl.pallas_call(functools.partial(terms_kernel, layout, offsets, first), o...  48.9 us
    ppermute x6, waiting for transfers between devices, swap(): return lax.ppermute(value, axis, [(0, 1), (1, 0)])  17.6 us
    ppermute x9, starting transfers between devices, ring(): return lax.ppermute(value, axis, [(i, (i + shift) % 4) for i in range(4)])  9.73 us
    ppermute x9, waiting for transfers between devices, ring(): return lax.ppermute(value, axis, [(i, (i + shift) % 4) for i in range(4)])  9.54 us
    ppermute x1, waiting for transfers between devices, per_device(): east = lax.ppermute(sides[:, :1], WIDE, [(i + 1, i) for i in range(15)])  8.99 us
    ppermute x2, waiting for transfers between devices, edges(): return (lax.ppermute(last, axes, up), lax.ppermute(leading, axes, down))  7.09 us
    ppermute x2, starting transfers between devices, edges(): return (lax.ppermute(last, axes, up), lax.ppermute(leading, axes, down))  6.31 us
    ppermute x6, starting transfers between devices, swap(): return lax.ppermute(value, axis, [(0, 1), (1, 0)])  5.77 us
  transfers between devices with their start and end apart: 20, of which 8 were waited for; matrix products, arithmetic and copies ran while one was open for 2% of the time, Pallas kernels for 20%

profile of v6, /device:TPU:1, one launch (start us, length us, event | category | flops | bytes accessed | tf_op | source)
XLA Modules:
  0.0 141.1 jit_solution(6511223594400014762)
XLA Ops:
  6.5 0.7 all-gather.3.cloned.1.call-update
  7.3 1.1 fusion
  8.3 1.3 collective-permute-start.3
  9.6 5.0 %collective-permute-start.2 = (bf16[1,8,128,128]{3,2,1,0:T(8,128)(2,1)S(1)}, bf16[1,8,128,128]{3,2,1,0:T(8,128)(2,1)S(1)}, u32[]{:S(2)}, u32[]{:S(2)}) collective-permute-start(bf16[1,8,128,128]{3,2,1,0:T(8,128)(2,1)S(1)} %get-tuple-element.34), channel_id=1, source_target_pairs={{0,16},{16,32},{32,48},{48,64},{64,80},{80,96},{96,112},{1,17},{17... | collective-permute-start | bytes 786440 | tf_op jit(solution)/shard_map/ppermute | solution.py:201
  14.7 3.5 %collective-permute-start.1 = (bf16[8,2,128,128]{3,2,1,0:T(8,128)(2,1)}, bf16[8,2,128,128]{3,2,1,0:T(8,128)(2,1)S(1)}, u32[]{:S(2)}, u32[]{:S(2)}) collective-permute-start(bf16[8,2,128,128]{3,2,1,0:T(8,128)(2,1)} %param.6), channel_id=1, source_target_pairs={{0,2},{2,0},{1,3},{3,1},{4,6},{6,4},{5,7},{7,5},{8,10},{10,8},{9,1... | collective-permute-start | bytes 1572872 | tf_op jit(solution)/shard_map/ppermute | solution.py:191
  18.2 0.6 collective-permute-done.3.refs_6_
  18.7 6.5 %collective-permute-done.2.refs_5_ = bf16[1,8,128,128]{3,2,1,0:T(8,128)(2,1)S(1)} collective-permute-done((bf16[1,8,128,128]{3,2,1,0:T(8,128)(2,1)S(1)}, bf16[1,8,128,128]{3,2,1,0:T(8,128)(2,1)S(1)}, u32[]{:S(2)}, u32[]{:S(2)}) %collective-permute-start.2) | collective-permute-done | bytes 262176 | tf_op jit(solution)/shard_map/ppermute | solution.py:201
  25.2 1.5 %collective-permute-start.7 = (bf16[8,4,128,128]{3,2,1,0:T(8,128)(2,1)}, bf16[8,4,128,128]{3,2,1,0:T(8,128)(2,1)S(1)}, u32[]{:S(2)}, u32[]{:S(2)}) collective-permute-start(bf16[8,4,128,128]{3,2,1,0:T(8,128)(2,1)} %refs_9_.1), channel_id=1, source_target_pairs={{0,32},{32,64},{64,96},{96,0},{1,33},{33,65},{65,97},{97,1},{2,34}... | collective-permute-start | bytes 3145736 | tf_op jit(solution)/shard_map/ppermute | solution.py:187
  26.7 13.8 %collective-permute-done.1 = bf16[8,2,128,128]{3,2,1,0:T(8,128)(2,1)S(1)} collective-permute-done((bf16[8,2,128,128]{3,2,1,0:T(8,128)(2,1)}, bf16[8,2,128,128]{3,2,1,0:T(8,128)(2,1)S(1)}, u32[]{:S(2)}, u32[]{:S(2)}) %collective-permute-start.1) | collective-permute-done | bytes 524320 | tf_op jit(solution)/shard_map/ppermute | solution.py:191
  40.5 2.7 %collective-permute-start.5 = (bf16[8,2,128,128]{3,2,1,0:T(8,128)(2,1)S(1)}, bf16[8,2,128,128]{3,2,1,0:T(8,128)(2,1)S(1)}, u32[]{:S(2)}, u32[]{:S(2)}) collective-permute-start(bf16[8,2,128,128]{3,2,1,0:T(8,128)(2,1)S(1)} %collective-permute-done.1), channel_id=1, source_target_pairs={{0,12},{4,0},{8,4},{12,8},{1,13},{5,1},{9,5},{13,9},{2,14},{6,2},{... | collective-permute-start | bytes 1572872 | tf_op jit(solution)/shard_map/ppermute | solution.py:187
  43.3 1.1 slice.32
  44.5 9.5 %collective-permute-done.5 = bf16[8,2,128,128]{3,2,1,0:T(8,128)(2,1)S(1)} collective-permute-done((bf16[8,2,128,128]{3,2,1,0:T(8,128)(2,1)S(1)}, bf16[8,2,128,128]{3,2,1,0:T(8,128)(2,1)S(1)}, u32[]{:S(2)}, u32[]{:S(2)}) %collective-permute-start.5) | collective-permute-done | bytes 524320 | tf_op jit(solution)/shard_map/ppermute | solution.py:187
  54.0 3.2 %collective-permute-start.13 = (bf16[10,1,128,128]{3,2,1,0:T(8,128)(2,1)S(1)}, bf16[10,1,128,128]{3,2,1,0:T(8,128)(2,1)S(1)}, u32[]{:S(2)}, u32[]{:S(2)}) collective-permute-start(bf16[10,1,128,128]{3,2,1,0:T(8,128)(2,1)S(1)} %get-tuple-element.35), channel_id=1, source_target_pairs={{1,0},{2,1},{3,2},{4,3},{5,4},{6,5},{7,6},{8,7},{9,8},{10,9},{11,1... | collective-permute-start | bytes 983048 | tf_op jit(solution)/shard_map/ppermute | solution.py:231
  57.3 2.5 %collective-permute-start.11 = (bf16[8,2,128,128]{3,2,1,0:T(8,128)(2,1)S(1)}, bf16[8,2,128,128]{3,2,1,0:T(8,128)(2,1)S(1)}, u32[]{:S(2)}, u32[]{:S(2)}) collective-permute-start(bf16[8,2,128,128]{3,2,1,0:T(8,128)(2,1)S(1)} %collective-permute-done.1), channel_id=1, source_target_pairs={{0,8},{4,12},{8,0},{12,4},{1,9},{5,13},{9,1},{13,5},{2,10},{6,14},... | collective-permute-start | bytes 1572872 | tf_op jit(solution)/shard_map/ppermute | solution.py:187
  59.8 0.8 collective-permute-start.10
  60.7 0.8 collective-permute-start.8
  61.5 9.0 %collective-permute-done.13.refs_8_ = bf16[10,1,128,128]{3,2,1,0:T(8,128)(2,1)S(1)} collective-permute-done((bf16[10,1,128,128]{3,2,1,0:T(8,128)(2,1)S(1)}, bf16[10,1,128,128]{3,2,1,0:T(8,128)(2,1)S(1)}, u32[]{:S(2)}, u32[]{:S(2)}) %collective-permute-start.13) | collective-permute-done | bytes 327712 | tf_op jit(solution)/shard_map/ppermute | solution.py:231
  70.5 1.9 %collective-permute-start.12 = (bf16[10,1,128,128]{3,2,1,0:T(8,128)(2,1)S(1)}, bf16[10,1,128,128]{3,2,1,0:T(8,128)(2,1)S(1)}, u32[]{:S(2)}, u32[]{:S(2)}) collective-permute-start(bf16[10,1,128,128]{3,2,1,0:T(8,128)(2,1)S(1)} %get-tuple-element.36), channel_id=1, source_target_pairs={{0,1},{1,2},{2,3},{3,4},{4,5},{5,6},{6,7},{7,8},{8,9},{9,10},{10,1... | collective-permute-start | bytes 983048 | tf_op jit(solution)/shard_map/ppermute | solution.py:230
  72.4 4.0 %collective-permute-done.12.refs_7_ = bf16[10,1,128,128]{3,2,1,0:T(8,128)(2,1)S(1)} collective-permute-done((bf16[10,1,128,128]{3,2,1,0:T(8,128)(2,1)S(1)}, bf16[10,1,128,128]{3,2,1,0:T(8,128)(2,1)S(1)}, u32[]{:S(2)}, u32[]{:S(2)}) %collective-permute-start.12) | collective-permute-done | bytes 327712 | tf_op jit(solution)/shard_map/ppermute | solution.py:230
  76.5 0.8 copy-done.8
  77.3 0.2 copy-done.9
  77.4 0.3 pad_maximum_fusion.refs_2_
  77.7 0.1 collective-permute-start.14
  77.9 0.5 collective-permute-start
  78.3 1.1 collective-permute-start.16
  79.4 0.4 collective-permute-start.15
  79.8 0.9 collective-permute-start.17
  80.7 3.2 %collective-permute-done.14.refs_3_ = bf16[4,8,2,128,128]{4,3,2,1,0:T(8,128)(2,1)} collective-permute-done((bf16[4,8,2,128,128]{4,3,2,1,0:T(8,128)(2,1)S(1)}, bf16[4,8,2,128,128]{4,3,2,1,0:T(8,128)(2,1)}, u32[]{:S(2)}, u32[]{:S(2)}) %collective-permute-start.14) | collective-permute-done | bytes 2097184 | tf_op jit(solution)/shard_map/ppermute | solution.py:191
  83.9 0.9 collective-permute-start.18
  84.7 0.6 collective-permute-done.refs_1_
  85.3 28.8 %shard_map.64.refs_13_ = f32[8,8,128,128]{3,2,1,0:T(8,128)} custom-call(s32[1]{0:T(128)} %bitcast.place, s32[32]{0:T(128)} %ls.3, s32[32]{0:T(128)} %rs.3, s32[8,8,32]{2,1,0:T(8,128)} %act.3, bf16[4,8,2,128,128]{4,3,2,1,0:T(8,128)(2,1)} %bitcast.7, bf16[4,8,2,128,128]{4,3,2,1,0:T(8,128)(2,1)} %collective-permute-done.refs_1_, ...), custom_call_target="tpu_custom_call" | custom-call | flops 1 | bytes 1 | tf_op jit(solution)/shard_map/pallas_call | solution.py:158
  114.2 20.1 %shard_map.65 = f32[8,8,128,128]{3,2,1,0:T(8,128)} custom-call(s32[1]{0:T(128)} %bitcast.place, s32[32]{0:T(128)} %ls.3, s32[32]{0:T(128)} %rs.3, s32[8,8,32]{2,1,0:T(8,128)} %act.3, bf16[4,8,2,128,128]{4,3,2,1,0:T(8,128)(2,1)} %bitcast.8, bf16[4,8,2,128,128]{4,3,2,1,0:T(8,128)(2,1)} %collective-permute-done.refs_1_, ...), custom_call_target="tpu_custom_call", output_to_operand_aliasing={{}: (17, {})} | custom-call | flops 1 | bytes 1 | tf_op jit(solution)/shard_map/pallas_call | solution.py:158
  (40 shorter events, 0.3 us)
Async XLA Ops:
  6.5 71.3 %all-gather.3.cloned.1.call-start = ((), (), s32[]{:S(2)}) async-start(), calls=%async_computation | async-start | bytes 2621440 | tf_op jit(solution)/shard_map/all_gather | solution.py:212
  8.3 10.4 %collective-permute-start.3 = (bf16[1,8,128,128]{3,2,1,0:T(8,128)(2,1)S(1)}, bf16[1,8,128,128]{3,2,1,0:T(8,128)(2,1)S(1)}, u32[]{:S(2)}, u32[]{:S(2)}) collective-permute-start(bf16[1,8,128,128]{3,2,1,0:T(8,128)(2,1)S(1)} %get-tuple-element.33), channel_id=1, source_target_pairs={{16,0},{32,16},{48,32},{64,48},{80,64},{96,80},{112,96},{17,1},{33... | collective-permute-start | bytes 786440 | tf_op jit(solution)/shard_map/ppermute | solution.py:201
  9.6 15.6 %collective-permute-start.2 = (bf16[1,8,128,128]{3,2,1,0:T(8,128)(2,1)S(1)}, bf16[1,8,128,128]{3,2,1,0:T(8,128)(2,1)S(1)}, u32[]{:S(2)}, u32[]{:S(2)}) collective-permute-start(bf16[1,8,128,128]{3,2,1,0:T(8,128)(2,1)S(1)} %get-tuple-element.34), channel_id=1, source_target_pairs={{0,16},{16,32},{32,48},{48,64},{64,80},{80,96},{96,112},{1,17},{17... | collective-permute-start | bytes 786440 | tf_op jit(solution)/shard_map/ppermute | solution.py:201
  14.7 25.9 %collective-permute-start.1 = (bf16[8,2,128,128]{3,2,1,0:T(8,128)(2,1)}, bf16[8,2,128,128]{3,2,1,0:T(8,128)(2,1)S(1)}, u32[]{:S(2)}, u32[]{:S(2)}) collective-permute-start(bf16[8,2,128,128]{3,2,1,0:T(8,128)(2,1)} %param.6), channel_id=1, source_target_pairs={{0,2},{2,0},{1,3},{3,1},{4,6},{6,4},{5,7},{7,5},{8,10},{10,8},{9,1... | collective-permute-start | bytes 1572872 | tf_op jit(solution)/shard_map/ppermute | solution.py:191
  18.7 41.1 %copy-start.3 = (bf16[1,8,128,128]{3,2,1,0:T(8,128)(2,1)}, bf16[1,8,128,128]{3,2,1,0:T(8,128)(2,1)S(1)}, u32[]{:S(2)}) copy-start(bf16[1,8,128,128]{3,2,1,0:T(8,128)(2,1)S(1)} %collective-permute-done.3.refs_6_) | copy-start | bytes 786436
  25.2 19.1 %copy-start.4 = (bf16[1,8,128,128]{3,2,1,0:T(8,128)(2,1)}, bf16[1,8,128,128]{3,2,1,0:T(8,128)(2,1)S(1)}, u32[]{:S(2)}) copy-start(bf16[1,8,128,128]{3,2,1,0:T(8,128)(2,1)S(1)} %collective-permute-done.2.refs_5_) | copy-start | bytes 786436
  25.2 34.5 %collective-permute-start.9 = (bf16[8,4,128,128]{3,2,1,0:T(8,128)(2,1)}, bf16[8,4,128,128]{3,2,1,0:T(8,128)(2,1)S(1)}, u32[]{:S(2)}, u32[]{:S(2)}) collective-permute-start(bf16[8,4,128,128]{3,2,1,0:T(8,128)(2,1)} %refs_9_.1), channel_id=1, source_target_pairs={{0,96},{32,0},{64,32},{96,64},{1,97},{33,1},{65,33},{97,65},{2,98}... | collective-permute-start | bytes 3145736 | tf_op jit(solution)/shard_map/ppermute | solution.py:187
  25.2 35.4 %collective-permute-start.7 = (bf16[8,4,128,128]{3,2,1,0:T(8,128)(2,1)}, bf16[8,4,128,128]{3,2,1,0:T(8,128)(2,1)S(1)}, u32[]{:S(2)}, u32[]{:S(2)}) collective-permute-start(bf16[8,4,128,128]{3,2,1,0:T(8,128)(2,1)} %refs_9_.1), channel_id=1, source_target_pairs={{0,32},{32,64},{64,96},{96,0},{1,33},{33,65},{65,97},{97,1},{2,34}... | collective-permute-start | bytes 3145736 | tf_op jit(solution)/shard_map/ppermute | solution.py:187
  40.5 13.5 %collective-permute-start.5 = (bf16[8,2,128,128]{3,2,1,0:T(8,128)(2,1)S(1)}, bf16[8,2,128,128]{3,2,1,0:T(8,128)(2,1)S(1)}, u32[]{:S(2)}, u32[]{:S(2)}) collective-permute-start(bf16[8,2,128,128]{3,2,1,0:T(8,128)(2,1)S(1)} %collective-permute-done.1), channel_id=1, source_target_pairs={{0,12},{4,0},{8,4},{12,8},{1,13},{5,1},{9,5},{13,9},{2,14},{6,2},{... | collective-permute-start | bytes 1572872 | tf_op jit(solution)/shard_map/ppermute | solution.py:187
  43.2 14.0 %collective-permute-start.4 = (bf16[8,2,128,128]{3,2,1,0:T(8,128)(2,1)S(1)}, bf16[8,2,128,128]{3,2,1,0:T(8,128)(2,1)S(1)}, u32[]{:S(2)}, u32[]{:S(2)}) collective-permute-start(bf16[8,2,128,128]{3,2,1,0:T(8,128)(2,1)S(1)} %collective-permute-done.1), channel_id=1, source_target_pairs={{0,4},{4,8},{8,12},{12,0},{1,5},{5,9},{9,13},{13,1},{2,6},{6,10},{... | collective-permute-start | bytes 1572872 | tf_op jit(solution)/shard_map/ppermute | solution.py:187
  43.3 33.1 %collective-permute-start.6 = (bf16[8,4,128,128]{3,2,1,0:T(8,128)(2,1)}, bf16[8,4,128,128]{3,2,1,0:T(8,128)(2,1)S(1)}, u32[]{:S(2)}, u32[]{:S(2)}) collective-permute-start(bf16[8,4,128,128]{3,2,1,0:T(8,128)(2,1)} %refs_9_.1), channel_id=1, source_target_pairs={{0,16},{16,0},{1,17},{17,1},{2,18},{18,2},{3,19},{19,3},{4,20},{20... | collective-permute-start | bytes 3145736 | tf_op jit(solution)/shard_map/ppermute | solution.py:191
  54.0 16.4 %collective-permute-start.13 = (bf16[10,1,128,128]{3,2,1,0:T(8,128)(2,1)S(1)}, bf16[10,1,128,128]{3,2,1,0:T(8,128)(2,1)S(1)}, u32[]{:S(2)}, u32[]{:S(2)}) collective-permute-start(bf16[10,1,128,128]{3,2,1,0:T(8,128)(2,1)S(1)} %get-tuple-element.35), channel_id=1, source_target_pairs={{1,0},{2,1},{3,2},{4,3},{5,4},{6,5},{7,6},{8,7},{9,8},{10,9},{11,1... | collective-permute-start | bytes 983048 | tf_op jit(solution)/shard_map/ppermute | solution.py:231
  57.3 19.1 %collective-permute-start.11 = (bf16[8,2,128,128]{3,2,1,0:T(8,128)(2,1)S(1)}, bf16[8,2,128,128]{3,2,1,0:T(8,128)(2,1)S(1)}, u32[]{:S(2)}, u32[]{:S(2)}) collective-permute-start(bf16[8,2,128,128]{3,2,1,0:T(8,128)(2,1)S(1)} %collective-permute-done.1), channel_id=1, source_target_pairs={{0,8},{4,12},{8,0},{12,4},{1,9},{5,13},{9,1},{13,5},{2,10},{6,14},... | collective-permute-start | bytes 1572872 | tf_op jit(solution)/shard_map/ppermute | solution.py:187
  59.8 17.9 %copy-start.1 = (bf16[8,4,128,128]{3,2,1,0:T(8,128)(2,1)}, bf16[8,4,128,128]{3,2,1,0:T(8,128)(2,1)S(1)}, u32[]{:S(2)}) copy-start(bf16[8,4,128,128]{3,2,1,0:T(8,128)(2,1)S(1)} %collective-permute-done.9.refs_12_) | copy-start | bytes 3145732
  59.8 16.6 %collective-permute-start.10 = (bf16[4,4,128,128]{3,2,1,0:T(8,128)(2,1)S(1)}, bf16[4,4,128,128]{3,2,1,0:T(8,128)(2,1)S(1)}, u32[]{:S(2)}, u32[]{:S(2)}) collective-permute-start(bf16[4,4,128,128]{3,2,1,0:T(8,128)(2,1)S(1)} %slice.37), channel_id=1, source_target_pairs={{0,96},{32,0},{64,32},{96,64},{1,97},{33,1},{65,33},{97,65},{2,98}... | collective-permute-start | bytes 1572872 | tf_op jit(solution)/shard_map/ppermute | solution.py:187
  60.7 15.8 %copy-start.2 = (bf16[8,4,128,128]{3,2,1,0:T(8,128)(2,1)}, bf16[8,4,128,128]{3,2,1,0:T(8,128)(2,1)S(1)}, u32[]{:S(2)}) copy-start(bf16[8,4,128,128]{3,2,1,0:T(8,128)(2,1)S(1)} %collective-permute-done.7.refs_11_) | copy-start | bytes 3145732
  60.7 15.7 %collective-permute-start.8 = (bf16[4,4,128,128]{3,2,1,0:T(8,128)(2,1)S(1)}, bf16[4,4,128,128]{3,2,1,0:T(8,128)(2,1)S(1)}, u32[]{:S(2)}, u32[]{:S(2)}) collective-permute-start(bf16[4,4,128,128]{3,2,1,0:T(8,128)(2,1)S(1)} %slice.36), channel_id=1, source_target_pairs={{0,32},{32,64},{64,96},{96,0},{1,33},{33,65},{65,97},{97,1},{2,34}... | collective-permute-start | bytes 1572872 | tf_op jit(solution)/shard_map/ppermute | solution.py:187
  70.5 6.0 %copy-start.5 = (bf16[10,1,128,128]{3,2,1,0:T(8,128)(2,1)}, bf16[10,1,128,128]{3,2,1,0:T(8,128)(2,1)S(1)}, u32[]{:S(2)}) copy-start(bf16[10,1,128,128]{3,2,1,0:T(8,128)(2,1)S(1)} %collective-permute-done.13.refs_8_) | copy-start | bytes 983044
  70.5 5.9 %collective-permute-start.12 = (bf16[10,1,128,128]{3,2,1,0:T(8,128)(2,1)S(1)}, bf16[10,1,128,128]{3,2,1,0:T(8,128)(2,1)S(1)}, u32[]{:S(2)}, u32[]{:S(2)}) collective-permute-start(bf16[10,1,128,128]{3,2,1,0:T(8,128)(2,1)S(1)} %get-tuple-element.36), channel_id=1, source_target_pairs={{0,1},{1,2},{2,3},{3,4},{4,5},{5,6},{6,7},{7,8},{8,9},{9,10},{10,1... | collective-permute-start | bytes 983048 | tf_op jit(solution)/shard_map/ppermute | solution.py:230
  76.4 1.3 copy-start.6
  76.4 8.9 %copy-start.7 = (bf16[8,4,128,128]{3,2,1,0:T(8,128)(2,1)}, bf16[8,4,128,128]{3,2,1,0:T(8,128)(2,1)S(1)}, u32[]{:S(2)}) copy-start(bf16[8,4,128,128]{3,2,1,0:T(8,128)(2,1)S(1)} %collective-permute-done.6.refs_10_) | copy-start | bytes 3145732
  76.4 0.9 copy-start.8
  76.4 1.0 copy-start.9
  77.7 7.6 %copy-start = (bf16[4,8,2,128,128]{4,3,2,1,0:T(8,128)(2,1)}, bf16[4,8,2,128,128]{4,3,2,1,0:T(8,128)(2,1)S(1)}, u32[]{:S(2)}) copy-start(bf16[4,8,2,128,128]{4,3,2,1,0:T(8,128)(2,1)S(1)} %pad_maximum_fusion.refs_2_) | copy-start | bytes 6291460
  77.7 6.1 %collective-permute-start.14 = (bf16[4,8,2,128,128]{4,3,2,1,0:T(8,128)(2,1)S(1)}, bf16[4,8,2,128,128]{4,3,2,1,0:T(8,128)(2,1)}, u32[]{:S(2)}, u32[]{:S(2)}) collective-permute-start(bf16[4,8,2,128,128]{4,3,2,1,0:T(8,128)(2,1)S(1)} %pad_maximum_fusion.refs_2_), channel_id=1, source_target_pairs={{0,1},{1,0},{2,3},{3,2},{4,5},{5,4},{6,7},{7,6},{8,9},{9,8},{10,11... | collective-permute-start | bytes 6291464 | tf_op jit(solution)/shard_map/ppermute | solution.py:191
  77.9 7.5 %collective-permute-start = (bf16[4,8,2,128,128]{4,3,2,1,0:T(8,128)(2,1)}, bf16[4,8,2,128,128]{4,3,2,1,0:T(8,128)(2,1)}, u32[]{:S(2)}, u32[]{:S(2)}) collective-permute-start(bf16[4,8,2,128,128]{4,3,2,1,0:T(8,128)(2,1)} %bitcast.6), channel_id=1, source_target_pairs={{0,1},{1,0},{2,3},{3,2},{4,5},{5,4},{6,7},{7,6},{8,9},{9,8},{10,11... | collective-permute-start | bytes 6291464 | tf_op jit(solution)/shard_map/ppermute | solution.py:191
  78.3 35.8 %collective-permute-start.16 = (bf16[8,4,128,128]{3,2,1,0:T(8,128)(2,1)S(1)}, bf16[8,4,128,128]{3,2,1,0:T(8,128)(2,1)}, u32[]{:S(2)}, u32[]{:S(2)}) collective-permute-start(bf16[8,4,128,128]{3,2,1,0:T(8,128)(2,1)S(1)} %collective-permute-done.6.refs_10_), channel_id=1, source_target_pairs={{0,96},{32,0},{64,32},{96,64},{1,97},{33,1},{65,33},{97,65},{2,98}... | collective-permute-start | bytes 3145736 | tf_op jit(solution)/shard_map/ppermute | solution.py:187
  79.4 34.8 %collective-permute-start.15 = (bf16[8,4,128,128]{3,2,1,0:T(8,128)(2,1)S(1)}, bf16[8,4,128,128]{3,2,1,0:T(8,128)(2,1)}, u32[]{:S(2)}, u32[]{:S(2)}) collective-permute-start(bf16[8,4,128,128]{3,2,1,0:T(8,128)(2,1)S(1)} %collective-permute-done.6.refs_10_), channel_id=1, source_target_pairs={{0,32},{32,64},{64,96},{96,0},{1,33},{33,65},{65,97},{97,1},{2,34}... | collective-permute-start | bytes 3145736 | tf_op jit(solution)/shard_map/ppermute | solution.py:187
  79.8 34.3 %collective-permute-start.17 = (bf16[4,4,128,128]{3,2,1,0:T(8,128)(2,1)}, bf16[4,4,128,128]{3,2,1,0:T(8,128)(2,1)}, u32[]{:S(2)}, u32[]{:S(2)}) collective-permute-start(bf16[4,4,128,128]{3,2,1,0:T(8,128)(2,1)} %copy-done.9), channel_id=1, source_target_pairs={{0,16},{16,0},{1,17},{17,1},{2,18},{18,2},{3,19},{19,3},{4,20},{20... | collective-permute-start | bytes 1572872 | tf_op jit(solution)/shard_map/ppermute | solution.py:191
  83.9 30.3 %collective-permute-start.18 = (bf16[4,4,128,128]{3,2,1,0:T(8,128)(2,1)}, bf16[4,4,128,128]{3,2,1,0:T(8,128)(2,1)}, u32[]{:S(2)}, u32[]{:S(2)}) collective-permute-start(bf16[4,4,128,128]{3,2,1,0:T(8,128)(2,1)} %copy-done.8), channel_id=1, source_target_pairs={{0,16},{16,0},{1,17},{17,1},{2,18},{18,2},{3,19},{19,3},{4,20},{20... | collective-permute-start | bytes 1572872 | tf_op jit(solution)/shard_map/ppermute | solution.py:191
Sparse Core Ops, SparseCore 0:
  9.0 34.0 all-gather.2

commit v7 on v6

--- a/solution.py
+++ b/solution.py
@@ -177,7 +177,7 @@
         ),
         input_output_aliases={} if first else {4 + len(operands) - 1: 0},
         compiler_params=pltpu.CompilerParams(
-            vmem_limit_bytes=56 << 20, dimension_semantics=("arbitrary",)
+            vmem_limit_bytes=32 << 20, dimension_semantics=("arbitrary",)
         ),
         cost_estimate=pl.CostEstimate(flops=1, bytes_accessed=1, transcendentals=0),
     )(place, ls, rs, act, *operands)

time: 142 us -> 152 us (1.070)
  local copies, waits for them, and re-layouts: 3.31 us -> 16.9 us
  Pallas kernels: 48.9 us -> 45.7 us
    unnamed x20 -> x40, local copies, waits for them, and re-layouts: 1.02 us -> 14.6 us
    pallas_call x2, Pallas kernels: 48.9 us -> 45.7 us  [add_terms(): pl.pallas_call(functools.partial(terms_kernel, layout, offsets, first), o...]
  transfers between devices with their start and end apart: 20 -> 20, of which waited for: 8 -> 8; matrix products, arithmetic and copies ran while one was open for 2% -> 2% of each run, Pallas kernels for 20% -> 18%
where the time goes in v7:
time: 152 us; the launch traced here: 151 us
  waiting for transfers between devices  48 us (32%)
  Pallas kernels  45.7 us (30%)
  starting transfers between devices  27 us (18%)
  local copies, waits for them, and re-layouts  16.9 us (11%)
  between operations  13.7 us (9%)
    pallas_call x2, Pallas kernels, add_terms(): pl.pallas_call(functools.partial(terms_kernel, layout, offsets, first), o...  45.7 us
    ppermute x6, waiting for transfers between devices, swap(): return lax.ppermute(value, axis, [(0, 1), (1, 0)])  17.6 us
    unnamed x40, local copies, waits for them, and re-layouts  14.6 us
    ppermute x9, starting transfers between devices, ring(): return lax.ppermute(value, axis, [(i, (i + shift) % 4) for i in range(4)])  9.73 us
    ppermute x9, waiting for transfers between devices, ring(): return lax.ppermute(value, axis, [(i, (i + shift) % 4) for i in range(4)])  9.53 us
    ppermute x1, waiting for transfers between devices, per_device(): east = lax.ppermute(sides[:, :1], WIDE, [(i + 1, i) for i in range(15)])  8.99 us
    ppermute x2, waiting for transfers between devices, edges(): return (lax.ppermute(last, axes, up), lax.ppermute(leading, axes, down))  7.09 us
    ppermute x2, starting transfers between devices, edges(): return (lax.ppermute(last, axes, up), lax.ppermute(leading, axes, down))  6.31 us
  transfers between devices with their start and end apart: 20, of which 8 were waited for; matrix products, arithmetic and copies ran while one was open for 2% of the time, Pallas kernels for 18%

profile of v7, /device:TPU:1, one launch (start us, length us, event | category | flops | bytes accessed | tf_op | source)
XLA Modules:
  0.0 151.5 jit_solution(15869309891308471309)
XLA Ops:
  7.3 1.1 fusion
  8.3 1.3 collective-permute-start.3
  9.6 5.0 %collective-permute-start.2 = (bf16[1,8,128,128]{3,2,1,0:T(8,128)(2,1)S(1)}, bf16[1,8,128,128]{3,2,1,0:T(8,128)(2,1)S(1)}, u32[]{:S(2)}, u32[]{:S(2)}) collective-permute-start(bf16[1,8,128,128]{3,2,1,0:T(8,128)(2,1)S(1)} %get-tuple-element.34), channel_id=1, source_target_pairs={{0,16},{16,32},{32,48},{48,64},{64,80},{80,96},{96,112},{1,17},{17... | collective-permute-start | bytes 786440 | tf_op jit(solution)/shard_map/ppermute | solution.py:201
  14.7 3.5 %collective-permute-start.1 = (bf16[8,2,128,128]{3,2,1,0:T(8,128)(2,1)}, bf16[8,2,128,128]{3,2,1,0:T(8,128)(2,1)S(1)}, u32[]{:S(2)}, u32[]{:S(2)}) collective-permute-start(bf16[8,2,128,128]{3,2,1,0:T(8,128)(2,1)} %param.6), channel_id=1, source_target_pairs={{0,2},{2,0},{1,3},{3,1},{4,6},{6,4},{5,7},{7,5},{8,10},{10,8},{9,1... | collective-permute-start | bytes 1572872 | tf_op jit(solution)/shard_map/ppermute | solution.py:191
  18.7 6.5 %collective-permute-done.2.refs_5_ = bf16[1,8,128,128]{3,2,1,0:T(8,128)(2,1)S(1)} collective-permute-done((bf16[1,8,128,128]{3,2,1,0:T(8,128)(2,1)S(1)}, bf16[1,8,128,128]{3,2,1,0:T(8,128)(2,1)S(1)}, u32[]{:S(2)}, u32[]{:S(2)}) %collective-permute-start.2) | collective-permute-done | bytes 262176 | tf_op jit(solution)/shard_map/ppermute | solution.py:201
  25.2 1.5 collective-permute-start.7
  26.7 13.8 %collective-permute-done.1 = bf16[8,2,128,128]{3,2,1,0:T(8,128)(2,1)S(1)} collective-permute-done((bf16[8,2,128,128]{3,2,1,0:T(8,128)(2,1)}, bf16[8,2,128,128]{3,2,1,0:T(8,128)(2,1)S(1)}, u32[]{:S(2)}, u32[]{:S(2)}) %collective-permute-start.1) | collective-permute-done | bytes 524320 | tf_op jit(solution)/shard_map/ppermute | solution.py:191
  40.5 2.7 %collective-permute-start.5 = (bf16[8,2,128,128]{3,2,1,0:T(8,128)(2,1)S(1)}, bf16[8,2,128,128]{3,2,1,0:T(8,128)(2,1)S(1)}, u32[]{:S(2)}, u32[]{:S(2)}) collective-permute-start(bf16[8,2,128,128]{3,2,1,0:T(8,128)(2,1)S(1)} %collective-permute-done.1), channel_id=1, source_target_pairs={{0,12},{4,0},{8,4},{12,8},{1,13},{5,1},{9,5},{13,9},{2,14},{6,2},{... | collective-permute-start | bytes 1572872 | tf_op jit(solution)/shard_map/ppermute | solution.py:187
  43.3 1.1 slice.32
  44.5 9.5 %collective-permute-done.5 = bf16[8,2,128,128]{3,2,1,0:T(8,128)(2,1)S(1)} collective-permute-done((bf16[8,2,128,128]{3,2,1,0:T(8,128)(2,1)S(1)}, bf16[8,2,128,128]{3,2,1,0:T(8,128)(2,1)S(1)}, u32[]{:S(2)}, u32[]{:S(2)}) %collective-permute-start.5) | collective-permute-done | bytes 524320 | tf_op jit(solution)/shard_map/ppermute | solution.py:187
  54.0 3.2 %collective-permute-start.13 = (bf16[10,1,128,128]{3,2,1,0:T(8,128)(2,1)S(1)}, bf16[10,1,128,128]{3,2,1,0:T(8,128)(2,1)S(1)}, u32[]{:S(2)}, u32[]{:S(2)}) collective-permute-start(bf16[10,1,128,128]{3,2,1,0:T(8,128)(2,1)S(1)} %get-tuple-element.35), channel_id=1, source_target_pairs={{1,0},{2,1},{3,2},{4,3},{5,4},{6,5},{7,6},{8,7},{9,8},{10,9},{11,1... | collective-permute-start | bytes 983048 | tf_op jit(solution)/shard_map/ppermute | solution.py:231
  57.3 2.5 %collective-permute-start.11 = (bf16[8,2,128,128]{3,2,1,0:T(8,128)(2,1)S(1)}, bf16[8,2,128,128]{3,2,1,0:T(8,128)(2,1)S(1)}, u32[]{:S(2)}, u32[]{:S(2)}) collective-permute-start(bf16[8,2,128,128]{3,2,1,0:T(8,128)(2,1)S(1)} %collective-permute-done.1), channel_id=1, source_target_pairs={{0,8},{4,12},{8,0},{12,4},{1,9},{5,13},{9,1},{13,5},{2,10},{6,14},... | collective-permute-start | bytes 1572872 | tf_op jit(solution)/shard_map/ppermute | solution.py:187
  61.5 9.0 %collective-permute-done.13.refs_8_ = bf16[10,1,128,128]{3,2,1,0:T(8,128)(2,1)S(1)} collective-permute-done((bf16[10,1,128,128]{3,2,1,0:T(8,128)(2,1)S(1)}, bf16[10,1,128,128]{3,2,1,0:T(8,128)(2,1)S(1)}, u32[]{:S(2)}, u32[]{:S(2)}) %collective-permute-start.13) | collective-permute-done | bytes 327712 | tf_op jit(solution)/shard_map/ppermute | solution.py:231
  71.2 1.9 %collective-permute-start.12 = (bf16[10,1,128,128]{3,2,1,0:T(8,128)(2,1)S(1)}, bf16[10,1,128,128]{3,2,1,0:T(8,128)(2,1)S(1)}, u32[]{:S(2)}, u32[]{:S(2)}) collective-permute-start(bf16[10,1,128,128]{3,2,1,0:T(8,128)(2,1)S(1)} %get-tuple-element.36), channel_id=1, source_target_pairs={{0,1},{1,2},{2,3},{3,4},{4,5},{5,6},{6,7},{7,8},{8,9},{9,10},{10,1... | collective-permute-start | bytes 983048 | tf_op jit(solution)/shard_map/ppermute | solution.py:230
  73.1 4.0 %collective-permute-done.12.refs_7_ = bf16[10,1,128,128]{3,2,1,0:T(8,128)(2,1)S(1)} collective-permute-done((bf16[10,1,128,128]{3,2,1,0:T(8,128)(2,1)S(1)}, bf16[10,1,128,128]{3,2,1,0:T(8,128)(2,1)S(1)}, u32[]{:S(2)}, u32[]{:S(2)}) %collective-permute-start.12) | collective-permute-done | bytes 327712 | tf_op jit(solution)/shard_map/ppermute | solution.py:230
  77.9 0.9 copy-done.11
  80.1 1.1 collective-permute-start.16
  81.5 0.9 collective-permute-start.17
  82.4 3.2 %collective-permute-done.14.refs_3_ = bf16[4,8,2,128,128]{4,3,2,1,0:T(8,128)(2,1)} collective-permute-done((bf16[4,8,2,128,128]{4,3,2,1,0:T(8,128)(2,1)S(1)}, bf16[4,8,2,128,128]{4,3,2,1,0:T(8,128)(2,1)}, u32[]{:S(2)}, u32[]{:S(2)}) %collective-permute-start.14) | collective-permute-done | bytes 2097184 | tf_op jit(solution)/shard_map/ppermute | solution.py:191
  85.6 0.9 collective-permute-start.18
  87.1 1.6 %copy-done = bf16[8,8,128,128]{3,2,1,0:T(8,128)(2,1)S(1)} copy-done((bf16[8,8,128,128]{3,2,1,0:T(8,128)(2,1)S(1)}, bf16[8,8,128,128]{3,2,1,0:T(8,128)(2,1)}, u32[]{:S(2)}) %copy-start) | copy-done | bytes 2097176
  88.7 1.6 %copy-done.1 = bf16[32,2,128,128]{3,2,1,0:T(8,128)(2,1)S(1)} copy-done((bf16[32,2,128,128]{3,2,1,0:T(8,128)(2,1)S(1)}, bf16[32,2,128,128]{3,2,1,0:T(8,128)(2,1)}, u32[]{:S(2)}) %copy-start.1) | copy-done | bytes 2097176
  90.2 1.2 copy-done.3
  91.5 0.9 copy-done.5
  92.4 1.0 copy-done.7
  93.4 1.0 copy-done.9
  94.4 1.2 copy-done.10
  95.6 1.2 copy-done.12
  96.8 1.0 copy-done.14
  97.9 1.0 copy-done.16
  98.9 27.2 %shard_map.64.refs_13_ = f32[8,8,128,128]{3,2,1,0:T(8,128)} custom-call(s32[1]{0:T(128)} %bitcast.place, s32[32]{0:T(128)S(1)} %copy-done.18, s32[32]{0:T(128)S(1)} %copy-done.19, s32[8,8,32]{2,1,0:T(8,128)S(1)} %copy-done.17, bf16[4,8,2,128,128]{4,3,2,1,0:T(8,128)(2,1)S(1)} %bitcast.7, bf16[4,8,2,128,128]{4,3,2,1,0:T(8,128)(2,1)} %collective-permute-done.refs_1_, ...), custom_call_target="tpu_custom_call" | custom-call | flops 1 | bytes 1 | tf_op jit(solution)/shard_map/pallas_call | solution.py:158
  126.2 18.4 %shard_map.65 = f32[8,8,128,128]{3,2,1,0:T(8,128)} custom-call(s32[1]{0:T(128)} %bitcast.place, s32[32]{0:T(128)S(1)} %copy-done.18, s32[32]{0:T(128)S(1)} %copy-done.19, s32[8,8,32]{2,1,0:T(8,128)S(1)} %copy-done.17, bf16[4,8,2,128,128]{4,3,2,1,0:T(8,128)(2,1)S(1)} %bitcast.8, ...), custom_call_target="tpu_custom_call", output_to_operand_aliasing={{}: (17, {})} | custom-call | flops 1 | bytes 1 | tf_op jit(solution)/shard_map/pallas_call | solution.py:158
  (60 shorter events, 6.8 us)
Async XLA Ops:
  6.5 73.0 %all-gather.3.cloned.1.call-start = ((), (), s32[]{:S(2)}) async-start(), calls=%async_computation | async-start | bytes 2621440 | tf_op jit(solution)/shard_map/all_gather | solution.py:212
  8.3 10.4 %collective-permute-start.3 = (bf16[1,8,128,128]{3,2,1,0:T(8,128)(2,1)S(1)}, bf16[1,8,128,128]{3,2,1,0:T(8,128)(2,1)S(1)}, u32[]{:S(2)}, u32[]{:S(2)}) collective-permute-start(bf16[1,8,128,128]{3,2,1,0:T(8,128)(2,1)S(1)} %get-tuple-element.33), channel_id=1, source_target_pairs={{16,0},{32,16},{48,32},{64,48},{80,64},{96,80},{112,96},{17,1},{33... | collective-permute-start | bytes 786440 | tf_op jit(solution)/shard_map/ppermute | solution.py:201
  9.6 15.6 %collective-permute-start.2 = (bf16[1,8,128,128]{3,2,1,0:T(8,128)(2,1)S(1)}, bf16[1,8,128,128]{3,2,1,0:T(8,128)(2,1)S(1)}, u32[]{:S(2)}, u32[]{:S(2)}) collective-permute-start(bf16[1,8,128,128]{3,2,1,0:T(8,128)(2,1)S(1)} %get-tuple-element.34), channel_id=1, source_target_pairs={{0,16},{16,32},{32,48},{48,64},{64,80},{80,96},{96,112},{1,17},{17... | collective-permute-start | bytes 786440 | tf_op jit(solution)/shard_map/ppermute | solution.py:201
  14.7 25.9 %collective-permute-start.1 = (bf16[8,2,128,128]{3,2,1,0:T(8,128)(2,1)}, bf16[8,2,128,128]{3,2,1,0:T(8,128)(2,1)S(1)}, u32[]{:S(2)}, u32[]{:S(2)}) collective-permute-start(bf16[8,2,128,128]{3,2,1,0:T(8,128)(2,1)} %param.6), channel_id=1, source_target_pairs={{0,2},{2,0},{1,3},{3,1},{4,6},{6,4},{5,7},{7,5},{8,10},{10,8},{9,1... | collective-permute-start | bytes 1572872 | tf_op jit(solution)/shard_map/ppermute | solution.py:191
  25.2 19.1 %copy-start.4 = (bf16[1,8,128,128]{3,2,1,0:T(8,128)(2,1)}, bf16[1,8,128,128]{3,2,1,0:T(8,128)(2,1)S(1)}, u32[]{:S(2)}) copy-start(bf16[1,8,128,128]{3,2,1,0:T(8,128)(2,1)S(1)} %collective-permute-done.2.refs_5_) | copy-start | bytes 786436
  25.2 34.5 %collective-permute-start.9 = (bf16[8,4,128,128]{3,2,1,0:T(8,128)(2,1)}, bf16[8,4,128,128]{3,2,1,0:T(8,128)(2,1)S(1)}, u32[]{:S(2)}, u32[]{:S(2)}) collective-permute-start(bf16[8,4,128,128]{3,2,1,0:T(8,128)(2,1)} %refs_9_.1), channel_id=1, source_target_pairs={{0,96},{32,0},{64,32},{96,64},{1,97},{33,1},{65,33},{97,65},{2,98}... | collective-permute-start | bytes 3145736 | tf_op jit(solution)/shard_map/ppermute | solution.py:187
  25.2 35.4 %collective-permute-start.7 = (bf16[8,4,128,128]{3,2,1,0:T(8,128)(2,1)}, bf16[8,4,128,128]{3,2,1,0:T(8,128)(2,1)S(1)}, u32[]{:S(2)}, u32[]{:S(2)}) collective-permute-start(bf16[8,4,128,128]{3,2,1,0:T(8,128)(2,1)} %refs_9_.1), channel_id=1, source_target_pairs={{0,32},{32,64},{64,96},{96,0},{1,33},{33,65},{65,97},{97,1},{2,34}... | collective-permute-start | bytes 3145736 | tf_op jit(solution)/shard_map/ppermute | solution.py:187
  40.5 13.5 %collective-permute-start.5 = (bf16[8,2,128,128]{3,2,1,0:T(8,128)(2,1)S(1)}, bf16[8,2,128,128]{3,2,1,0:T(8,128)(2,1)S(1)}, u32[]{:S(2)}, u32[]{:S(2)}) collective-permute-start(bf16[8,2,128,128]{3,2,1,0:T(8,128)(2,1)S(1)} %collective-permute-done.1), channel_id=1, source_target_pairs={{0,12},{4,0},{8,4},{12,8},{1,13},{5,1},{9,5},{13,9},{2,14},{6,2},{... | collective-permute-start | bytes 1572872 | tf_op jit(solution)/shard_map/ppermute | solution.py:187
  43.2 14.0 %collective-permute-start.4 = (bf16[8,2,128,128]{3,2,1,0:T(8,128)(2,1)S(1)}, bf16[8,2,128,128]{3,2,1,0:T(8,128)(2,1)S(1)}, u32[]{:S(2)}, u32[]{:S(2)}) collective-permute-start(bf16[8,2,128,128]{3,2,1,0:T(8,128)(2,1)S(1)} %collective-permute-done.1), channel_id=1, source_target_pairs={{0,4},{4,8},{8,12},{12,0},{1,5},{5,9},{9,13},{13,1},{2,6},{6,10},{... | collective-permute-start | bytes 1572872 | tf_op jit(solution)/shard_map/ppermute | solution.py:187
  43.3 34.6 %collective-permute-start.6 = (bf16[8,4,128,128]{3,2,1,0:T(8,128)(2,1)}, bf16[8,4,128,128]{3,2,1,0:T(8,128)(2,1)S(1)}, u32[]{:S(2)}, u32[]{:S(2)}) collective-permute-start(bf16[8,4,128,128]{3,2,1,0:T(8,128)(2,1)} %refs_9_.1), channel_id=1, source_target_pairs={{0,16},{16,0},{1,17},{17,1},{2,18},{18,2},{3,19},{19,3},{4,20},{20... | collective-permute-start | bytes 3145736 | tf_op jit(solution)/shard_map/ppermute | solution.py:191
  54.0 16.4 %collective-permute-start.13 = (bf16[10,1,128,128]{3,2,1,0:T(8,128)(2,1)S(1)}, bf16[10,1,128,128]{3,2,1,0:T(8,128)(2,1)S(1)}, u32[]{:S(2)}, u32[]{:S(2)}) collective-permute-start(bf16[10,1,128,128]{3,2,1,0:T(8,128)(2,1)S(1)} %get-tuple-element.35), channel_id=1, source_target_pairs={{1,0},{2,1},{3,2},{4,3},{5,4},{6,5},{7,6},{8,7},{9,8},{10,9},{11,1... | collective-permute-start | bytes 983048 | tf_op jit(solution)/shard_map/ppermute | solution.py:231
  57.3 20.6 %collective-permute-start.11 = (bf16[8,2,128,128]{3,2,1,0:T(8,128)(2,1)S(1)}, bf16[8,2,128,128]{3,2,1,0:T(8,128)(2,1)S(1)}, u32[]{:S(2)}, u32[]{:S(2)}) collective-permute-start(bf16[8,2,128,128]{3,2,1,0:T(8,128)(2,1)S(1)} %collective-permute-done.1), channel_id=1, source_target_pairs={{0,8},{4,12},{8,0},{12,4},{1,9},{5,13},{9,1},{13,5},{2,10},{6,14},... | collective-permute-start | bytes 1572872 | tf_op jit(solution)/shard_map/ppermute | solution.py:187
  59.8 18.1 %collective-permute-start.10 = (bf16[4,4,128,128]{3,2,1,0:T(8,128)(2,1)S(1)}, bf16[4,4,128,128]{3,2,1,0:T(8,128)(2,1)S(1)}, u32[]{:S(2)}, u32[]{:S(2)}) collective-permute-start(bf16[4,4,128,128]{3,2,1,0:T(8,128)(2,1)S(1)} %slice.37), channel_id=1, source_target_pairs={{0,96},{32,0},{64,32},{96,64},{1,97},{33,1},{65,33},{97,65},{2,98}... | collective-permute-start | bytes 1572872 | tf_op jit(solution)/shard_map/ppermute | solution.py:187
  60.7 17.3 %copy-start.2 = (bf16[8,4,128,128]{3,2,1,0:T(8,128)(2,1)}, bf16[8,4,128,128]{3,2,1,0:T(8,128)(2,1)S(1)}, u32[]{:S(2)}) copy-start(bf16[8,4,128,128]{3,2,1,0:T(8,128)(2,1)S(1)} %collective-permute-done.7.refs_11_) | copy-start | bytes 3145732
  60.7 17.2 %collective-permute-start.8 = (bf16[4,4,128,128]{3,2,1,0:T(8,128)(2,1)S(1)}, bf16[4,4,128,128]{3,2,1,0:T(8,128)(2,1)S(1)}, u32[]{:S(2)}, u32[]{:S(2)}) collective-permute-start(bf16[4,4,128,128]{3,2,1,0:T(8,128)(2,1)S(1)} %slice.36), channel_id=1, source_target_pairs={{0,32},{32,64},{64,96},{96,0},{1,33},{33,65},{65,97},{97,1},{2,34}... | collective-permute-start | bytes 1572872 | tf_op jit(solution)/shard_map/ppermute | solution.py:187
  71.2 5.9 %collective-permute-start.12 = (bf16[10,1,128,128]{3,2,1,0:T(8,128)(2,1)S(1)}, bf16[10,1,128,128]{3,2,1,0:T(8,128)(2,1)S(1)}, u32[]{:S(2)}, u32[]{:S(2)}) collective-permute-start(bf16[10,1,128,128]{3,2,1,0:T(8,128)(2,1)S(1)} %get-tuple-element.36), channel_id=1, source_target_pairs={{0,1},{1,2},{2,3},{3,4},{4,5},{5,6},{6,7},{7,8},{8,9},{9,10},{10,1... | collective-permute-start | bytes 983048 | tf_op jit(solution)/shard_map/ppermute | solution.py:230
  77.9 1.1 copy-start.13
  77.9 1.3 copy-start.15
  79.2 7.9 %copy-start.17 = (s32[8,8,32]{2,1,0:T(8,128)S(1)}, s32[8,8,32]{2,1,0:T(8,128)}, u32[]{:S(2)}) copy-start(s32[8,8,32]{2,1,0:T(8,128)} %act.3) | copy-start | bytes 24580
  79.2 7.9 %copy-start.18 = (s32[32]{0:T(128)S(1)}, s32[32]{0:T(128)}, u32[]{:S(2)}) copy-start(s32[32]{0:T(128)} %ls.3) | copy-start | bytes 388
  79.2 7.9 %copy-start.19 = (s32[32]{0:T(128)S(1)}, s32[32]{0:T(128)}, u32[]{:S(2)}) copy-start(s32[32]{0:T(128)} %rs.3) | copy-start | bytes 388
  79.5 6.1 %collective-permute-start.14 = (bf16[4,8,2,128,128]{4,3,2,1,0:T(8,128)(2,1)S(1)}, bf16[4,8,2,128,128]{4,3,2,1,0:T(8,128)(2,1)}, u32[]{:S(2)}, u32[]{:S(2)}) collective-permute-start(bf16[4,8,2,128,128]{4,3,2,1,0:T(8,128)(2,1)S(1)} %pad_maximum_fusion.refs_2_), channel_id=1, source_target_pairs={{0,1},{1,0},{2,3},{3,2},{4,5},{5,4},{6,7},{7,6},{8,9},{9,8},{10,11... | collective-permute-start | bytes 6291464 | tf_op jit(solution)/shard_map/ppermute | solution.py:191
  79.6 7.5 %collective-permute-start = (bf16[4,8,2,128,128]{4,3,2,1,0:T(8,128)(2,1)}, bf16[4,8,2,128,128]{4,3,2,1,0:T(8,128)(2,1)}, u32[]{:S(2)}, u32[]{:S(2)}) collective-permute-start(bf16[4,8,2,128,128]{4,3,2,1,0:T(8,128)(2,1)} %bitcast.6), channel_id=1, source_target_pairs={{0,1},{1,0},{2,3},{3,2},{4,5},{5,4},{6,7},{7,6},{8,9},{9,8},{10,11... | collective-permute-start | bytes 6291464 | tf_op jit(solution)/shard_map/ppermute | solution.py:191
  80.1 46.1 %collective-permute-start.16 = (bf16[8,4,128,128]{3,2,1,0:T(8,128)(2,1)}, bf16[8,4,128,128]{3,2,1,0:T(8,128)(2,1)}, u32[]{:S(2)}, u32[]{:S(2)}) collective-permute-start(bf16[8,4,128,128]{3,2,1,0:T(8,128)(2,1)} %copy-done.11), channel_id=1, source_target_pairs={{0,96},{32,0},{64,32},{96,64},{1,97},{33,1},{65,33},{97,65},{2,98}... | collective-permute-start | bytes 3145736 | tf_op jit(solution)/shard_map/ppermute | solution.py:187
  81.1 45.1 %collective-permute-start.15 = (bf16[8,4,128,128]{3,2,1,0:T(8,128)(2,1)}, bf16[8,4,128,128]{3,2,1,0:T(8,128)(2,1)}, u32[]{:S(2)}, u32[]{:S(2)}) collective-permute-start(bf16[8,4,128,128]{3,2,1,0:T(8,128)(2,1)} %copy-done.11), channel_id=1, source_target_pairs={{0,32},{32,64},{64,96},{96,0},{1,33},{33,65},{65,97},{97,1},{2,34}... | collective-permute-start | bytes 3145736 | tf_op jit(solution)/shard_map/ppermute | solution.py:187
  81.5 44.6 %collective-permute-start.17 = (bf16[4,4,128,128]{3,2,1,0:T(8,128)(2,1)}, bf16[4,4,128,128]{3,2,1,0:T(8,128)(2,1)}, u32[]{:S(2)}, u32[]{:S(2)}) collective-permute-start(bf16[4,4,128,128]{3,2,1,0:T(8,128)(2,1)} %copy-done.15), channel_id=1, source_target_pairs={{0,16},{16,0},{1,17},{17,1},{2,18},{18,2},{3,19},{19,3},{4,20},{20... | collective-permute-start | bytes 1572872 | tf_op jit(solution)/shard_map/ppermute | solution.py:191
  85.6 40.5 %collective-permute-start.18 = (bf16[4,4,128,128]{3,2,1,0:T(8,128)(2,1)}, bf16[4,4,128,128]{3,2,1,0:T(8,128)(2,1)}, u32[]{:S(2)}, u32[]{:S(2)}) collective-permute-start(bf16[4,4,128,128]{3,2,1,0:T(8,128)(2,1)} %copy-done.13), channel_id=1, source_target_pairs={{0,16},{16,0},{1,17},{17,1},{2,18},{18,2},{3,19},{19,3},{4,20},{20... | collective-permute-start | bytes 1572872 | tf_op jit(solution)/shard_map/ppermute | solution.py:191
  87.1 1.6 %copy-start = (bf16[8,8,128,128]{3,2,1,0:T(8,128)(2,1)S(1)}, bf16[8,8,128,128]{3,2,1,0:T(8,128)(2,1)}, u32[]{:S(2)}) copy-start(bf16[8,8,128,128]{3,2,1,0:T(8,128)(2,1)} %refs_4_.3) | copy-start | bytes 6291460
  88.6 1.6 %copy-start.1 = (bf16[32,2,128,128]{3,2,1,0:T(8,128)(2,1)S(1)}, bf16[32,2,128,128]{3,2,1,0:T(8,128)(2,1)}, u32[]{:S(2)}) copy-start(bf16[32,2,128,128]{3,2,1,0:T(8,128)(2,1)} %all-gather.3.cloned.1.call-done) | copy-start | bytes 6291460
  90.2 1.2 copy-start.3
  94.4 1.2 copy-start.10
  95.6 1.2 copy-start.12
  (8 other events, 7.4 us)
Sparse Core Ops, SparseCore 0:
  9.0 34.0 all-gather.2
